TPU v7x, 32 devices: a whole 2x2x4 slice. The times are simulated.
32 devices in a mesh: rows: 8 (over z, x), ch: 4 (over y, core).
Axes of the slice: x: 2, y: 2, z: 4, core: 2. Of those that a mesh axis runs over, the one named last changes fastest.
Arguments:
- features: bfloat16 [64, 4096], P('ch', 'rows'), may hold values from -6 to 6
- tiles: bfloat16 [32, 20, 128, 128], P('rows'), may hold values from -0.0625 to 0.0625
- tile_cols: int32 [32, 20], P('rows'), may hold values from 0 to 11, as said below
- needs: int32 [8, 8, 1], P('rows'), may hold values from -1 to 3, as said below
- weights: bfloat16 [4, 64, 64], P(None, 'ch'), may hold values from -0.375 to 0.375
- cotangent: bfloat16 [64, 4096], P('ch', 'rows'), may hold values from -6 to 6
Outputs:
- output: bfloat16 [64, 4096], P('ch', 'rows')
- feature_grad: bfloat16 [64, 4096], P('ch', 'rows')
- weight_grad: float32 [4, 64, 64], P(None, 'ch')
Inputs may be any that keep to these rules, and one draw needn't show every extreme that they name: needs[d, o, s] is a block index of device o, or -1 where unset; row o = d is unset; slot 0 is set for every o other than d; the set entries of one (d, o) differ; some device o has all 1 slots set by every other device. `tile_cols`: the first tile of row block b is its own block (entry b mod 4); an entry v >= 4 names cell v - 4 = 1 o + s with needs[d, o, s] set; every set entry of needs[d] is named by some tile of device d.
All inputs are finite; a program needn't handle non-finite values.
Results may differ from a plain program's by a relative error of at most 0.0055.
Values may be sent and summed in bfloat16 or wider, within the bound.
No kernel may reach another device: no remote copies, remote signals or barrier semaphores. Data moves between devices by JAX's collectives and lax.ppermute only.
A program may use at most 64 MiB of HBM per device.

v0:
```python
import jax
import jax.numpy as jnp
from jax import lax
from jax.sharding import PartitionSpec as P

K = 4


def body(features, tiles, tile_cols, needs, weights, cotangent):
    channels = features.shape[0]
    node_count = features.shape[1]
    blocks = tiles.shape[0]
    per_row = tiles.shape[1]
    block_width = tiles.shape[2]
    slot_count = needs.shape[2]
    shards = lax.axis_size("rows")
    flat_cols = tile_cols.reshape(-1)
    position = lax.axis_index("rows")
    ghost_cell = jnp.clip(flat_cols - blocks, 0, shards * slot_count - 1)
    needed = needs[0].reshape(-1)[ghost_cell]
    remote = ghost_cell // slot_count * blocks + jnp.maximum(needed, 0)
    source_index = jnp.where(flat_cols < blocks, position * blocks + flat_cols, remote)
    extent = blocks * shards

    def gather_source(values):
        return lax.all_gather(values, "rows", axis=1, tiled=True)

    def return_partials(partials):
        return lax.psum_scatter(partials, "rows", scatter_dimension=1, tiled=True)

    def forward_apply(term):
        source = gather_source(term.reshape(channels, blocks, block_width))
        picked = source[:, source_index, :].reshape(channels, blocks, per_row, block_width)
        result = jnp.einsum("crtj,rtij->cri", picked, tiles, preferred_element_type=jnp.float32)
        return result.reshape(channels, node_count)

    def transposed_apply(rounded):
        shaped = rounded.reshape(channels, blocks, block_width)
        contrib = jnp.einsum("cri,rtij->crtj", shaped, tiles, preferred_element_type=jnp.float32)
        contrib = contrib.reshape(channels, blocks * per_row, block_width)
        partials = (
            jnp.zeros((channels, extent, block_width), jnp.float32)
            .at[:, source_index, :]
            .add(contrib)
        )
        return return_partials(partials).reshape(channels, node_count)

    cheb_terms = [features, forward_apply(features).astype(jnp.bfloat16)]
    for degree in range(2, K):
        latest = 2.0 * forward_apply(cheb_terms[-1]) - cheb_terms[-2].astype(jnp.float32)
        cheb_terms.append(latest.astype(jnp.bfloat16))
    stacked = jnp.stack(cheb_terms)
    output = lax.psum_scatter(
        jnp.einsum("kio,kin->on", weights, stacked, preferred_element_type=jnp.float32),
        "ch",
        scatter_dimension=0,
        tiled=True,
    ).astype(jnp.bfloat16)
    grad_out = lax.all_gather(cotangent, "ch", axis=0, tiled=True)
    local_wgrad = jnp.einsum("kin,on->kio", stacked, grad_out, preferred_element_type=jnp.float32)
    weight_grad = lax.psum(local_wgrad, "rows")
    term_grads = jnp.einsum("kio,on->kin", weights, grad_out, preferred_element_type=jnp.float32)
    adjoints = [term_grads[degree] for degree in range(K)]
    for degree in range(K - 1, 1, -1):
        rounded = adjoints[degree].astype(jnp.bfloat16)
        adjoints[degree - 1] = adjoints[degree - 1] + 2.0 * transposed_apply(rounded)
        adjoints[degree - 2] = adjoints[degree - 2] - adjoints[degree]
    last = transposed_apply(adjoints[1].astype(jnp.bfloat16))
    feature_grad = (adjoints[0] + last).astype(jnp.bfloat16)
    return (output, feature_grad, weight_grad)


def solution(mesh):
    placed = (
        P("ch", "rows"),
        P("rows", None, None, None),
        P("rows", None),
        P("rows", None, None),
        P(None, "ch", None),
        P("ch", "rows"),
    )
    return jax.shard_map(
        body,
        mesh=mesh,
        in_specs=placed,
        out_specs=(P("ch", "rows"), P("ch", "rows"), P(None, "ch", None)),
        check_vma=False,
    )
```

profile of v0, /device:TPU:0, one launch (start us, length us, event | category | flops | bytes accessed | tf_op | source)
XLA Modules:
  0.0 292.2 jit_solution(1852419735173445717)
XLA Ops:
  7.2 0.0 copy-start
  7.2 0.0 reduce-scatter.7.cloned.1.call-start
  7.2 1.6 fusion.37
  8.9 0.7 broadcast_compare_fusion
  9.5 0.7 add_clamp_fusion
  10.2 0.1 add.100
  10.3 0.1 min.12
  10.4 0.1 lt.31
  10.5 6.4 %all_gather.15 = bf16[64,512]{1,0:T(8,128)(2,1)S(1)} all-gather(bf16[16,512]{1,0:T(8,128)(2,1)} %param.11), channel_id=1, replica_groups=mesh['rows'=8,'ch'=4] {'ch'}, dimensions={0}, use_global_device_ids=true | all-gather | bytes 81920 | tf_op jit(solution)/shard_map/all_gather | solution.py:59
  16.9 0.6 copy-done.5
  17.6 0.8 fusion.8
  18.4 0.0 copy-start.4
  18.4 0.6 copy-done.4
  19.1 0.0 copy-done
  19.1 0.0 copy-start.7
  19.1 0.5 fusion.21
  19.6 5.7 %fusion.30 = s32[80]{0:T(128)} fusion(pred[80,1]{0,1:T(4,128)(4,1)S(1)} %lt.31, s32[80,1]{0,1:T(1,128)S(1)} %add.100, s32[80,1]{0,1:T(1,128)S(1)} %min.12, s32[]{:T(128)} %bitcast.3, s32[]{:T(128)} %bitcast.4, s32[]{:T(128)} %bitcast.5, s32[]{:T(128)} %bitcast.6, s32[]{:T(128)} %bitcast.7, s32[]{:T(128)} %bitcast.9, s32[]{:T(128)} %bitcast.8, s32[]{:T(128)} %bitcast.2), kind=kLoop, calls=%fused_computation.64 | loop fusion | flops 1920 | bytes 1072 | tf_op jit(solution)/shard_map/select_n | solution.py:33
  25.2 3.7 %scatter_fusion = f32[16,32,128]{2,0,1:T(8,128)S(1)} fusion(f32[16,32,128]{2,0,1:T(8,128)S(1)} %broadcast.155.clone, s32[80]{0:T(128)} %fusion.30, f32[80,16,128]{2,1,0:T(8,128)S(1)} %bitcast.172), kind=kCustom, calls=%fused_computation.3 | custom fusion | flops 163840 | bytes 1966400 | tf_op jit(solution)/shard_map/scatter-add | solution.py:44
  28.9 0.0 copy-start.2
  29.0 0.7 copy-done.2
  29.6 0.0 reduce-scatter.7.cloned.1.call-update
  29.7 0.0 reduce-scatter.9.cloned.1.call-start
  29.7 1.4 slice_subtract_fusion
  31.1 0.7 pad_clamp_fusion
  31.8 0.0 copy-done.7
  31.8 31.4 %all_gather.12 = bf16[16,32,128]{2,0,1:T(8,128)(2,1)S(1)} all-gather(bf16[16,4,128]{2,0,1:T(8,128)(2,1)S(1)} %copy_bitcast_fusion.1), channel_id=1, replica_groups=mesh['rows'=8,'ch'=4] {'rows'}, dimensions={1}, use_global_device_ids=true | all-gather | bytes 147456 | tf_op jit(solution)/shard_map/all_gather | solution.py:26
  63.2 0.6 gather_fusion
  63.8 0.8 fusion.5
  64.6 30.5 %all_gather.13 = bf16[16,32,128]{2,0,1:T(8,128)(2,1)S(1)} all-gather(bf16[16,4,128]{2,0,1:T(8,128)(2,1)S(1)} %fusion.5), channel_id=1, replica_groups=mesh['rows'=8,'ch'=4] {'rows'}, dimensions={1}, use_global_device_ids=true | all-gather | bytes 147456 | tf_op jit(solution)/shard_map/all_gather | solution.py:26
  95.1 0.6 copy.36
  95.7 0.6 squeeze.12
  96.4 0.6 gather_fusion.1
  97.0 0.8 fusion.3
  97.8 0.6 fusion.36
  98.4 30.5 %all_gather.14 = bf16[16,32,128]{2,0,1:T(8,128)(2,1)S(1)} all-gather(bf16[16,4,128]{2,0,1:T(8,128)(2,1)S(1)} %bitcast.179), channel_id=1, replica_groups=mesh['rows'=8,'ch'=4] {'rows'}, dimensions={1}, use_global_device_ids=true | all-gather | bytes 147456 | tf_op jit(solution)/shard_map/all_gather | solution.py:26
  128.9 1.4 gather_fusion.2
  130.3 1.2 fusion.16
  131.5 3.7 %scatter_fusion.1 = f32[16,32,128]{2,0,1:T(8,128)S(1)} fusion(f32[16,32,128]{2,0,1:T(8,128)S(1)} %broadcast.155.clone.1, s32[80]{0:T(128)} %fusion.30, f32[80,16,128]{2,1,0:T(8,128)S(1)} %bitcast.171), kind=kCustom, calls=%fused_computation.4 | custom fusion | flops 163840 | bytes 1966400 | tf_op jit(solution)/shard_map/scatter-add | solution.py:44
  135.2 0.0 copy-start.3
  135.3 0.0 copy-start.8
  135.3 0.0 copy-start.10
  135.3 0.0 copy-start.12
  135.3 0.0 copy-start.6
  135.3 0.6 copy-done.3
  136.0 0.0 reduce-scatter.9.cloned.1.call-update
  136.0 0.0 reduce-scatter.5.cloned.1.call-start
  136.0 1.7 fusion.1
  137.8 0.0 copy-done.8
  137.9 0.0 copy-start.11
  137.9 0.0 copy-done.10
  137.9 0.0 copy-done.12
  137.9 0.9 convolution_bitcast_fusion
  138.8 0.0 reduce-scatter.5.cloned.1.call-update
  138.8 0.0 reduce-scatter.11.cloned.1.call-start
  138.9 59.4 %reduce-scatter.9.cloned.1.call-done = f32[16,4,128]{2,0,1:T(8,128)} async-done(((f32[16,32,128]{2,0,1:T(8,128)}), f32[16,4,128]{2,0,1:T(8,128)}) %reduce-scatter.9.cloned.1.call-update) | async-done | bytes 32784 | tf_op jit(solution)/shard_map/reduce_scatter | solution.py:29
  198.3 1.2 fusion.19
  199.6 3.7 %scatter_fusion.2 = f32[16,32,128]{2,0,1:T(8,128)S(1)} fusion(f32[16,32,128]{2,0,1:T(8,128)S(1)} %broadcast.155, s32[80]{0:T(128)} %fusion.30, f32[80,16,128]{2,1,0:T(8,128)S(1)} %bitcast.170), kind=kCustom, calls=%fused_computation.5 | custom fusion | flops 163840 | bytes 1966400 | tf_op jit(solution)/shard_map/scatter-add | solution.py:44
  203.3 0.7 copy-done.1
  204.0 0.0 reduce-scatter.11.cloned.1.call-update
  204.0 1.0 fusion.6
  205.0 35.8 %psum.7 = f32[4,16,64]{2,1,0:T(8,128)} all-reduce(f32[4,16,64]{2,1,0:T(8,128)S(1)} %fusion.6), channel_id=1, replica_groups=mesh['rows'=8,'ch'=4] {'rows'}, use_global_device_ids=true, to_apply=%region_7.8 | all-reduce | flops 4096 | bytes 32768 | tf_op jit(solution)/shard_map/psum | solution.py:61
  240.8 1.4 convert_element_type.76
  242.2 42.0 %reduce-scatter.11.cloned.1.call-done = f32[16,4,128]{2,0,1:T(8,128)} async-done(((f32[16,32,128]{2,0,1:T(8,128)}), f32[16,4,128]{2,0,1:T(8,128)}) %reduce-scatter.11.cloned.1.call-update) | async-done | bytes 32784 | tf_op jit(solution)/shard_map/reduce_scatter | solution.py:29
  284.2 1.4 fusion.10
  (20 shorter events, 0.2 us)
Async XLA Ops:
  7.2 11.9 %copy-start = (bf16[4,20,128,128]{3,2,1,0:T(8,128)(2,1)S(1)}, bf16[4,20,128,128]{3,2,1,0:T(8,128)(2,1)}, u32[]{:S(2)}) copy-start(bf16[4,20,128,128]{3,2,1,0:T(8,128)(2,1)} %param.7) | copy-start | bytes 7864324
  7.2 123.1 %reduce-scatter.7.cloned.1.call-start = ((), (), s32[]{:S(2)}) async-start(), calls=%async_computation.5 | async-start | bytes 294912 | tf_op jit(solution)/shard_map/reduce_scatter | solution.py:29
  16.9 0.6 copy-start.5
  18.4 0.6 copy-start.4
  19.1 12.7 %copy-start.7 = (bf16[16,512]{1,0:T(8,128)(2,1)S(1)}, bf16[16,512]{1,0:T(8,128)(2,1)}, u32[]{:S(2)}) copy-start(bf16[16,512]{1,0:T(8,128)(2,1)} %param.6) | copy-start | bytes 49156
  28.9 0.7 copy-start.2
  29.7 168.7 %reduce-scatter.9.cloned.1.call-start = ((), (), s32[]{:S(2)}) async-start(), calls=%async_computation.6 | async-start | bytes 294912 | tf_op jit(solution)/shard_map/reduce_scatter | solution.py:29
  135.2 0.7 copy-start.3
  135.3 2.6 copy-start.8
  135.3 2.6 copy-start.10
  135.3 2.6 copy-start.12
  135.3 3.6 %copy-start.6 = (f32[1,16,512]{2,1,0:T(8,128)S(1)}, f32[1,16,512]{2,1,0:T(8,128)}, u32[]{:S(2)}) copy-start(f32[1,16,512]{2,1,0:T(8,128)} %get-tuple-element.3) | copy-start | bytes 98308
  136.0 104.9 %reduce-scatter.5.cloned.1.call-start = ((), (), s32[]{:S(2)}) async-start(), calls=%async_computation.4 | async-start | bytes 163840 | tf_op jit(solution)/shard_map/reduce_scatter | solution.py:53
  137.9 61.7 %copy-start.9 = (bf16[1,16,512]{2,1,0:T(8,128)(2,1)}, bf16[1,16,512]{2,1,0:T(8,128)(2,1)S(1)}, u32[]{:S(2)}) copy-start(bf16[1,16,512]{2,1,0:T(8,128)(2,1)S(1)} %convert_element_type.71) | copy-start | bytes 49156
  137.9 1.0 copy-start.11
  138.8 145.4 %reduce-scatter.11.cloned.1.call-start = ((), (), s32[]{:S(2)}) async-start(), calls=%async_computation.7 | async-start | bytes 294912 | tf_op jit(solution)/shard_map/reduce_scatter | solution.py:29
  203.3 0.7 copy-start.1
Sparse Core Ops, SparseCore 0:
  29.8 63.0 reduce-scatter.6
  136.1 62.1 reduce-scatter.8
  200.8 18.6 reduce-scatter.4
  223.0 61.1 reduce-scatter.10
where the time goes:
time: 293 us; the launch traced here: 292 us
  blocking collectives  135 us (46%)
  waiting for transfers between devices  102 us (35%)
  other arithmetic  23.6 us (8%)
  between operations  14 us (5%)
  local copies, waits for them, and re-layouts  9.28 us (3%)
  matrix products  8.93 us (3%)
    reduce_scatter x3, waiting for transfers between devices, return_partials(): return lax.psum_scatter(partials, 'rows', scatter_dimension=1, tiled=True)  101 us
    all_gather x3, blocking collectives, gather_source(): return lax.all_gather(values, 'rows', axis=1, tiled=True)  92.4 us
    psum x1, blocking collectives, body(): weight_grad = lax.psum(local_wgrad, 'rows')  35.8 us
    scatter-add x3, other arithmetic, transposed_apply(): partials = jnp.zeros((channels, extent, block_width), jnp.float32).at[:,...  11.1 us
    all_gather x1, blocking collectives, body(): grad_out = lax.all_gather(cotangent, 'ch', axis=0, tiled=True)  6.45 us
  transfers between devices with their start and end apart: 4, of which 2 were waited for; matrix products, arithmetic and copies ran while one was open for 6% of the time, Pallas kernels for 0%

commit v1 on v0

v1 whole, which is shorter than its diff:
```python
import functools

import jax
import jax.numpy as jnp
from jax import lax
from jax.experimental import pallas as pl
from jax.experimental.pallas import tpu as pltpu
from jax.sharding import PartitionSpec as P

K = 4
BF = jnp.bfloat16
F32 = jnp.float32
SMEM = pltpu.MemorySpace.SMEM
VMEM = pltpu.MemorySpace.VMEM


def nn(a, b):
    return lax.dot_general(a, b, (((1,), (0,)), ((), ())), preferred_element_type=F32)


def nt(a, b):
    return lax.dot_general(a, b, (((1,), (1,)), ((), ())), preferred_element_type=F32)


def lanes(index, width):
    return pl.ds(pl.multiple_of(index * width, width), width)


def push_kernel(cols, needs, f, c, w, tiles, x1, pack, cells, where, buf, acc, sems):
    nb, tpr = cols.shape
    n, ci, bw = acc.shape

    def scan(i, count):
        r = i // (tpr - 1)
        t = i % (tpr - 1) + 1
        v = cols[r, t]
        ghost = v >= nb

        @pl.when(ghost)
        def _():
            cells[count] = v - nb
            where[count] = r
            pltpu.make_async_copy(tiles.at[r, t], buf.at[count], sems.at[count]).start()

        return count + ghost.astype(jnp.int32)

    count = lax.fori_loop(0, nb * (tpr - 1), scan, 0)
    for o in range(n):
        acc[o] = jnp.zeros((ci, bw), F32)
        for b in range(nb):
            x1[o, b * ci : (b + 1) * ci, :] = f[:, b * bw : (b + 1) * bw]
        x1[o, (nb + 1) * ci :, :] = jnp.full((ci, bw), needs[0, o, 0].astype(F32)).astype(BF)
    pack[0:ci] = f[...]
    pack[ci : 2 * ci] = c[...]
    for k in range(K):
        width = w.shape[2]
        pack[2 * ci :, k * width : (k + 1) * width] = w[k]

    def product(i, carry):
        pltpu.make_async_copy(tiles.at[0, 0], buf.at[i], sems.at[i]).wait()
        o = cells[i]
        acc[o] += nn(c[:, lanes(where[i], bw)], buf[i])
        return carry

    lax.fori_loop(0, count, product, 0)
    for o in range(n):
        x1[o, nb * ci : (nb + 1) * ci, :] = acc[o].astype(BF)


def combine_kernel(cols, f, c, tiles, op, lf, ltc, total):
    r = pl.program_id(0)
    tpr = tiles.shape[1]
    bw = tiles.shape[2]
    own = f.shape[1]
    total[...] = jnp.zeros_like(total)
    for t in range(tpr):
        at = lanes(cols[r, t], bw)
        total[:, at] += tiles[0, t].astype(F32)
    op[...] = total[...].astype(BF)
    local = op[:, :own]
    lf[...] = nt(f[...], local)
    part = nn(c[:, lanes(r, bw)], local)

    @pl.when(r == 0)
    def _():
        ltc[...] = part

    @pl.when(r > 0)
    def _():
        ltc[...] += part


def first_kernel(needs, y1, op, lf, ltc, x2, tu, marks_ref, gh):
    n, rows, bw = y1.shape
    ci, own = lf.shape
    nb = own // bw
    q = x2.shape[0] // n
    for o in range(n):
        at = jnp.maximum(needs[0, o, 0], 0) * ci
        gh[:, o * bw : (o + 1) * bw] = y1[o, pl.ds(pl.multiple_of(at, ci), ci), :]
    t1 = (lf[...] + nt(gh[...], op[:, own:])).astype(BF)
    marks = [y1[o, (nb + 1) * ci :, :].astype(F32) for o in range(n)]
    for o in range(n):
        marks_ref[o] = y1[o, (nb + 1) * ci :, :]
    u1 = []
    for b in range(nb):
        u = ltc[:, b * bw : (b + 1) * bw]
        for o in range(n):
            u = u + jnp.where(marks[o] == b, y1[o, nb * ci : (nb + 1) * ci, :].astype(F32), 0.0)
        u1.append(u.astype(BF))
    tu[0:ci] = t1
    for b in range(nb):
        tu[ci:, b * bw : (b + 1) * bw] = u1[b]
    sent = nn(tu[ci:], op[:, own:]).astype(BF)
    tf = t1.astype(F32)
    for o in range(n):
        blk = jnp.zeros((ci, bw), F32)
        for b in range(nb):
            blk = jnp.where(marks[o] == b, tf[:, b * bw : (b + 1) * bw], blk)
        blk = blk.astype(BF)
        for s in range(q):
            x2[o * q + s, 0:ci, :] = blk
            x2[o * q + s, ci:, :] = sent[:, o * bw : (o + 1) * bw]


def gather_kernel(q, refs):
    packs = refs[:q]
    tus = refs[q : 2 * q]
    op, tpre, upre, full, wt, wg, wbuf = refs[2 * q :]
    own = tpre.shape[1]
    total = tpre.shape[0]
    ci = total // q
    co = wt.shape[1]
    me = lax.axis_index("ch")
    for s in range(q):
        at = lax.rem(me - s + q, q) * ci
        spot = pl.ds(pl.multiple_of(at, ci), ci)
        full[0, spot, :] = packs[s][0:ci, :]
        full[1, spot, :] = packs[s][ci : 2 * ci, :]
        full[2, spot, :] = tus[s][0:ci, :]
        full[3, spot, :] = tus[s][ci:, :]
        wbuf[spot, :] = packs[s][2 * ci :, : K * co].astype(F32)
    for k in range(K):
        turned = wbuf[:, k * co : (k + 1) * co].T
        wt[k] = turned.astype(BF)
    local = op[:, :own]
    tpre[...] = 2.0 * nt(full[2], local) - full[0].astype(F32)
    upre[...] = 2.0 * nn(full[3], local) - full[1].astype(F32)
    wg[0] = nt(packs[0][0:ci, :], full[1])
    wg[1] = nt(tus[0][0:ci, :], full[1])


def second_kernel(q, y2, marks_ref, op, tpre, upre, full, wt, wg, w, x3, two, gh2, gh, low):
    n, ci, bw = marks_ref.shape
    total, own = tpre.shape
    nb = own // bw
    me = lax.axis_index("ch")
    mine = pl.ds(pl.multiple_of(me * ci, ci), ci)
    for o in range(n):
        for s in range(q):
            gh[s * ci : (s + 1) * ci, o * bw : (o + 1) * bw] = y2[o * q + s, 0:ci, :]
    two[0] = (tpre[...] + 2.0 * nt(gh[...], op[:, own:])).astype(BF)
    marks = [marks_ref[o].astype(F32) for o in range(n)]
    for s in range(q):
        for b in range(nb):
            u = jnp.zeros((ci, bw), F32)
            for o in range(n):
                u = u + jnp.where(marks[o] == b, y2[o * q + s, ci:, :].astype(F32), 0.0)
            spot = (slice(s * ci, (s + 1) * ci), slice(b * bw, (b + 1) * bw))
            two[(1,) + spot] = (upre[spot] + 2.0 * u).astype(BF)
    g = nn(wt[K - 1, mine, :], two[0]).astype(BF)
    h = nn(w[K - 1], two[1]).astype(BF)
    gh2[0] = g
    gh2[1] = h
    sent = nn(h, op[:, own:]).astype(BF)
    t2 = two[0, mine, :]
    co = w.shape[2]
    wg2 = nt(t2, full[1])
    wg3 = 2.0 * nt(t2, full[3]) - wg[1]
    low[0:ci, 0:co] = wg[0]
    low[0:ci, co:] = wg[1]
    low[ci:, 0:co] = wg2
    low[ci:, co:] = wg3
    packed = low[...].astype(BF)
    gf = g.astype(F32)
    for o in range(n):
        blk = jnp.zeros((ci, bw), F32)
        for b in range(nb):
            blk = jnp.where(marks[o] == b, gf[:, b * bw : (b + 1) * bw], blk)
        x3[o, 0:ci, :] = blk.astype(BF)
        x3[o, ci : 2 * ci, :] = sent[:, o * bw : (o + 1) * bw]
        x3[o, 2 * ci :, :] = packed


def local_kernel(op, full, two, gh2, wt, w, outl, fgl):
    ci, own = outl.shape
    me = lax.axis_index("ch")
    mine = pl.ds(pl.multiple_of(me * ci, ci), ci)
    local = op[:, :own]
    out = nn(wt[0, mine, :], full[0]) + nn(wt[1, mine, :], full[2]) - nn(wt[3, mine, :], full[2])
    outl[...] = out + nn(wt[2, mine, :], two[0]) + 2.0 * nt(gh2[0], local)
    fg = nn(w[0], full[1]) + nn(w[1], full[3]) - nn(w[3], full[3])
    fgl[...] = fg + nn(w[2], two[1]) + 2.0 * nn(gh2[1], local)


def last_kernel(y3, marks_ref, op, outl, fgl, out, fg, wgrad, gh):
    n, ci, bw = marks_ref.shape
    own = outl.shape[1]
    nb = own // bw
    co = wgrad.shape[2]
    for o in range(n):
        gh[:, o * bw : (o + 1) * bw] = y3[o, 0:ci, :]
    out[...] = (outl[...] + 2.0 * nt(gh[...], op[:, own:])).astype(BF)
    for b in range(nb):
        u = jnp.zeros((ci, bw), F32)
        for o in range(n):
            u = u + jnp.where(marks_ref[o].astype(F32) == b, y3[o, ci : 2 * ci, :].astype(F32), 0.0)
        spot = slice(b * bw, (b + 1) * bw)
        fg[:, spot] = (fgl[:, spot] + 2.0 * u).astype(BF)
    wsum = y3[0, 2 * ci :, :].astype(F32)
    for o in range(1, n):
        wsum = wsum + y3[o, 2 * ci :, :].astype(F32)
    wgrad[0] = wsum[0:ci, 0:co]
    wgrad[1] = wsum[0:ci, co:]
    wgrad[2] = wsum[ci:, 0:co]
    wgrad[3] = wsum[ci:, co:]


def body(features, tiles, tile_cols, needs, weights, cotangent):
    ci, own = features.shape
    nb, tpr, bw, _ = tiles.shape
    co = weights.shape[2]
    n = lax.axis_size("rows")
    q = lax.axis_size("ch")
    total = ci * q
    cells = nb + n
    wide = cells * bw
    struct = jax.ShapeDtypeStruct
    smem = pl.BlockSpec(memory_space=SMEM)
    vmem = pl.BlockSpec(memory_space=VMEM)
    limit = (16 << 20) + 4 * own * wide * 2
    params = pltpu.CompilerParams(vmem_limit_bytes=limit)

    x1, pack = pl.pallas_call(
        push_kernel,
        out_shape=(struct((n, (nb + 2) * ci, bw), BF), struct((3 * ci, own), BF)),
        in_specs=[smem, smem, vmem, vmem, vmem, pl.BlockSpec(memory_space=pl.ANY)],
        out_specs=(vmem, vmem),
        scratch_shapes=[
            pltpu.SMEM((nb * tpr,), jnp.int32),
            pltpu.SMEM((nb * tpr,), jnp.int32),
            pltpu.VMEM((nb * tpr, bw, bw), BF),
            pltpu.VMEM((n, ci, bw), F32),
            pltpu.SemaphoreType.DMA((nb * tpr,)),
        ],
        compiler_params=params,
        name="push",
    )(tile_cols, needs, features, cotangent, weights, tiles)
    y1 = lax.all_to_all(x1, "rows", 0, 0)

    op, lf, ltc = pl.pallas_call(
        combine_kernel,
        grid=(nb,),
        out_shape=(struct((own, wide), BF), struct((ci, own), F32), struct((ci, own), F32)),
        in_specs=[
            smem,
            pl.BlockSpec((ci, own), lambda r: (0, 0)),
            pl.BlockSpec((ci, own), lambda r: (0, 0)),
            pl.BlockSpec((1, tpr, bw, bw), lambda r: (r, 0, 0, 0)),
        ],
        out_specs=(
            pl.BlockSpec((bw, wide), lambda r: (r, 0)),
            pl.BlockSpec((ci, bw), lambda r: (0, r)),
            pl.BlockSpec((ci, own), lambda r: (0, 0)),
        ),
        scratch_shapes=[pltpu.VMEM((bw, wide), F32)],
        compiler_params=params,
        cost_estimate=pl.CostEstimate(flops=4 * ci * own * own, bytes_accessed=8 << 20, transcendentals=0),
        name="combine",
    )(tile_cols, features, cotangent, tiles)

    def around(value):
        moved = [value]
        for s in range(1, q):
            moved.append(lax.ppermute(value, "ch", [(i, (i + s) % q) for i in range(q)]))
        return moved

    packs = around(pack)

    x2, tu, marks = pl.pallas_call(
        first_kernel,
        out_shape=(struct((n * q, 2 * ci, bw), BF), struct((2 * ci, own), BF), struct((n, ci, bw), BF)),
        in_specs=[smem, vmem, vmem, vmem, vmem],
        out_specs=(vmem,) * 3,
        scratch_shapes=[pltpu.VMEM((ci, n * bw), BF)],
        compiler_params=params,
        name="first",
    )(needs, y1, op, lf, ltc)
    y2 = lax.all_to_all(x2, ("rows", "ch"), 0, 0)
    tus = around(tu)

    tpre, upre, full, wt, wg = pl.pallas_call(
        lambda *refs: gather_kernel(q, refs),
        out_shape=(
            struct((total, own), F32),
            struct((total, own), F32),
            struct((4, total, own), BF),
            struct((K, co, total), BF),
            struct((2, ci, co), F32),
        ),
        in_specs=[vmem] * (2 * q + 1),
        out_specs=(vmem,) * 5,
        scratch_shapes=[pltpu.VMEM((total, K * co), F32)],
        compiler_params=params,
        cost_estimate=pl.CostEstimate(flops=4 * total * own * own, bytes_accessed=4 << 20, transcendentals=0),
        name="gather",
    )(*packs, *tus, op)

    x3, two, gh2 = pl.pallas_call(
        functools.partial(second_kernel, q),
        out_shape=(struct((n, 4 * ci, bw), BF), struct((2, total, own), BF), struct((2, ci, own), BF)),
        in_specs=[vmem] * 9,
        out_specs=(vmem,) * 3,
        scratch_shapes=[pltpu.VMEM((total, n * bw), BF), pltpu.VMEM((2 * ci, bw), F32)],
        compiler_params=params,
        name="second",
    )(y2, marks, op, tpre, upre, full, wt, wg, weights)
    y3 = lax.all_to_all(x3, "rows", 0, 0)

    outl, fgl = pl.pallas_call(
        local_kernel,
        out_shape=(struct((ci, own), F32), struct((ci, own), F32)),
        in_specs=[vmem] * 6,
        out_specs=(vmem,) * 2,
        compiler_params=params,
        cost_estimate=pl.CostEstimate(flops=8 * total * ci * own, bytes_accessed=4 << 20, transcendentals=0),
        name="local",
    )(op, full, two, gh2, wt, weights)

    output, feature_grad, weight_grad = pl.pallas_call(
        last_kernel,
        out_shape=(struct((ci, own), BF), struct((ci, own), BF), struct((K, ci, co), F32)),
        in_specs=[vmem] * 5,
        out_specs=(vmem,) * 3,
        scratch_shapes=[pltpu.VMEM((ci, n * bw), BF)],
        compiler_params=params,
        name="last",
    )(y3, marks, op, outl, fgl)
    return output, feature_grad, weight_grad


def solution(mesh):
    placed = (
        P("ch", "rows"),
        P("rows", None, None, None),
        P("rows", None),
        P("rows", None, None),
        P(None, "ch", None),
        P("ch", "rows"),
    )
    return jax.shard_map(
        body,
        mesh=mesh,
        in_specs=placed,
        out_specs=(P("ch", "rows"), P("ch", "rows"), P(None, "ch", None)),
        check_vma=False,
    )
```

time: 293 us -> 57.5 us (0.20)
  blocking collectives: 135 us -> 0 us
  waiting for transfers between devices: 102 us -> 15.4 us
  other arithmetic: 23.6 us -> 0 us
  starting transfers between devices: 0.16 us -> 20.4 us
  between operations: 14 us -> 0.72 us
  Pallas kernels: 0 us -> 13.1 us
  matrix products: 8.93 us -> 0 us
    reduce_scatter x4 -> x0, waiting for transfers between devices: 101 us -> none  [the longest x3 101 us: return_partials(): return lax.psum_scatter(partials, 'rows', scatter_dimension=1, tiled=True)]
    all_gather x4 -> x0, blocking collectives: 98.8 us -> none  [the longest x3 92.4 us: gather_source(): return lax.all_gather(values, 'rows', axis=1, tiled=True)]
    psum x1 -> x0, blocking collectives: 35.8 us -> none  [body(): weight_grad = lax.psum(local_wgrad, 'rows')]
    all_to_all x0 -> x3, starting transfers between devices: none -> 15.1 us  [the longest x1 7.27 us: body(): y1 = lax.all_to_all(x1, 'rows', 0, 0)]
    pallas_call x0 -> x7, Pallas kernels: none -> 13.1 us  [the longest x1 5.37 us: body(): pl.pallas_call(push_kernel, out_shape=(struct((n, (nb + 2) * ci, bw), BF)...]
    all_to_all x0 -> x3, waiting for transfers between devices: none -> 11.7 us  [the longest x1 6.96 us: body(): y3 = lax.all_to_all(x3, 'rows', 0, 0)]
    scatter-add x3 -> x0, other arithmetic: 11.1 us -> none  [transposed_apply(): partials = jnp.zeros((channels, extent, block_width), jnp.float32).at[:,...]
    dot_general x9 -> x0, matrix products: 8.93 us -> none  [the longest x3 3.3 us: forward_apply(): jnp.einsum('crtj,rtij->cri', picked, tiles, preferred_element_type=jnp.fl...]
  transfers between devices with their start and end apart: 4 -> 9, of which waited for: 2 -> 6; matrix products, arithmetic and copies ran while one was open for 6% -> 0% of each run, Pallas kernels for 0% -> 6%
where the time goes in v1:
time: 57.5 us; the launch traced here: 56.7 us
  starting transfers between devices  20.4 us (35%)
  waiting for transfers between devices  15.4 us (27%)
  Pallas kernels  13.1 us (23%)
  local copies, waits for them, and re-layouts  7.06 us (12%)
  between operations  0.72 us (1%)
    all_to_all x1, starting transfers between devices, body(): y1 = lax.all_to_all(x1, 'rows', 0, 0)  7.27 us
    unnamed x21, local copies, waits for them, and re-layouts  7.06 us
    all_to_all x1, waiting for transfers between devices, body(): y3 = lax.all_to_all(x3, 'rows', 0, 0)  6.96 us
    pallas_call x1, Pallas kernels, body(): pl.pallas_call(push_kernel, out_shape=(struct((n, (nb + 2) * ci, bw), BF)...  5.37 us
    ppermute x6, starting transfers between devices, around(): lax.ppermute(value, 'ch', [(i, (i + s) % q) for i in range(q)])  5.36 us
    all_to_all x1, starting transfers between devices, body(): y3 = lax.all_to_all(x3, 'rows', 0, 0)  4.6 us
    ppermute x6, waiting for transfers between devices, around(): lax.ppermute(value, 'ch', [(i, (i + s) % q) for i in range(q)])  3.64 us
    all_to_all x1, waiting for transfers between devices, body(): y1 = lax.all_to_all(x1, 'rows', 0, 0)  3.58 us
  transfers between devices with their start and end apart: 9, of which 6 were waited for; matrix products, arithmetic and copies ran while one was open for 0% of the time, Pallas kernels for 6%

profile of v1, /device:TPU:0, one launch (start us, length us, event | category | flops | bytes accessed | tf_op | source)
XLA Modules:
  0.0 56.7 jit_solution(13550080929964971359)
XLA Ops:
  0.6 0.0 copy-start.9
  0.6 0.7 %copy.10.needs = s32[1,8,1]{2,1,0:T(8,128)S(1)} copy(s32[1,8,1]{1,2,0:T(1,128)} %param.9) | data formatting | bytes 64 | tf_op args[3]
  1.4 0.0 copy-start
  1.4 1.7 %copy-done = bf16[4,20,128,128]{3,2,1,0:T(8,128)(2,1)S(1)} copy-done((bf16[4,20,128,128]{3,2,1,0:T(8,128)(2,1)S(1)}, bf16[4,20,128,128]{3,2,1,0:T(8,128)(2,1)}, u32[]{:S(2)}) %copy-start) | copy-done | bytes 2621464
  3.1 0.0 copy-start.2
  3.1 0.7 %copy-done.2 = bf16[4,16,64]{2,1,0:T(8,128)(2,1)S(1)} copy-done((bf16[4,16,64]{2,1,0:T(8,128)(2,1)S(1)}, bf16[4,16,64]{2,1,0:T(8,128)(2,1)}, u32[]{:S(2)}) %copy-start.2) | copy-done | bytes 8216
  3.8 0.0 copy-start.4
  3.8 0.7 %copy-done.4 = bf16[16,512]{1,0:T(8,128)(2,1)S(1)} copy-done((bf16[16,512]{1,0:T(8,128)(2,1)S(1)}, bf16[16,512]{1,0:T(8,128)(2,1)}, u32[]{:S(2)}) %copy-start.4) | copy-done | bytes 16408
  4.6 0.0 copy-start.6
  4.6 0.7 %copy-done.6 = bf16[16,512]{1,0:T(8,128)(2,1)S(1)} copy-done((bf16[16,512]{1,0:T(8,128)(2,1)S(1)}, bf16[16,512]{1,0:T(8,128)(2,1)}, u32[]{:S(2)}) %copy-start.6) | copy-done | bytes 16408
  5.3 0.0 copy-start.8
  5.3 0.7 %copy-done.8 = s32[4,20]{1,0:T(4,128)S(1)} copy-done((s32[4,20]{1,0:T(4,128)S(1)}, s32[4,20]{1,0:T(4,128)}, u32[]{:S(2)}) %copy-start.8) | copy-done | bytes 344
  6.0 0.0 copy-start.5
  6.0 0.0 copy-start.7
  6.0 5.4 %push.1 = (bf16[8,96,128]{2,1,0:T(8,128)(2,1)}, bf16[48,512]{1,0:T(8,128)(2,1)S(1)}) custom-call(s32[4,20]{1,0:T(4,128)S(1)} %copy-done.8, s32[1,8,1]{2,1,0:T(8,128)S(1)} %copy.10.needs, bf16[16,512]{1,0:T(8,128)(2,1)S(1)} %copy-done.4, bf16[16,512]{1,0:T(8,128)(2,1)S(1)} %copy-done.6, bf16[4,16,64]{2,1,0:T(8,128)(2,1)S(1)} %copy-done.2, ...), custom_call_target="tpu_custom_call" | custom-call | tf_op jit(solution)/shard_map/push/pallas_call | solution.py:244
  11.3 7.3 %all-to-all-start = ((bf16[8,96,128]{2,1,0:T(8,128)(2,1)}), bf16[8,96,128]{2,1,0:T(8,128)(2,1)S(1)}, u32[]{:S(2)}, u32[]{:S(2)}) async-start(bf16[8,96,128]{2,1,0:T(8,128)(2,1)} %get-tuple-element.21), calls=%async_computation | async-start | bytes 393216 | tf_op jit(solution)/shard_map/all_to_all | solution.py:259
  18.6 0.0 copy-done.9
  18.6 0.0 copy-done.5
  18.6 0.0 copy-done.7
  18.6 0.0 copy-start.1
  18.6 1.7 %copy-done.1 = bf16[4,20,128,128]{3,2,1,0:T(8,128)(2,1)S(1)} copy-done((bf16[4,20,128,128]{3,2,1,0:T(8,128)(2,1)S(1)}, bf16[4,20,128,128]{3,2,1,0:T(8,128)(2,1)}, u32[]{:S(2)}) %copy-start.1) | copy-done | bytes 2621464
  20.4 2.6 %combine.1 = (bf16[512,1536]{1,0:T(8,128)(2,1)S(1)}, f32[16,512]{1,0:T(8,128)S(1)}, f32[16,512]{1,0:T(8,128)S(1)}) custom-call(s32[4,20]{1,0:T(4,128)S(1)} %copy-done.9, bf16[16,512]{1,0:T(8,128)(2,1)S(1)} %copy-done.5, bf16[16,512]{1,0:T(8,128)(2,1)S(1)} %copy-done.7, bf16[4,20,128,128]{3,2,1,0:T(8,128)(2,1)S(1)} %copy-done.1), custom_call_target="tpu_custom_call" | custom-call | flops 16777216 | bytes 8388608 | tf_op jit(solution)/shard_map/combine/pallas_call | solution.py:261
  23.0 0.0 copy-start.3
  23.0 3.6 %all-to-all-done.y1 = bf16[8,96,128]{2,1,0:T(8,128)(2,1)S(1)} async-done(((bf16[8,96,128]{2,1,0:T(8,128)(2,1)}), bf16[8,96,128]{2,1,0:T(8,128)(2,1)S(1)}, u32[]{:S(2)}, u32[]{:S(2)}) %all-to-all-start) | async-done | bytes 196640 | tf_op jit(solution)/shard_map/all_to_all | solution.py:259
  26.6 1.8 %first.1 = (bf16[32,32,128]{2,1,0:T(8,128)(2,1)}, bf16[32,512]{1,0:T(8,128)(2,1)S(1)}, bf16[8,16,128]{2,1,0:T(8,128)(2,1)S(1)}) custom-call(s32[1,8,1]{2,1,0:T(8,128)S(1)} %copy.10.needs, bf16[8,96,128]{2,1,0:T(8,128)(2,1)S(1)} %all-to-all-done.y1, bf16[512,1536]{1,0:T(8,128)(2,1)S(1)} %get-tuple-element.22.op.refs_8_, f32[16,512]{1,0:T(8,128)S(1)} %get-tuple-element.23.lf, ...), custom_call_target="tpu_custom_call" | custom-call | tf_op jit(solution)/shard_map/first/pallas_call | solution.py:290
  28.4 3.2 %all-to-all-start.1 = ((bf16[32,32,128]{2,1,0:T(8,128)(2,1)}), bf16[32,32,128]{2,1,0:T(8,128)(2,1)S(1)}, u32[]{:S(2)}, u32[]{:S(2)}) async-start(bf16[32,32,128]{2,1,0:T(8,128)(2,1)} %get-tuple-element.25), calls=%async_computation.1 | async-start | bytes 524288 | tf_op jit(solution)/shard_map/all_to_all | solution.py:299
  31.6 1.6 %collective-permute-start.2 = (bf16[48,512]{1,0:T(8,128)(2,1)S(1)}, bf16[48,512]{1,0:T(8,128)(2,1)S(1)}, u32[]{:S(2)}, u32[]{:S(2)}) collective-permute-start(bf16[48,512]{1,0:T(8,128)(2,1)S(1)} %get-tuple-element.27.refs_0_), channel_id=1, source_target_pairs={{0,3},{1,0},{2,1},{3,2},{4,7},{5,4},{6,5},{7,6},{8,11},{9,8},{10,9... | collective-permute-start | bytes 147464 | tf_op jit(solution)/shard_map/ppermute | solution.py:285
  33.2 0.4 collective-permute-start.1
  33.5 0.1 collective-permute-start
  33.7 1.6 %collective-permute-start.5 = (bf16[32,512]{1,0:T(8,128)(2,1)S(1)}, bf16[32,512]{1,0:T(8,128)(2,1)S(1)}, u32[]{:S(2)}, u32[]{:S(2)}) collective-permute-start(bf16[32,512]{1,0:T(8,128)(2,1)S(1)} %get-tuple-element.28.refs_4_), channel_id=1, source_target_pairs={{0,3},{1,0},{2,1},{3,2},{4,7},{5,4},{6,5},{7,6},{8,11},{9,8},{10,9... | collective-permute-start | bytes 98312 | tf_op jit(solution)/shard_map/ppermute | solution.py:285
  35.3 1.7 %collective-permute-start.4 = (bf16[32,512]{1,0:T(8,128)(2,1)S(1)}, bf16[32,512]{1,0:T(8,128)(2,1)S(1)}, u32[]{:S(2)}, u32[]{:S(2)}) collective-permute-start(bf16[32,512]{1,0:T(8,128)(2,1)S(1)} %get-tuple-element.28.refs_4_), channel_id=1, source_target_pairs={{0,2},{1,3},{2,0},{3,1},{4,6},{5,7},{6,4},{7,5},{8,10},{9,11},{10,... | collective-permute-start | bytes 98312 | tf_op jit(solution)/shard_map/ppermute | solution.py:285
  36.9 0.0 collective-permute-done.2.refs_3_
  36.9 0.0 collective-permute-start.3
  37.0 1.8 %collective-permute-done.1.refs_2_ = bf16[48,512]{1,0:T(8,128)(2,1)S(1)} collective-permute-done((bf16[48,512]{1,0:T(8,128)(2,1)S(1)}, bf16[48,512]{1,0:T(8,128)(2,1)S(1)}, u32[]{:S(2)}, u32[]{:S(2)}) %collective-permute-start.1) | collective-permute-done | bytes 49184 | tf_op jit(solution)/shard_map/ppermute | solution.py:285
  38.8 0.0 collective-permute-done.refs_1_
  38.8 0.0 collective-permute-done.5.refs_7_
  38.8 1.5 %collective-permute-done.4.refs_6_ = bf16[32,512]{1,0:T(8,128)(2,1)S(1)} collective-permute-done((bf16[32,512]{1,0:T(8,128)(2,1)S(1)}, bf16[32,512]{1,0:T(8,128)(2,1)S(1)}, u32[]{:S(2)}, u32[]{:S(2)}) %collective-permute-start.4) | collective-permute-done | bytes 32800 | tf_op jit(solution)/shard_map/ppermute | solution.py:285
  40.3 0.3 collective-permute-done.3.refs_5_
  40.6 0.4 gather.1
  41.0 1.2 %all-to-all-done.1.y2 = bf16[32,32,128]{2,1,0:T(8,128)(2,1)S(1)} async-done(((bf16[32,32,128]{2,1,0:T(8,128)(2,1)}), bf16[32,32,128]{2,1,0:T(8,128)(2,1)S(1)}, u32[]{:S(2)}, u32[]{:S(2)}) %all-to-all-start.1) | async-done | bytes 262176 | tf_op jit(solution)/shard_map/all_to_all | solution.py:299
  42.2 0.0 copy-done.3
  42.2 1.6 %second.1 = (bf16[8,64,128]{2,1,0:T(8,128)(2,1)}, bf16[2,64,512]{2,1,0:T(8,128)(2,1)S(1)}, bf16[2,16,512]{2,1,0:T(8,128)(2,1)S(1)}) custom-call(bf16[32,32,128]{2,1,0:T(8,128)(2,1)S(1)} %all-to-all-done.1.y2, bf16[8,16,128]{2,1,0:T(8,128)(2,1)S(1)} %get-tuple-element.26.marks_ref, bf16[512,1536]{1,0:T(8,128)(2,1)S(1)} %get-tuple-element.22.op.refs_8_, ...), custom_call_target="tpu_custom_call" | custom-call | tf_op jit(solution)/shard_map/second/pallas_call | solution.py:319
  43.8 4.6 %all-to-all-start.2 = ((bf16[8,64,128]{2,1,0:T(8,128)(2,1)}), bf16[8,64,128]{2,1,0:T(8,128)(2,1)S(1)}, u32[]{:S(2)}, u32[]{:S(2)}) async-start(bf16[8,64,128]{2,1,0:T(8,128)(2,1)} %get-tuple-element.34), calls=%async_computation.2 | async-start | bytes 262144 | tf_op jit(solution)/shard_map/all_to_all | solution.py:328
  48.4 0.4 local.1
  48.8 7.0 %all-to-all-done.2.y3 = bf16[8,64,128]{2,1,0:T(8,128)(2,1)S(1)} async-done(((bf16[8,64,128]{2,1,0:T(8,128)(2,1)}), bf16[8,64,128]{2,1,0:T(8,128)(2,1)S(1)}, u32[]{:S(2)}, u32[]{:S(2)}) %all-to-all-start.2) | async-done | bytes 131104 | tf_op jit(solution)/shard_map/all_to_all | solution.py:328
  55.7 1.0 %last.1 = (bf16[16,512]{1,0:T(8,128)(2,1)}, bf16[16,512]{1,0:T(8,128)(2,1)}, f32[4,16,64]{2,1,0:T(8,128)}) custom-call(bf16[8,64,128]{2,1,0:T(8,128)(2,1)S(1)} %all-to-all-done.2.y3, bf16[8,16,128]{2,1,0:T(8,128)(2,1)S(1)} %get-tuple-element.26.marks_ref, bf16[512,1536]{1,0:T(8,128)(2,1)S(1)} %get-tuple-element.22.op.refs_8_, ...), custom_call_target="tpu_custom_call" | custom-call | tf_op jit(solution)/shard_map/last/pallas_call | solution.py:340
Async XLA Ops:
  0.6 18.0 %copy-start.9 = (s32[4,20]{1,0:T(4,128)S(1)}, s32[4,20]{1,0:T(4,128)}, u32[]{:S(2)}) copy-start(s32[4,20]{1,0:T(4,128)} %cols.3) | copy-start | bytes 964
  1.4 1.7 %copy-start = (bf16[4,20,128,128]{3,2,1,0:T(8,128)(2,1)S(1)}, bf16[4,20,128,128]{3,2,1,0:T(8,128)(2,1)}, u32[]{:S(2)}) copy-start(bf16[4,20,128,128]{3,2,1,0:T(8,128)(2,1)} %tiles.3) | copy-start | bytes 7864324
  3.1 0.7 %copy-start.2 = (bf16[4,16,64]{2,1,0:T(8,128)(2,1)S(1)}, bf16[4,16,64]{2,1,0:T(8,128)(2,1)}, u32[]{:S(2)}) copy-start(bf16[4,16,64]{2,1,0:T(8,128)(2,1)} %w.5) | copy-start | bytes 24580
  3.8 0.7 %copy-start.4 = (bf16[16,512]{1,0:T(8,128)(2,1)S(1)}, bf16[16,512]{1,0:T(8,128)(2,1)}, u32[]{:S(2)}) copy-start(bf16[16,512]{1,0:T(8,128)(2,1)} %f.3) | copy-start | bytes 49156
  4.6 0.7 %copy-start.6 = (bf16[16,512]{1,0:T(8,128)(2,1)S(1)}, bf16[16,512]{1,0:T(8,128)(2,1)}, u32[]{:S(2)}) copy-start(bf16[16,512]{1,0:T(8,128)(2,1)} %c.3) | copy-start | bytes 49156
  5.3 0.7 %copy-start.8 = (s32[4,20]{1,0:T(4,128)S(1)}, s32[4,20]{1,0:T(4,128)}, u32[]{:S(2)}) copy-start(s32[4,20]{1,0:T(4,128)} %cols.3) | copy-start | bytes 964
  6.0 12.7 %copy-start.5 = (bf16[16,512]{1,0:T(8,128)(2,1)S(1)}, bf16[16,512]{1,0:T(8,128)(2,1)}, u32[]{:S(2)}) copy-start(bf16[16,512]{1,0:T(8,128)(2,1)} %f.3) | copy-start | bytes 49156
  6.0 12.7 %copy-start.7 = (bf16[16,512]{1,0:T(8,128)(2,1)S(1)}, bf16[16,512]{1,0:T(8,128)(2,1)}, u32[]{:S(2)}) copy-start(bf16[16,512]{1,0:T(8,128)(2,1)} %c.3) | copy-start | bytes 49156
  11.3 15.2 %all-to-all-start = ((bf16[8,96,128]{2,1,0:T(8,128)(2,1)}), bf16[8,96,128]{2,1,0:T(8,128)(2,1)S(1)}, u32[]{:S(2)}, u32[]{:S(2)}) async-start(bf16[8,96,128]{2,1,0:T(8,128)(2,1)} %get-tuple-element.21), calls=%async_computation | async-start | bytes 393216 | tf_op jit(solution)/shard_map/all_to_all | solution.py:259
  18.6 1.7 %copy-start.1 = (bf16[4,20,128,128]{3,2,1,0:T(8,128)(2,1)S(1)}, bf16[4,20,128,128]{3,2,1,0:T(8,128)(2,1)}, u32[]{:S(2)}) copy-start(bf16[4,20,128,128]{3,2,1,0:T(8,128)(2,1)} %tiles.3) | copy-start | bytes 7864324
  23.0 19.2 %copy-start.3 = (bf16[4,16,64]{2,1,0:T(8,128)(2,1)S(1)}, bf16[4,16,64]{2,1,0:T(8,128)(2,1)}, u32[]{:S(2)}) copy-start(bf16[4,16,64]{2,1,0:T(8,128)(2,1)} %w.5) | copy-start | bytes 24580
  28.4 13.8 %all-to-all-start.1 = ((bf16[32,32,128]{2,1,0:T(8,128)(2,1)}), bf16[32,32,128]{2,1,0:T(8,128)(2,1)S(1)}, u32[]{:S(2)}, u32[]{:S(2)}) async-start(bf16[32,32,128]{2,1,0:T(8,128)(2,1)} %get-tuple-element.25), calls=%async_computation.1 | async-start | bytes 524288 | tf_op jit(solution)/shard_map/all_to_all | solution.py:299
  31.6 5.4 %collective-permute-start.2 = (bf16[48,512]{1,0:T(8,128)(2,1)S(1)}, bf16[48,512]{1,0:T(8,128)(2,1)S(1)}, u32[]{:S(2)}, u32[]{:S(2)}) collective-permute-start(bf16[48,512]{1,0:T(8,128)(2,1)S(1)} %get-tuple-element.27.refs_0_), channel_id=1, source_target_pairs={{0,3},{1,0},{2,1},{3,2},{4,7},{5,4},{6,5},{7,6},{8,11},{9,8},{10,9... | collective-permute-start | bytes 147464 | tf_op jit(solution)/shard_map/ppermute | solution.py:285
  33.2 5.6 %collective-permute-start.1 = (bf16[48,512]{1,0:T(8,128)(2,1)S(1)}, bf16[48,512]{1,0:T(8,128)(2,1)S(1)}, u32[]{:S(2)}, u32[]{:S(2)}) collective-permute-start(bf16[48,512]{1,0:T(8,128)(2,1)S(1)} %get-tuple-element.27.refs_0_), channel_id=1, source_target_pairs={{0,2},{1,3},{2,0},{3,1},{4,6},{5,7},{6,4},{7,5},{8,10},{9,11},{10,... | collective-permute-start | bytes 147464 | tf_op jit(solution)/shard_map/ppermute | solution.py:285
  33.5 5.2 %collective-permute-start = (bf16[48,512]{1,0:T(8,128)(2,1)S(1)}, bf16[48,512]{1,0:T(8,128)(2,1)S(1)}, u32[]{:S(2)}, u32[]{:S(2)}) collective-permute-start(bf16[48,512]{1,0:T(8,128)(2,1)S(1)} %get-tuple-element.27.refs_0_), channel_id=1, source_target_pairs={{0,1},{1,2},{2,3},{3,0},{4,5},{5,6},{6,7},{7,4},{8,9},{9,10},{10,1... | collective-permute-start | bytes 147464 | tf_op jit(solution)/shard_map/ppermute | solution.py:285
  33.7 5.1 %collective-permute-start.5 = (bf16[32,512]{1,0:T(8,128)(2,1)S(1)}, bf16[32,512]{1,0:T(8,128)(2,1)S(1)}, u32[]{:S(2)}, u32[]{:S(2)}) collective-permute-start(bf16[32,512]{1,0:T(8,128)(2,1)S(1)} %get-tuple-element.28.refs_4_), channel_id=1, source_target_pairs={{0,3},{1,0},{2,1},{3,2},{4,7},{5,4},{6,5},{7,6},{8,11},{9,8},{10,9... | collective-permute-start | bytes 98312 | tf_op jit(solution)/shard_map/ppermute | solution.py:285
  35.3 5.0 %collective-permute-start.4 = (bf16[32,512]{1,0:T(8,128)(2,1)S(1)}, bf16[32,512]{1,0:T(8,128)(2,1)S(1)}, u32[]{:S(2)}, u32[]{:S(2)}) collective-permute-start(bf16[32,512]{1,0:T(8,128)(2,1)S(1)} %get-tuple-element.28.refs_4_), channel_id=1, source_target_pairs={{0,2},{1,3},{2,0},{3,1},{4,6},{5,7},{6,4},{7,5},{8,10},{9,11},{10,... | collective-permute-start | bytes 98312 | tf_op jit(solution)/shard_map/ppermute | solution.py:285
  36.9 3.7 %collective-permute-start.3 = (bf16[32,512]{1,0:T(8,128)(2,1)S(1)}, bf16[32,512]{1,0:T(8,128)(2,1)S(1)}, u32[]{:S(2)}, u32[]{:S(2)}) collective-permute-start(bf16[32,512]{1,0:T(8,128)(2,1)S(1)} %get-tuple-element.28.refs_4_), channel_id=1, source_target_pairs={{0,1},{1,2},{2,3},{3,0},{4,5},{5,6},{6,7},{7,4},{8,9},{9,10},{10,1... | collective-permute-start | bytes 98312 | tf_op jit(solution)/shard_map/ppermute | solution.py:285
  43.8 11.9 %all-to-all-start.2 = ((bf16[8,64,128]{2,1,0:T(8,128)(2,1)}), bf16[8,64,128]{2,1,0:T(8,128)(2,1)S(1)}, u32[]{:S(2)}, u32[]{:S(2)}) async-start(bf16[8,64,128]{2,1,0:T(8,128)(2,1)} %get-tuple-element.34), calls=%async_computation.2 | async-start | bytes 262144 | tf_op jit(solution)/shard_map/all_to_all | solution.py:328

commit v2 on v1

--- a/solution.py
+++ b/solution.py
@@ -26,68 +26,72 @@
     return pl.ds(pl.multiple_of(index * width, width), width)
 
 
-def push_kernel(cols, needs, f, c, w, tiles, x1, pack, cells, where, buf, acc, sems):
+def push_kernel(cols_h, needs_h, f_h, c_h, w_h, tiles, x1, pack, cols, needs, cells, where, f, c, w, buf, acc, sems):
     nb, tpr = cols.shape
     n, ci, bw = acc.shape
-
-    def scan(i, count):
-        r = i // (tpr - 1)
-        t = i % (tpr - 1) + 1
-        v = cols[r, t]
-        ghost = v >= nb
-
-        @pl.when(ghost)
-        def _():
+    small = [(cols_h, cols), (needs_h, needs), (f_h, f), (c_h, c), (w_h, w)]
+    copies = [pltpu.make_async_copy(src, dst, sems.at[i]) for i, (src, dst) in enumerate(small)]
+    for r in range(nb):
+        copies.append(pltpu.make_async_copy(tiles.at[r], buf.at[pl.ds(r * tpr, tpr)], sems.at[len(small) + r]))
+    for copy in copies:
+        copy.start()
+    for o in range(n):
+        acc[o] = jnp.zeros((ci, bw), F32)
+    copies[0].wait()
+    count = jnp.int32(0)
+    for r in range(nb):
+        for t in range(1, tpr):
+            v = cols[r, t]
             cells[count] = v - nb
-            where[count] = r
-            pltpu.make_async_copy(tiles.at[r, t], buf.at[count], sems.at[count]).start()
-
-        return count + ghost.astype(jnp.int32)
-
-    count = lax.fori_loop(0, nb * (tpr - 1), scan, 0)
-    for o in range(n):
-        acc[o] = jnp.zeros((ci, bw), F32)
+            where[count] = r * tpr + t
+            count = count + (v >= nb).astype(jnp.int32)
+    for copy in copies[1:5]:
+        copy.wait()
+    for o in range(n):
         for b in range(nb):
             x1[o, b * ci : (b + 1) * ci, :] = f[:, b * bw : (b + 1) * bw]
-        x1[o, (nb + 1) * ci :, :] = jnp.full((ci, bw), needs[0, o, 0].astype(F32)).astype(BF)
+        x1[o, (nb + 1) * ci :, :] = jnp.full((ci, bw), needs[0, o].astype(F32)).astype(BF)
     pack[0:ci] = f[...]
     pack[ci : 2 * ci] = c[...]
     for k in range(K):
         width = w.shape[2]
         pack[2 * ci :, k * width : (k + 1) * width] = w[k]
-
-    def product(i, carry):
-        pltpu.make_async_copy(tiles.at[0, 0], buf.at[i], sems.at[i]).wait()
-        o = cells[i]
-        acc[o] += nn(c[:, lanes(where[i], bw)], buf[i])
+    for copy in copies[5:]:
+        copy.wait()
+
+    def products(step, carry):
+        for j in range(n):
+            i = jnp.minimum(step * n + j, nb * tpr - 1)
+            live = i < count
+            o = jnp.where(live, cells[i], 0)
+            at = jnp.where(live, where[i], 0)
+            part = nn(c[:, lanes(at // tpr, bw)], buf[at])
+            acc[o] += jnp.where(live, part, 0.0)
         return carry
 
-    lax.fori_loop(0, count, product, 0)
+    lax.fori_loop(0, (count + n - 1) // n, products, 0)
     for o in range(n):
         x1[o, nb * ci : (nb + 1) * ci, :] = acc[o].astype(BF)
 
 
-def combine_kernel(cols, f, c, tiles, op, lf, ltc, total):
-    r = pl.program_id(0)
-    tpr = tiles.shape[1]
+def combine_kernel(cols, f, c, tiles, op, lf, ltc, total, buf, sems):
+    nb, tpr = cols.shape
     bw = tiles.shape[2]
     own = f.shape[1]
-    total[...] = jnp.zeros_like(total)
-    for t in range(tpr):
-        at = lanes(cols[r, t], bw)
-        total[:, at] += tiles[0, t].astype(F32)
-    op[...] = total[...].astype(BF)
+    copies = [pltpu.make_async_copy(tiles.at[r], buf.at[r], sems.at[r]) for r in range(nb)]
+    for copy in copies:
+        copy.start()
+    for r in range(nb):
+        rows = slice(r * bw, (r + 1) * bw)
+        total[...] = jnp.zeros_like(total)
+        copies[r].wait()
+        for t in range(tpr):
+            at = lanes(cols[r, t], bw)
+            total[:, at] += buf[r, t].astype(F32)
+        op[rows, :] = total[...].astype(BF)
     local = op[:, :own]
     lf[...] = nt(f[...], local)
-    part = nn(c[:, lanes(r, bw)], local)
-
-    @pl.when(r == 0)
-    def _():
-        ltc[...] = part
-
-    @pl.when(r > 0)
-    def _():
-        ltc[...] += part
+    ltc[...] = nn(c[...], local)
 
 
 def first_kernel(needs, y1, op, lf, ltc, x2, tu, marks_ref, gh):
@@ -96,7 +100,7 @@
     nb = own // bw
     q = x2.shape[0] // n
     for o in range(n):
-        at = jnp.maximum(needs[0, o, 0], 0) * ci
+        at = jnp.maximum(needs[0, o], 0) * ci
         gh[:, o * bw : (o + 1) * bw] = y1[o, pl.ds(pl.multiple_of(at, ci), ci), :]
     t1 = (lf[...] + nt(gh[...], op[:, own:])).astype(BF)
     marks = [y1[o, (nb + 1) * ci :, :].astype(F32) for o in range(n)]
@@ -238,43 +242,45 @@
     struct = jax.ShapeDtypeStruct
     smem = pl.BlockSpec(memory_space=SMEM)
     vmem = pl.BlockSpec(memory_space=VMEM)
+    hbm = pl.BlockSpec(memory_space=pltpu.MemorySpace.HBM)
     limit = (16 << 20) + 4 * own * wide * 2
     params = pltpu.CompilerParams(vmem_limit_bytes=limit)
-
+    packed = pltpu.CompilerParams(vmem_limit_bytes=62 << 20)
+
+    needs = needs.reshape(1, n)
     x1, pack = pl.pallas_call(
         push_kernel,
         out_shape=(struct((n, (nb + 2) * ci, bw), BF), struct((3 * ci, own), BF)),
-        in_specs=[smem, smem, vmem, vmem, vmem, pl.BlockSpec(memory_space=pl.ANY)],
+        in_specs=[hbm] * 6,
         out_specs=(vmem, vmem),
         scratch_shapes=[
+            pltpu.SMEM((nb, tpr), jnp.int32),
+            pltpu.SMEM((1, n), jnp.int32),
             pltpu.SMEM((nb * tpr,), jnp.int32),
             pltpu.SMEM((nb * tpr,), jnp.int32),
+            pltpu.VMEM((ci, own), BF),
+            pltpu.VMEM((ci, own), BF),
+            pltpu.VMEM((K, ci, co), BF),
             pltpu.VMEM((nb * tpr, bw, bw), BF),
             pltpu.VMEM((n, ci, bw), F32),
-            pltpu.SemaphoreType.DMA((nb * tpr,)),
+            pltpu.SemaphoreType.DMA((5 + nb,)),
         ],
-        compiler_params=params,
+        compiler_params=packed,
         name="push",
     )(tile_cols, needs, features, cotangent, weights, tiles)
     y1 = lax.all_to_all(x1, "rows", 0, 0)
 
     op, lf, ltc = pl.pallas_call(
         combine_kernel,
-        grid=(nb,),
         out_shape=(struct((own, wide), BF), struct((ci, own), F32), struct((ci, own), F32)),
-        in_specs=[
-            smem,
-            pl.BlockSpec((ci, own), lambda r: (0, 0)),
-            pl.BlockSpec((ci, own), lambda r: (0, 0)),
-            pl.BlockSpec((1, tpr, bw, bw), lambda r: (r, 0, 0, 0)),
+        in_specs=[smem, vmem, vmem, hbm],
+        out_specs=(vmem,) * 3,
+        scratch_shapes=[
+            pltpu.VMEM((bw, wide), F32),
+            pltpu.VMEM((nb, tpr, bw, bw), BF),
+            pltpu.SemaphoreType.DMA((nb,)),
         ],
-        out_specs=(
-            pl.BlockSpec((bw, wide), lambda r: (r, 0)),
-            pl.BlockSpec((ci, bw), lambda r: (0, r)),
-            pl.BlockSpec((ci, own), lambda r: (0, 0)),
-        ),
-        scratch_shapes=[pltpu.VMEM((bw, wide), F32)],
-        compiler_params=params,
+        compiler_params=pltpu.CompilerParams(vmem_limit_bytes=51 << 20),
         cost_estimate=pl.CostEstimate(flops=4 * ci * own * own, bytes_accessed=8 << 20, transcendentals=0),
         name="combine",
     )(tile_cols, features, cotangent, tiles)
@@ -286,6 +292,7 @@
         return moved
 
     packs = around(pack)
+    y1, *packs = lax.optimization_barrier((y1, *packs))
 
     x2, tu, marks = pl.pallas_call(
         first_kernel,

time: 57.5 us -> 48 us (0.83)
  local copies, waits for them, and re-layouts: 7.06 us -> 0.03 us
  waiting for transfers between devices: 15.4 us -> 18 us
  starting transfers between devices: 20.4 us -> 17.8 us
  Pallas kernels: 13.1 us -> 11 us
    unnamed x21 -> x12, local copies, waits for them, and re-layouts: 7.06 us -> 0.03 us
    pallas_call x1, Pallas kernels: 5.37 us -> 2.71 us  [body(): pl.pallas_call(push_kernel, out_shape=(struct((n, (nb + 2) * ci, bw), BF)...]
    all_to_all x1, waiting for transfers between devices: 1.2 us -> 3.69 us  [body(): y2 = lax.all_to_all(x2, ('rows', 'ch'), 0, 0)]
    ppermute x6, starting transfers between devices: 5.36 us -> 3.83 us  [around(): lax.ppermute(value, 'ch', [(i, (i + s) % q) for i in range(q)])]
    ppermute x6, waiting for transfers between devices: 3.64 us -> 4.96 us  [around(): lax.ppermute(value, 'ch', [(i, (i + s) % q) for i in range(q)])]
    all_to_all x1, starting transfers between devices: 4.6 us -> 3.37 us  [body(): y3 = lax.all_to_all(x3, 'rows', 0, 0)]
    all_to_all x1, waiting for transfers between devices: 3.58 us -> 2.45 us  [body(): y1 = lax.all_to_all(x1, 'rows', 0, 0)]
    pallas_call x1, Pallas kernels: 2.58 us -> 3.18 us  [body(): pl.pallas_call(combine_kernel, out_shape=(struct((own, wide), BF), struct...]
  transfers between devices with their start and end apart: 9 -> 9, of which waited for: 6 -> 7; matrix products, arithmetic and copies ran while one was open for 0% -> 0% of each run, Pallas kernels for 6% -> 8%
where the time goes in v2:
time: 48 us; the launch traced here: 47.6 us
  waiting for transfers between devices  18 us (38%)
  starting transfers between devices  17.8 us (37%)
  Pallas kernels  11 us (23%)
  between operations  0.73 us (2%)
    all_to_all x1, starting transfers between devices, body(): y1 = lax.all_to_all(x1, 'rows', 0, 0)  7.4 us
    all_to_all x1, waiting for transfers between devices, body(): y3 = lax.all_to_all(x3, 'rows', 0, 0)  6.89 us
    ppermute x6, waiting for transfers between devices, around(): lax.ppermute(value, 'ch', [(i, (i + s) % q) for i in range(q)])  4.96 us
    ppermute x6, starting transfers between devices, around(): lax.ppermute(value, 'ch', [(i, (i + s) % q) for i in range(q)])  3.83 us
    all_to_all x1, waiting for transfers between devices, body(): y2 = lax.all_to_all(x2, ('rows', 'ch'), 0, 0)  3.69 us
    all_to_all x1, starting transfers between devices, body(): y3 = lax.all_to_all(x3, 'rows', 0, 0)  3.37 us
    all_to_all x1, starting transfers between devices, body(): y2 = lax.all_to_all(x2, ('rows', 'ch'), 0, 0)  3.19 us
    pallas_call x1, Pallas kernels, body(): pl.pallas_call(combine_kernel, out_shape=(struct((own, wide), BF), struct...  3.18 us
  transfers between devices with their start and end apart: 9, of which 7 were waited for; matrix products, arithmetic and copies ran while one was open for 0% of the time, Pallas kernels for 8%

profile of v2, /device:TPU:0, one launch (start us, length us, event | category | flops | bytes accessed | tf_op | source)
XLA Modules:
  0.0 47.6 jit_solution(17708450061800811482)
XLA Ops:
  0.6 0.0 copy-start.2
  0.6 0.0 copy-start.4
  0.7 0.0 copy-start.1
  0.7 0.0 copy-start.5
  0.7 2.7 %push.1 = (bf16[8,96,128]{2,1,0:T(8,128)(2,1)}, bf16[48,512]{1,0:T(8,128)(2,1)}) custom-call(s32[4,20]{1,0:T(4,128)} %cols.1, s32[1,8]{1,0:T(1,128)} %bitcast.1, bf16[16,512]{1,0:T(8,128)(2,1)} %f.1, bf16[16,512]{1,0:T(8,128)(2,1)} %c.1, bf16[4,16,64]{2,1,0:T(8,128)(2,1)} %w.3, bf16[4,20,128,128]{3,2,1,0:T(8,128)(2,1)} %tiles.3), custom_call_target="tpu_custom_call" | custom-call | tf_op jit(solution)/shard_map/push/pallas_call | solution.py:251
  3.4 0.0 copy-start.3
  3.4 7.4 %all-to-all-start = ((bf16[8,96,128]{2,1,0:T(8,128)(2,1)}), bf16[8,96,128]{2,1,0:T(8,128)(2,1)S(1)}, u32[]{:S(2)}, u32[]{:S(2)}) async-start(bf16[8,96,128]{2,1,0:T(8,128)(2,1)} %get-tuple-element.26), calls=%async_computation | async-start | bytes 393216 | tf_op jit(solution)/shard_map/all_to_all | solution.py:271
  10.8 0.7 %collective-permute-start.2 = (bf16[48,512]{1,0:T(8,128)(2,1)}, bf16[48,512]{1,0:T(8,128)(2,1)S(1)}, u32[]{:S(2)}, u32[]{:S(2)}) collective-permute-start(bf16[48,512]{1,0:T(8,128)(2,1)} %get-tuple-element.34.refs_0_), channel_id=1, source_target_pairs={{0,3},{1,0},{2,1},{3,2},{4,7},{5,4},{6,5},{7,6},{8,11},{9,8},{10,9... | collective-permute-start | bytes 147464 | tf_op jit(solution)/shard_map/ppermute | solution.py:291
  11.5 0.9 %collective-permute-start.1 = (bf16[48,512]{1,0:T(8,128)(2,1)}, bf16[48,512]{1,0:T(8,128)(2,1)S(1)}, u32[]{:S(2)}, u32[]{:S(2)}) collective-permute-start(bf16[48,512]{1,0:T(8,128)(2,1)} %get-tuple-element.34.refs_0_), channel_id=1, source_target_pairs={{0,2},{1,3},{2,0},{3,1},{4,6},{5,7},{6,4},{7,5},{8,10},{9,11},{10,... | collective-permute-start | bytes 147464 | tf_op jit(solution)/shard_map/ppermute | solution.py:291
  12.4 0.2 collective-permute-start
  12.5 0.0 copy-done.2
  12.5 0.0 copy-done.4
  12.6 0.0 copy-done.1
  12.6 3.2 %combine.1 = (bf16[512,1536]{1,0:T(8,128)(2,1)S(1)}, f32[16,512]{1,0:T(8,128)S(1)}, f32[16,512]{1,0:T(8,128)S(1)}) custom-call(s32[4,20]{1,0:T(4,128)S(1)} %copy-done.4, bf16[16,512]{1,0:T(8,128)(2,1)S(1)} %copy-done.1, bf16[16,512]{1,0:T(8,128)(2,1)S(1)} %copy-done.2, bf16[4,20,128,128]{3,2,1,0:T(8,128)(2,1)} %tiles.3), custom_call_target="tpu_custom_call" | custom-call | flops 16777216 | bytes 8388608 | tf_op jit(solution)/shard_map/combine/pallas_call | solution.py:273
  15.7 0.0 copy-start
  15.8 0.0 collective-permute-done.2.refs_3_
  15.8 0.2 collective-permute-done.1.refs_2_
  16.0 0.3 collective-permute-done.refs_1_
  16.3 2.4 %all-to-all-done.y1 = bf16[8,96,128]{2,1,0:T(8,128)(2,1)S(1)} async-done(((bf16[8,96,128]{2,1,0:T(8,128)(2,1)}), bf16[8,96,128]{2,1,0:T(8,128)(2,1)S(1)}, u32[]{:S(2)}, u32[]{:S(2)}) %all-to-all-start) | async-done | bytes 196640 | tf_op jit(solution)/shard_map/all_to_all | solution.py:271
  18.7 0.0 copy-done.5
  18.8 1.8 %first.1 = (bf16[32,32,128]{2,1,0:T(8,128)(2,1)}, bf16[32,512]{1,0:T(8,128)(2,1)S(1)}, bf16[8,16,128]{2,1,0:T(8,128)(2,1)S(1)}) custom-call(s32[1,8]{1,0:T(1,128)S(1)} %bitcast.2, bf16[8,96,128]{2,1,0:T(8,128)(2,1)S(1)} %all-to-all-done.y1, bf16[512,1536]{1,0:T(8,128)(2,1)S(1)} %get-tuple-element.29.op.refs_8_, f32[16,512]{1,0:T(8,128)S(1)} %get-tuple-element.30.lf, ...), custom_call_target="tpu_custom_call" | custom-call | tf_op jit(solution)/shard_map/first/pallas_call | solution.py:297
  20.5 3.2 %all-to-all-start.1 = ((bf16[32,32,128]{2,1,0:T(8,128)(2,1)}), bf16[32,32,128]{2,1,0:T(8,128)(2,1)S(1)}, u32[]{:S(2)}, u32[]{:S(2)}) async-start(bf16[32,32,128]{2,1,0:T(8,128)(2,1)} %get-tuple-element.32), calls=%async_computation.1 | async-start | bytes 524288 | tf_op jit(solution)/shard_map/all_to_all | solution.py:306
  23.7 1.6 %collective-permute-start.5 = (bf16[32,512]{1,0:T(8,128)(2,1)S(1)}, bf16[32,512]{1,0:T(8,128)(2,1)S(1)}, u32[]{:S(2)}, u32[]{:S(2)}) collective-permute-start(bf16[32,512]{1,0:T(8,128)(2,1)S(1)} %get-tuple-element.38.refs_4_), channel_id=1, source_target_pairs={{0,3},{1,0},{2,1},{3,2},{4,7},{5,4},{6,5},{7,6},{8,11},{9,8},{10,9... | collective-permute-start | bytes 98312 | tf_op jit(solution)/shard_map/ppermute | solution.py:291
  25.3 0.4 collective-permute-start.4
  25.7 0.1 collective-permute-start.3
  25.8 2.0 %collective-permute-done.5.refs_7_ = bf16[32,512]{1,0:T(8,128)(2,1)S(1)} collective-permute-done((bf16[32,512]{1,0:T(8,128)(2,1)S(1)}, bf16[32,512]{1,0:T(8,128)(2,1)S(1)}, u32[]{:S(2)}, u32[]{:S(2)}) %collective-permute-start.5) | collective-permute-done | bytes 32800 | tf_op jit(solution)/shard_map/ppermute | solution.py:291
  27.8 2.4 %collective-permute-done.4.refs_6_ = bf16[32,512]{1,0:T(8,128)(2,1)S(1)} collective-permute-done((bf16[32,512]{1,0:T(8,128)(2,1)S(1)}, bf16[32,512]{1,0:T(8,128)(2,1)S(1)}, u32[]{:S(2)}, u32[]{:S(2)}) %collective-permute-start.4) | collective-permute-done | bytes 32800 | tf_op jit(solution)/shard_map/ppermute | solution.py:291
  30.2 0.0 collective-permute-done.3.refs_5_
  30.2 0.0 copy-done.3
  30.2 0.4 gather.1
  30.6 3.7 %all-to-all-done.1.y2 = bf16[32,32,128]{2,1,0:T(8,128)(2,1)S(1)} async-done(((bf16[32,32,128]{2,1,0:T(8,128)(2,1)}), bf16[32,32,128]{2,1,0:T(8,128)(2,1)S(1)}, u32[]{:S(2)}, u32[]{:S(2)}) %all-to-all-start.1) | async-done | bytes 262176 | tf_op jit(solution)/shard_map/all_to_all | solution.py:306
  34.3 0.0 copy-done
  34.3 1.6 %second.1 = (bf16[8,64,128]{2,1,0:T(8,128)(2,1)}, bf16[2,64,512]{2,1,0:T(8,128)(2,1)S(1)}, bf16[2,16,512]{2,1,0:T(8,128)(2,1)S(1)}) custom-call(bf16[32,32,128]{2,1,0:T(8,128)(2,1)S(1)} %all-to-all-done.1.y2, bf16[8,16,128]{2,1,0:T(8,128)(2,1)S(1)} %get-tuple-element.33.marks_ref, bf16[512,1536]{1,0:T(8,128)(2,1)S(1)} %get-tuple-element.29.op.refs_8_, ...), custom_call_target="tpu_custom_call" | custom-call | tf_op jit(solution)/shard_map/second/pallas_call | solution.py:326
  35.9 3.4 %all-to-all-start.2 = ((bf16[8,64,128]{2,1,0:T(8,128)(2,1)}), bf16[8,64,128]{2,1,0:T(8,128)(2,1)S(1)}, u32[]{:S(2)}, u32[]{:S(2)}) async-start(bf16[8,64,128]{2,1,0:T(8,128)(2,1)} %get-tuple-element.44), calls=%async_computation.2 | async-start | bytes 262144 | tf_op jit(solution)/shard_map/all_to_all | solution.py:335
  39.3 0.4 local.1
  39.7 6.9 %all-to-all-done.2.y3 = bf16[8,64,128]{2,1,0:T(8,128)(2,1)S(1)} async-done(((bf16[8,64,128]{2,1,0:T(8,128)(2,1)}), bf16[8,64,128]{2,1,0:T(8,128)(2,1)S(1)}, u32[]{:S(2)}, u32[]{:S(2)}) %all-to-all-start.2) | async-done | bytes 131104 | tf_op jit(solution)/shard_map/all_to_all | solution.py:335
  46.6 1.0 %last.1 = (bf16[16,512]{1,0:T(8,128)(2,1)}, bf16[16,512]{1,0:T(8,128)(2,1)}, f32[4,16,64]{2,1,0:T(8,128)}) custom-call(bf16[8,64,128]{2,1,0:T(8,128)(2,1)S(1)} %all-to-all-done.2.y3, bf16[8,16,128]{2,1,0:T(8,128)(2,1)S(1)} %get-tuple-element.33.marks_ref, bf16[512,1536]{1,0:T(8,128)(2,1)S(1)} %get-tuple-element.29.op.refs_8_, ...), custom_call_target="tpu_custom_call" | custom-call | tf_op jit(solution)/shard_map/last/pallas_call | solution.py:347
Async XLA Ops:
  0.6 11.9 %copy-start.2 = (bf16[16,512]{1,0:T(8,128)(2,1)S(1)}, bf16[16,512]{1,0:T(8,128)(2,1)}, u32[]{:S(2)}) copy-start(bf16[16,512]{1,0:T(8,128)(2,1)} %c.1) | copy-start | bytes 49156
  0.6 11.9 %copy-start.4 = (s32[4,20]{1,0:T(4,128)S(1)}, s32[4,20]{1,0:T(4,128)}, u32[]{:S(2)}) copy-start(s32[4,20]{1,0:T(4,128)} %cols.1) | copy-start | bytes 964
  0.7 11.9 %copy-start.1 = (bf16[16,512]{1,0:T(8,128)(2,1)S(1)}, bf16[16,512]{1,0:T(8,128)(2,1)}, u32[]{:S(2)}) copy-start(bf16[16,512]{1,0:T(8,128)(2,1)} %f.1) | copy-start | bytes 49156
  0.7 18.1 %copy-start.5 = (s32[1,8,1]{1,2,0:T(1,128)S(1)}, s32[1,8,1]{1,2,0:T(1,128)}, u32[]{:S(2)}) copy-start(s32[1,8,1]{1,2,0:T(1,128)} %param.9) | copy-start | bytes 100
  3.4 26.8 %copy-start.3 = (bf16[48,512]{1,0:T(8,128)(2,1)S(1)}, bf16[48,512]{1,0:T(8,128)(2,1)}, u32[]{:S(2)}) copy-start(bf16[48,512]{1,0:T(8,128)(2,1)} %get-tuple-element.34.refs_0_) | copy-start | bytes 147460
  3.4 15.3 %all-to-all-start = ((bf16[8,96,128]{2,1,0:T(8,128)(2,1)}), bf16[8,96,128]{2,1,0:T(8,128)(2,1)S(1)}, u32[]{:S(2)}, u32[]{:S(2)}) async-start(bf16[8,96,128]{2,1,0:T(8,128)(2,1)} %get-tuple-element.26), calls=%async_computation | async-start | bytes 393216 | tf_op jit(solution)/shard_map/all_to_all | solution.py:271
  10.8 5.0 %collective-permute-start.2 = (bf16[48,512]{1,0:T(8,128)(2,1)}, bf16[48,512]{1,0:T(8,128)(2,1)S(1)}, u32[]{:S(2)}, u32[]{:S(2)}) collective-permute-start(bf16[48,512]{1,0:T(8,128)(2,1)} %get-tuple-element.34.refs_0_), channel_id=1, source_target_pairs={{0,3},{1,0},{2,1},{3,2},{4,7},{5,4},{6,5},{7,6},{8,11},{9,8},{10,9... | collective-permute-start | bytes 147464 | tf_op jit(solution)/shard_map/ppermute | solution.py:291
  11.5 4.5 %collective-permute-start.1 = (bf16[48,512]{1,0:T(8,128)(2,1)}, bf16[48,512]{1,0:T(8,128)(2,1)S(1)}, u32[]{:S(2)}, u32[]{:S(2)}) collective-permute-start(bf16[48,512]{1,0:T(8,128)(2,1)} %get-tuple-element.34.refs_0_), channel_id=1, source_target_pairs={{0,2},{1,3},{2,0},{3,1},{4,6},{5,7},{6,4},{7,5},{8,10},{9,11},{10,... | collective-permute-start | bytes 147464 | tf_op jit(solution)/shard_map/ppermute | solution.py:291
  12.4 3.9 %collective-permute-start = (bf16[48,512]{1,0:T(8,128)(2,1)}, bf16[48,512]{1,0:T(8,128)(2,1)S(1)}, u32[]{:S(2)}, u32[]{:S(2)}) collective-permute-start(bf16[48,512]{1,0:T(8,128)(2,1)} %get-tuple-element.34.refs_0_), channel_id=1, source_target_pairs={{0,1},{1,2},{2,3},{3,0},{4,5},{5,6},{6,7},{7,4},{8,9},{9,10},{10,1... | collective-permute-start | bytes 147464 | tf_op jit(solution)/shard_map/ppermute | solution.py:291
  15.7 18.6 %copy-start = (bf16[4,16,64]{2,1,0:T(8,128)(2,1)S(1)}, bf16[4,16,64]{2,1,0:T(8,128)(2,1)}, u32[]{:S(2)}) copy-start(bf16[4,16,64]{2,1,0:T(8,128)(2,1)} %w.3) | copy-start | bytes 24580
  20.5 13.8 %all-to-all-start.1 = ((bf16[32,32,128]{2,1,0:T(8,128)(2,1)}), bf16[32,32,128]{2,1,0:T(8,128)(2,1)S(1)}, u32[]{:S(2)}, u32[]{:S(2)}) async-start(bf16[32,32,128]{2,1,0:T(8,128)(2,1)} %get-tuple-element.32), calls=%async_computation.1 | async-start | bytes 524288 | tf_op jit(solution)/shard_map/all_to_all | solution.py:306
  23.7 4.1 %collective-permute-start.5 = (bf16[32,512]{1,0:T(8,128)(2,1)S(1)}, bf16[32,512]{1,0:T(8,128)(2,1)S(1)}, u32[]{:S(2)}, u32[]{:S(2)}) collective-permute-start(bf16[32,512]{1,0:T(8,128)(2,1)S(1)} %get-tuple-element.38.refs_4_), channel_id=1, source_target_pairs={{0,3},{1,0},{2,1},{3,2},{4,7},{5,4},{6,5},{7,6},{8,11},{9,8},{10,9... | collective-permute-start | bytes 98312 | tf_op jit(solution)/shard_map/ppermute | solution.py:291
  25.3 4.9 %collective-permute-start.4 = (bf16[32,512]{1,0:T(8,128)(2,1)S(1)}, bf16[32,512]{1,0:T(8,128)(2,1)S(1)}, u32[]{:S(2)}, u32[]{:S(2)}) collective-permute-start(bf16[32,512]{1,0:T(8,128)(2,1)S(1)} %get-tuple-element.38.refs_4_), channel_id=1, source_target_pairs={{0,2},{1,3},{2,0},{3,1},{4,6},{5,7},{6,4},{7,5},{8,10},{9,11},{10,... | collective-permute-start | bytes 98312 | tf_op jit(solution)/shard_map/ppermute | solution.py:291
  25.7 4.6 %collective-permute-start.3 = (bf16[32,512]{1,0:T(8,128)(2,1)S(1)}, bf16[32,512]{1,0:T(8,128)(2,1)S(1)}, u32[]{:S(2)}, u32[]{:S(2)}) collective-permute-start(bf16[32,512]{1,0:T(8,128)(2,1)S(1)} %get-tuple-element.38.refs_4_), channel_id=1, source_target_pairs={{0,1},{1,2},{2,3},{3,0},{4,5},{5,6},{6,7},{7,4},{8,9},{9,10},{10,1... | collective-permute-start | bytes 98312 | tf_op jit(solution)/shard_map/ppermute | solution.py:291
  35.9 10.7 %all-to-all-start.2 = ((bf16[8,64,128]{2,1,0:T(8,128)(2,1)}), bf16[8,64,128]{2,1,0:T(8,128)(2,1)S(1)}, u32[]{:S(2)}, u32[]{:S(2)}) async-start(bf16[8,64,128]{2,1,0:T(8,128)(2,1)} %get-tuple-element.44), calls=%async_computation.2 | async-start | bytes 262144 | tf_op jit(solution)/shard_map/all_to_all | solution.py:335

commit v3 on v2

--- a/solution.py
+++ b/solution.py
@@ -26,10 +26,23 @@
     return pl.ds(pl.multiple_of(index * width, width), width)
 
 
-def push_kernel(cols_h, needs_h, f_h, c_h, w_h, tiles, x1, pack, cols, needs, cells, where, f, c, w, buf, acc, sems):
+def turn(n):
+    return 5 * n // 8
+
+
+def member(device, n):
+    return (device - turn(n)) % n
+
+
+def row_exchange(value, n):
+    order = [(i + turn(n)) % n for i in range(n)]
+    return lax.all_to_all(value, "rows", 0, 0, axis_index_groups=[order])
+
+
+def push_kernel(cols_h, needs_h, f_h, c_h, tiles, x1, cols, needs, cells, where, f, c, buf, acc, sems):
     nb, tpr = cols.shape
     n, ci, bw = acc.shape
-    small = [(cols_h, cols), (needs_h, needs), (f_h, f), (c_h, c), (w_h, w)]
+    small = [(cols_h, cols), (needs_h, needs), (f_h, f), (c_h, c)]
     copies = [pltpu.make_async_copy(src, dst, sems.at[i]) for i, (src, dst) in enumerate(small)]
     for r in range(nb):
         copies.append(pltpu.make_async_copy(tiles.at[r], buf.at[pl.ds(r * tpr, tpr)], sems.at[len(small) + r]))
@@ -45,18 +58,13 @@
             cells[count] = v - nb
             where[count] = r * tpr + t
             count = count + (v >= nb).astype(jnp.int32)
-    for copy in copies[1:5]:
+    for copy in copies[1:4]:
         copy.wait()
     for o in range(n):
         for b in range(nb):
-            x1[o, b * ci : (b + 1) * ci, :] = f[:, b * bw : (b + 1) * bw]
-        x1[o, (nb + 1) * ci :, :] = jnp.full((ci, bw), needs[0, o].astype(F32)).astype(BF)
-    pack[0:ci] = f[...]
-    pack[ci : 2 * ci] = c[...]
-    for k in range(K):
-        width = w.shape[2]
-        pack[2 * ci :, k * width : (k + 1) * width] = w[k]
-    for copy in copies[5:]:
+            x1[member(o, n), b * ci : (b + 1) * ci, :] = f[:, b * bw : (b + 1) * bw]
+        x1[member(o, n), (nb + 1) * ci :, :] = jnp.full((8, bw), needs[0, o].astype(F32)).astype(BF)
+    for copy in copies[4:]:
         copy.wait()
 
     def products(step, carry):
@@ -71,7 +79,7 @@
 
     lax.fori_loop(0, (count + n - 1) // n, products, 0)
     for o in range(n):
-        x1[o, nb * ci : (nb + 1) * ci, :] = acc[o].astype(BF)
+        x1[member(o, n), nb * ci : (nb + 1) * ci, :] = acc[o].astype(BF)
 
 
 def combine_kernel(cols, f, c, tiles, op, lf, ltc, total, buf, sems):
@@ -94,28 +102,35 @@
     ltc[...] = nn(c[...], local)
 
 
-def first_kernel(needs, y1, op, lf, ltc, x2, tu, marks_ref, gh):
+def first_kernel(needs, y1, op, lf, ltc, f, c, w, x2, tu, marks_ref, gh):
     n, rows, bw = y1.shape
     ci, own = lf.shape
     nb = own // bw
     q = x2.shape[0] // n
     for o in range(n):
         at = jnp.maximum(needs[0, o], 0) * ci
-        gh[:, o * bw : (o + 1) * bw] = y1[o, pl.ds(pl.multiple_of(at, ci), ci), :]
+        gh[:, o * bw : (o + 1) * bw] = y1[member(o, n), pl.ds(pl.multiple_of(at, ci), ci), :]
     t1 = (lf[...] + nt(gh[...], op[:, own:])).astype(BF)
-    marks = [y1[o, (nb + 1) * ci :, :].astype(F32) for o in range(n)]
-    for o in range(n):
-        marks_ref[o] = y1[o, (nb + 1) * ci :, :]
+    marks = []
+    for o in range(n):
+        mark = y1[member(o, n), (nb + 1) * ci :, :].astype(F32)
+        marks.append(jnp.concatenate([mark] * (ci // 8), axis=0))
+        marks_ref[o] = marks[o].astype(BF)
     u1 = []
     for b in range(nb):
         u = ltc[:, b * bw : (b + 1) * bw]
         for o in range(n):
-            u = u + jnp.where(marks[o] == b, y1[o, nb * ci : (nb + 1) * ci, :].astype(F32), 0.0)
+            u = u + jnp.where(marks[o] == b, y1[member(o, n), nb * ci : (nb + 1) * ci, :].astype(F32), 0.0)
         u1.append(u.astype(BF))
+    for b in range(nb):
+        tu[ci : 2 * ci, b * bw : (b + 1) * bw] = u1[b]
+    sent = nn(tu[ci : 2 * ci], op[:, own:]).astype(BF)
     tu[0:ci] = t1
-    for b in range(nb):
-        tu[ci:, b * bw : (b + 1) * bw] = u1[b]
-    sent = nn(tu[ci:], op[:, own:]).astype(BF)
+    tu[2 * ci : 3 * ci] = f[...]
+    tu[3 * ci : 4 * ci] = c[...]
+    co = w.shape[2]
+    for k in range(K):
+        tu[4 * ci :, k * co : (k + 1) * co] = w[k]
     tf = t1.astype(F32)
     for o in range(n):
         blk = jnp.zeros((ci, bw), F32)
@@ -128,30 +143,27 @@
 
 
 def gather_kernel(q, refs):
-    packs = refs[:q]
-    tus = refs[q : 2 * q]
-    op, tpre, upre, full, wt, wg, wbuf = refs[2 * q :]
+    tus, op, tpre, upre, full, wt, wg, wbuf = refs
     own = tpre.shape[1]
     total = tpre.shape[0]
     ci = total // q
     co = wt.shape[1]
     me = lax.axis_index("ch")
     for s in range(q):
-        at = lax.rem(me - s + q, q) * ci
-        spot = pl.ds(pl.multiple_of(at, ci), ci)
-        full[0, spot, :] = packs[s][0:ci, :]
-        full[1, spot, :] = packs[s][ci : 2 * ci, :]
+        spot = slice(s * ci, (s + 1) * ci)
+        full[0, spot, :] = tus[s][2 * ci : 3 * ci, :]
+        full[1, spot, :] = tus[s][3 * ci : 4 * ci, :]
         full[2, spot, :] = tus[s][0:ci, :]
-        full[3, spot, :] = tus[s][ci:, :]
-        wbuf[spot, :] = packs[s][2 * ci :, : K * co].astype(F32)
+        full[3, spot, :] = tus[s][ci : 2 * ci, :]
+        wbuf[spot, :] = tus[s][4 * ci :, : K * co].astype(F32)
     for k in range(K):
         turned = wbuf[:, k * co : (k + 1) * co].T
         wt[k] = turned.astype(BF)
     local = op[:, :own]
     tpre[...] = 2.0 * nt(full[2], local) - full[0].astype(F32)
     upre[...] = 2.0 * nn(full[3], local) - full[1].astype(F32)
-    wg[0] = nt(packs[0][0:ci, :], full[1])
-    wg[1] = nt(tus[0][0:ci, :], full[1])
+    wg[0] = nt(tus[me, 2 * ci : 3 * ci, :], full[1])
+    wg[1] = nt(tus[me, 0:ci, :], full[1])
 
 
 def second_kernel(q, y2, marks_ref, op, tpre, upre, full, wt, wg, w, x3, two, gh2, gh, low):
@@ -191,9 +203,9 @@
         blk = jnp.zeros((ci, bw), F32)
         for b in range(nb):
             blk = jnp.where(marks[o] == b, gf[:, b * bw : (b + 1) * bw], blk)
-        x3[o, 0:ci, :] = blk.astype(BF)
-        x3[o, ci : 2 * ci, :] = sent[:, o * bw : (o + 1) * bw]
-        x3[o, 2 * ci :, :] = packed
+        x3[member(o, n), 0:ci, :] = blk.astype(BF)
+        x3[member(o, n), ci : 2 * ci, :] = sent[:, o * bw : (o + 1) * bw]
+        x3[member(o, n), 2 * ci :, :] = packed
 
 
 def local_kernel(op, full, two, gh2, wt, w, outl, fgl):
@@ -213,17 +225,17 @@
     nb = own // bw
     co = wgrad.shape[2]
     for o in range(n):
-        gh[:, o * bw : (o + 1) * bw] = y3[o, 0:ci, :]
+        gh[:, o * bw : (o + 1) * bw] = y3[member(o, n), 0:ci, :]
     out[...] = (outl[...] + 2.0 * nt(gh[...], op[:, own:])).astype(BF)
     for b in range(nb):
         u = jnp.zeros((ci, bw), F32)
         for o in range(n):
-            u = u + jnp.where(marks_ref[o].astype(F32) == b, y3[o, ci : 2 * ci, :].astype(F32), 0.0)
+            u = u + jnp.where(marks_ref[o].astype(F32) == b, y3[member(o, n), ci : 2 * ci, :].astype(F32), 0.0)
         spot = slice(b * bw, (b + 1) * bw)
         fg[:, spot] = (fgl[:, spot] + 2.0 * u).astype(BF)
-    wsum = y3[0, 2 * ci :, :].astype(F32)
+    wsum = y3[member(0, n), 2 * ci :, :].astype(F32)
     for o in range(1, n):
-        wsum = wsum + y3[o, 2 * ci :, :].astype(F32)
+        wsum = wsum + y3[member(o, n), 2 * ci :, :].astype(F32)
     wgrad[0] = wsum[0:ci, 0:co]
     wgrad[1] = wsum[0:ci, co:]
     wgrad[2] = wsum[ci:, 0:co]
@@ -248,11 +260,11 @@
     packed = pltpu.CompilerParams(vmem_limit_bytes=62 << 20)
 
     needs = needs.reshape(1, n)
-    x1, pack = pl.pallas_call(
+    x1 = pl.pallas_call(
         push_kernel,
-        out_shape=(struct((n, (nb + 2) * ci, bw), BF), struct((3 * ci, own), BF)),
-        in_specs=[hbm] * 6,
-        out_specs=(vmem, vmem),
+        out_shape=struct((n, (nb + 1) * ci + 8, bw), BF),
+        in_specs=[hbm] * 5,
+        out_specs=vmem,
         scratch_shapes=[
             pltpu.SMEM((nb, tpr), jnp.int32),
             pltpu.SMEM((1, n), jnp.int32),
@@ -260,15 +272,14 @@
             pltpu.SMEM((nb * tpr,), jnp.int32),
             pltpu.VMEM((ci, own), BF),
             pltpu.VMEM((ci, own), BF),
-            pltpu.VMEM((K, ci, co), BF),
             pltpu.VMEM((nb * tpr, bw, bw), BF),
             pltpu.VMEM((n, ci, bw), F32),
-            pltpu.SemaphoreType.DMA((5 + nb,)),
+            pltpu.SemaphoreType.DMA((4 + nb,)),
         ],
         compiler_params=packed,
         name="push",
-    )(tile_cols, needs, features, cotangent, weights, tiles)
-    y1 = lax.all_to_all(x1, "rows", 0, 0)
+    )(tile_cols, needs, features, cotangent, tiles)
+    y1 = row_exchange(x1, n)
 
     op, lf, ltc = pl.pallas_call(
         combine_kernel,
@@ -285,26 +296,17 @@
         name="combine",
     )(tile_cols, features, cotangent, tiles)
 
-    def around(value):
-        moved = [value]
-        for s in range(1, q):
-            moved.append(lax.ppermute(value, "ch", [(i, (i + s) % q) for i in range(q)]))
-        return moved
-
-    packs = around(pack)
-    y1, *packs = lax.optimization_barrier((y1, *packs))
-
     x2, tu, marks = pl.pallas_call(
         first_kernel,
-        out_shape=(struct((n * q, 2 * ci, bw), BF), struct((2 * ci, own), BF), struct((n, ci, bw), BF)),
-        in_specs=[smem, vmem, vmem, vmem, vmem],
+        out_shape=(struct((n * q, 2 * ci, bw), BF), struct((5 * ci, own), BF), struct((n, ci, bw), BF)),
+        in_specs=[smem] + [vmem] * 7,
         out_specs=(vmem,) * 3,
         scratch_shapes=[pltpu.VMEM((ci, n * bw), BF)],
         compiler_params=params,
         name="first",
-    )(needs, y1, op, lf, ltc)
+    )(needs, y1, op, lf, ltc, features, cotangent, weights)
     y2 = lax.all_to_all(x2, ("rows", "ch"), 0, 0)
-    tus = around(tu)
+    tus = lax.all_gather(tu, "ch", axis=0)
 
     tpre, upre, full, wt, wg = pl.pallas_call(
         lambda *refs: gather_kernel(q, refs),
@@ -315,13 +317,13 @@
             struct((K, co, total), BF),
             struct((2, ci, co), F32),
         ),
-        in_specs=[vmem] * (2 * q + 1),
+        in_specs=[vmem] * 2,
         out_specs=(vmem,) * 5,
         scratch_shapes=[pltpu.VMEM((total, K * co), F32)],
         compiler_params=params,
         cost_estimate=pl.CostEstimate(flops=4 * total * own * own, bytes_accessed=4 << 20, transcendentals=0),
         name="gather",
-    )(*packs, *tus, op)
+    )(tus, op)
 
     x3, two, gh2 = pl.pallas_call(
         functools.partial(second_kernel, q),
@@ -332,7 +334,7 @@
         compiler_params=params,
         name="second",
     )(y2, marks, op, tpre, upre, full, wt, wg, weights)
-    y3 = lax.all_to_all(x3, "rows", 0, 0)
+    y3 = row_exchange(x3, n)
 
     outl, fgl = pl.pallas_call(
         local_kernel,

time: 48 us -> 45.2 us (0.942)
  waiting for transfers between devices: 18 us -> 7.84 us
  blocking collectives: 0 us -> 8.05 us
  starting transfers between devices: 17.8 us -> 17.1 us
    all_gather x0 -> x1, blocking collectives: none -> 8.05 us  [body(): tus = lax.all_gather(tu, 'ch', axis=0)]
    ppermute x6 -> x0, waiting for transfers between devices: 4.96 us -> none  [around(): lax.ppermute(value, 'ch', [(i, (i + s) % q) for i in range(q)])]
    ppermute x6 -> x0, starting transfers between devices: 3.83 us -> none  [around(): lax.ppermute(value, 'ch', [(i, (i + s) % q) for i in range(q)])]
    all_to_all x2, waiting for transfers between devices: 9.34 us -> 5.69 us  [row_exchange(): return lax.all_to_all(value, 'rows', 0, 0, axis_index_groups=[order])]
    all_to_all x2, starting transfers between devices: 10.8 us -> 13.4 us  [row_exchange(): return lax.all_to_all(value, 'rows', 0, 0, axis_index_groups=[order])]
    all_to_all x1, waiting for transfers between devices: 3.69 us -> 2.15 us  [body(): y2 = lax.all_to_all(x2, ('rows', 'ch'), 0, 0)]
    all_to_all x1, starting transfers between devices: 3.19 us -> 3.71 us  [body(): y2 = lax.all_to_all(x2, ('rows', 'ch'), 0, 0)]
  transfers between devices with their start and end apart: 9 -> 3, of which waited for: 7 -> 3; matrix products, arithmetic and copies ran while one was open for 0% -> 0% of each run, Pallas kernels for 8% -> 9%
where the time goes in v3:
time: 45.2 us; the launch traced here: 44.7 us
  starting transfers between devices  17.1 us (38%)
  Pallas kernels  11 us (24%)
  blocking collectives  8.05 us (18%)
  waiting for transfers between devices  7.84 us (17%)
  between operations  0.71 us (2%)
    all_to_all x2, starting transfers between devices, row_exchange(): return lax.all_to_all(value, 'rows', 0, 0, axis_index_groups=[order])  13.4 us
    all_gather x1, blocking collectives, body(): tus = lax.all_gather(tu, 'ch', axis=0)  8.05 us
    all_to_all x2, waiting for transfers between devices, row_exchange(): return lax.all_to_all(value, 'rows', 0, 0, axis_index_groups=[order])  5.69 us
    all_to_all x1, starting transfers between devices, body(): y2 = lax.all_to_all(x2, ('rows', 'ch'), 0, 0)  3.71 us
    pallas_call x1, Pallas kernels, body(): pl.pallas_call(combine_kernel, out_shape=(struct((own, wide), BF), struct...  3.18 us
    pallas_call x1, Pallas kernels, body(): pl.pallas_call(push_kernel, out_shape=struct((n, (nb + 1) * ci + 8, bw),...  2.69 us
    all_to_all x1, waiting for transfers between devices, body(): y2 = lax.all_to_all(x2, ('rows', 'ch'), 0, 0)  2.15 us
    pallas_call x1, Pallas kernels, body(): pl.pallas_call(first_kernel, out_shape=(struct((n * q, 2 * ci, bw), BF),...  1.77 us
  transfers between devices with their start and end apart: 3, of which 3 were waited for; matrix products, arithmetic and copies ran while one was open for 0% of the time, Pallas kernels for 9%

profile of v3, /device:TPU:0, one launch (start us, length us, event | category | flops | bytes accessed | tf_op | source)
XLA Modules:
  0.0 44.7 jit_solution(3354213092920666332)
XLA Ops:
  0.6 0.0 copy-start.1
  0.6 0.0 copy-start
  0.7 0.0 copy-start.3
  0.7 0.0 copy-start.2
  0.7 0.0 copy-start.4
  0.7 2.7 %push.1 = bf16[8,88,128]{2,1,0:T(8,128)(2,1)} custom-call(s32[4,20]{1,0:T(4,128)} %cols.1, s32[1,8]{1,0:T(1,128)} %bitcast.3, bf16[16,512]{1,0:T(8,128)(2,1)} %f.3, bf16[16,512]{1,0:T(8,128)(2,1)} %c.3, bf16[4,20,128,128]{3,2,1,0:T(8,128)(2,1)} %tiles.3), custom_call_target="tpu_custom_call" | custom-call | tf_op jit(solution)/shard_map/push/pallas_call | solution.py:263
  3.4 8.3 %all-to-all-start = ((bf16[8,88,128]{2,1,0:T(8,128)(2,1)}), bf16[8,88,128]{2,1,0:T(8,128)(2,1)S(1)}, u32[]{:S(2)}, u32[]{:S(2)}) async-start(bf16[8,88,128]{2,1,0:T(8,128)(2,1)} %push.1), calls=%async_computation | async-start | bytes 360448 | tf_op jit(solution)/shard_map/all_to_all | solution.py:39
  11.7 0.0 copy-done.1
  11.7 0.0 copy-done
  11.7 0.0 copy-done.3
  11.7 3.2 %combine.1 = (bf16[512,1536]{1,0:T(8,128)(2,1)S(1)}, f32[16,512]{1,0:T(8,128)S(1)}, f32[16,512]{1,0:T(8,128)S(1)}) custom-call(s32[4,20]{1,0:T(4,128)S(1)} %copy-done.3, bf16[16,512]{1,0:T(8,128)(2,1)S(1)} %copy-done, bf16[16,512]{1,0:T(8,128)(2,1)S(1)} %copy-done.1, bf16[4,20,128,128]{3,2,1,0:T(8,128)(2,1)} %tiles.3), custom_call_target="tpu_custom_call" | custom-call | flops 16777216 | bytes 8388608 | tf_op jit(solution)/shard_map/combine/pallas_call | solution.py:284
  14.9 2.0 %all-to-all-done.y1 = bf16[8,88,128]{2,1,0:T(8,128)(2,1)S(1)} async-done(((bf16[8,88,128]{2,1,0:T(8,128)(2,1)}), bf16[8,88,128]{2,1,0:T(8,128)(2,1)S(1)}, u32[]{:S(2)}, u32[]{:S(2)}) %all-to-all-start) | async-done | bytes 180256 | tf_op jit(solution)/shard_map/all_to_all | solution.py:39
  16.9 0.0 copy-done.2
  16.9 0.0 copy-done.4
  16.9 1.8 %first.1 = (bf16[32,32,128]{2,1,0:T(8,128)(2,1)}, bf16[80,512]{1,0:T(8,128)(2,1)S(1)}, bf16[8,16,128]{2,1,0:T(8,128)(2,1)S(1)}) custom-call(s32[1,8]{1,0:T(1,128)S(1)} %bitcast.4, bf16[8,88,128]{2,1,0:T(8,128)(2,1)S(1)} %all-to-all-done.y1, bf16[512,1536]{1,0:T(8,128)(2,1)S(1)} %get-tuple-element.19.op.refs_1_, f32[16,512]{1,0:T(8,128)S(1)} %get-tuple-element.20.lf, ...), custom_call_target="tpu_custom_call" | custom-call | tf_op jit(solution)/shard_map/first/pallas_call | solution.py:299
  18.6 3.7 %all-to-all-start.1 = ((bf16[32,32,128]{2,1,0:T(8,128)(2,1)}), bf16[32,32,128]{2,1,0:T(8,128)(2,1)S(1)}, u32[]{:S(2)}, u32[]{:S(2)}) async-start(bf16[32,32,128]{2,1,0:T(8,128)(2,1)} %get-tuple-element.22), calls=%async_computation.1 | async-start | bytes 524288 | tf_op jit(solution)/shard_map/all_to_all | solution.py:308
  22.3 8.0 %all-gather = bf16[320,512]{1,0:T(8,128)(2,1)S(1)} all-gather(bf16[80,512]{1,0:T(8,128)(2,1)S(1)} %get-tuple-element.24), channel_id=2, replica_groups=mesh['rows'=8,'ch'=4] {'ch'}, dimensions={0}, use_global_device_ids=true | all-gather | bytes 409600 | tf_op jit(solution)/shard_map/all_gather | solution.py:309
  30.4 0.4 gather.1
  30.8 2.2 %all-to-all-done.1.y2 = bf16[32,32,128]{2,1,0:T(8,128)(2,1)S(1)} async-done(((bf16[32,32,128]{2,1,0:T(8,128)(2,1)}), bf16[32,32,128]{2,1,0:T(8,128)(2,1)S(1)}, u32[]{:S(2)}, u32[]{:S(2)}) %all-to-all-start.1) | async-done | bytes 262176 | tf_op jit(solution)/shard_map/all_to_all | solution.py:308
  32.9 1.6 %second.1 = (bf16[8,64,128]{2,1,0:T(8,128)(2,1)}, bf16[2,64,512]{2,1,0:T(8,128)(2,1)S(1)}, bf16[2,16,512]{2,1,0:T(8,128)(2,1)S(1)}) custom-call(bf16[32,32,128]{2,1,0:T(8,128)(2,1)S(1)} %all-to-all-done.1.y2, bf16[8,16,128]{2,1,0:T(8,128)(2,1)S(1)} %get-tuple-element.23.marks_ref, bf16[512,1536]{1,0:T(8,128)(2,1)S(1)} %get-tuple-element.19.op.refs_1_, ...), custom_call_target="tpu_custom_call" | custom-call | tf_op jit(solution)/shard_map/second/pallas_call | solution.py:328
  34.5 5.1 %all-to-all-start.2 = ((bf16[8,64,128]{2,1,0:T(8,128)(2,1)}), bf16[8,64,128]{2,1,0:T(8,128)(2,1)S(1)}, u32[]{:S(2)}, u32[]{:S(2)}) async-start(bf16[8,64,128]{2,1,0:T(8,128)(2,1)} %get-tuple-element.30), calls=%async_computation.2 | async-start | bytes 262144 | tf_op jit(solution)/shard_map/all_to_all | solution.py:39
  39.6 0.4 local.1
  40.0 3.7 %all-to-all-done.2.y3 = bf16[8,64,128]{2,1,0:T(8,128)(2,1)S(1)} async-done(((bf16[8,64,128]{2,1,0:T(8,128)(2,1)}), bf16[8,64,128]{2,1,0:T(8,128)(2,1)S(1)}, u32[]{:S(2)}, u32[]{:S(2)}) %all-to-all-start.2) | async-done | bytes 131104 | tf_op jit(solution)/shard_map/all_to_all | solution.py:39
  43.7 1.0 %last.1 = (bf16[16,512]{1,0:T(8,128)(2,1)}, bf16[16,512]{1,0:T(8,128)(2,1)}, f32[4,16,64]{2,1,0:T(8,128)}) custom-call(bf16[8,64,128]{2,1,0:T(8,128)(2,1)S(1)} %all-to-all-done.2.y3, bf16[8,16,128]{2,1,0:T(8,128)(2,1)S(1)} %get-tuple-element.23.marks_ref, bf16[512,1536]{1,0:T(8,128)(2,1)S(1)} %get-tuple-element.19.op.refs_1_, ...), custom_call_target="tpu_custom_call" | custom-call | tf_op jit(solution)/shard_map/last/pallas_call | solution.py:349
Async XLA Ops:
  0.6 11.0 %copy-start.1 = (bf16[16,512]{1,0:T(8,128)(2,1)S(1)}, bf16[16,512]{1,0:T(8,128)(2,1)}, u32[]{:S(2)}) copy-start(bf16[16,512]{1,0:T(8,128)(2,1)} %c.3) | copy-start | bytes 49156
  0.6 11.0 %copy-start = (bf16[16,512]{1,0:T(8,128)(2,1)S(1)}, bf16[16,512]{1,0:T(8,128)(2,1)}, u32[]{:S(2)}) copy-start(bf16[16,512]{1,0:T(8,128)(2,1)} %f.3) | copy-start | bytes 49156
  0.7 11.0 %copy-start.3 = (s32[4,20]{1,0:T(4,128)S(1)}, s32[4,20]{1,0:T(4,128)}, u32[]{:S(2)}) copy-start(s32[4,20]{1,0:T(4,128)} %cols.1) | copy-start | bytes 964
  0.7 16.2 %copy-start.2 = (bf16[4,16,64]{2,1,0:T(8,128)(2,1)S(1)}, bf16[4,16,64]{2,1,0:T(8,128)(2,1)}, u32[]{:S(2)}) copy-start(bf16[4,16,64]{2,1,0:T(8,128)(2,1)} %w.5) | copy-start | bytes 24580
  0.7 16.2 %copy-start.4 = (s32[1,8,1]{1,2,0:T(1,128)S(1)}, s32[1,8,1]{1,2,0:T(1,128)}, u32[]{:S(2)}) copy-start(s32[1,8,1]{1,2,0:T(1,128)} %param.9) | copy-start | bytes 100
  3.4 13.5 %all-to-all-start = ((bf16[8,88,128]{2,1,0:T(8,128)(2,1)}), bf16[8,88,128]{2,1,0:T(8,128)(2,1)S(1)}, u32[]{:S(2)}, u32[]{:S(2)}) async-start(bf16[8,88,128]{2,1,0:T(8,128)(2,1)} %push.1), calls=%async_computation | async-start | bytes 360448 | tf_op jit(solution)/shard_map/all_to_all | solution.py:39
  18.6 14.3 %all-to-all-start.1 = ((bf16[32,32,128]{2,1,0:T(8,128)(2,1)}), bf16[32,32,128]{2,1,0:T(8,128)(2,1)S(1)}, u32[]{:S(2)}, u32[]{:S(2)}) async-start(bf16[32,32,128]{2,1,0:T(8,128)(2,1)} %get-tuple-element.22), calls=%async_computation.1 | async-start | bytes 524288 | tf_op jit(solution)/shard_map/all_to_all | solution.py:308
  34.5 9.2 %all-to-all-start.2 = ((bf16[8,64,128]{2,1,0:T(8,128)(2,1)}), bf16[8,64,128]{2,1,0:T(8,128)(2,1)S(1)}, u32[]{:S(2)}, u32[]{:S(2)}) async-start(bf16[8,64,128]{2,1,0:T(8,128)(2,1)} %get-tuple-element.30), calls=%async_computation.2 | async-start | bytes 262144 | tf_op jit(solution)/shard_map/all_to_all | solution.py:39

commit v4 on v3

--- a/solution.py
+++ b/solution.py
@@ -39,10 +39,28 @@
     return lax.all_to_all(value, "rows", 0, 0, axis_index_groups=[order])
 
 
-def push_kernel(cols_h, needs_h, f_h, c_h, tiles, x1, cols, needs, cells, where, f, c, buf, acc, sems):
+def spread(device, pair, n, half):
+    return (device * half + pair - turn(n) * half) % (n * half)
+
+
+def spread_exchange(value, n, q):
+    half = q // 2
+    groups = []
+    for parity in range(2):
+        members = [row * q + 2 * pair + parity for row in range(n) for pair in range(half)]
+        start = turn(n) * half
+        groups.append(members[start:] + members[:start])
+    return lax.all_to_all(value, ("rows", "ch"), 0, 0, axis_index_groups=groups)
+
+
+def swap(value, q, bit):
+    return lax.ppermute(value, "ch", [(i, i ^ bit) for i in range(q)])
+
+
+def push_kernel(cols_h, needs_h, f_h, c_h, w_h, tiles, x1, pack, cols, needs, cells, where, f, c, w, buf, acc, sems):
     nb, tpr = cols.shape
     n, ci, bw = acc.shape
-    small = [(cols_h, cols), (needs_h, needs), (f_h, f), (c_h, c)]
+    small = [(cols_h, cols), (needs_h, needs), (f_h, f), (c_h, c), (w_h, w)]
     copies = [pltpu.make_async_copy(src, dst, sems.at[i]) for i, (src, dst) in enumerate(small)]
     for r in range(nb):
         copies.append(pltpu.make_async_copy(tiles.at[r], buf.at[pl.ds(r * tpr, tpr)], sems.at[len(small) + r]))
@@ -58,13 +76,18 @@
             cells[count] = v - nb
             where[count] = r * tpr + t
             count = count + (v >= nb).astype(jnp.int32)
-    for copy in copies[1:4]:
+    for copy in copies[1:5]:
         copy.wait()
     for o in range(n):
         for b in range(nb):
             x1[member(o, n), b * ci : (b + 1) * ci, :] = f[:, b * bw : (b + 1) * bw]
         x1[member(o, n), (nb + 1) * ci :, :] = jnp.full((8, bw), needs[0, o].astype(F32)).astype(BF)
-    for copy in copies[4:]:
+    pack[0:ci] = f[...]
+    pack[ci : 2 * ci] = c[...]
+    for k in range(K):
+        width = w.shape[2]
+        pack[2 * ci :, k * width : (k + 1) * width] = w[k]
+    for copy in copies[5:]:
         copy.wait()
 
     def products(step, carry):
@@ -102,11 +125,11 @@
     ltc[...] = nn(c[...], local)
 
 
-def first_kernel(needs, y1, op, lf, ltc, f, c, w, x2, tu, marks_ref, gh):
+def first_kernel(needs, y1, op, lf, ltc, x2, tu, marks_ref, gh):
     n, rows, bw = y1.shape
     ci, own = lf.shape
     nb = own // bw
-    q = x2.shape[0] // n
+    half = x2.shape[0] // n
     for o in range(n):
         at = jnp.maximum(needs[0, o], 0) * ci
         gh[:, o * bw : (o + 1) * bw] = y1[member(o, n), pl.ds(pl.multiple_of(at, ci), ci), :]
@@ -126,64 +149,70 @@
         tu[ci : 2 * ci, b * bw : (b + 1) * bw] = u1[b]
     sent = nn(tu[ci : 2 * ci], op[:, own:]).astype(BF)
     tu[0:ci] = t1
-    tu[2 * ci : 3 * ci] = f[...]
-    tu[3 * ci : 4 * ci] = c[...]
-    co = w.shape[2]
-    for k in range(K):
-        tu[4 * ci :, k * co : (k + 1) * co] = w[k]
     tf = t1.astype(F32)
     for o in range(n):
         blk = jnp.zeros((ci, bw), F32)
         for b in range(nb):
             blk = jnp.where(marks[o] == b, tf[:, b * bw : (b + 1) * bw], blk)
         blk = blk.astype(BF)
-        for s in range(q):
-            x2[o * q + s, 0:ci, :] = blk
-            x2[o * q + s, ci:, :] = sent[:, o * bw : (o + 1) * bw]
+        for s in range(half):
+            x2[spread(o, s, n, half), 0:ci, :] = blk
+            x2[spread(o, s, n, half), ci:, :] = sent[:, o * bw : (o + 1) * bw]
 
 
 def gather_kernel(q, refs):
-    tus, op, tpre, upre, full, wt, wg, wbuf = refs
+    packs = refs[:q]
+    tus = refs[q : 2 * q]
+    op, w, tpre, upre, full, wt, wg, outl, fgl, wbuf = refs[2 * q :]
     own = tpre.shape[1]
     total = tpre.shape[0]
     ci = total // q
     co = wt.shape[1]
     me = lax.axis_index("ch")
     for s in range(q):
-        spot = slice(s * ci, (s + 1) * ci)
-        full[0, spot, :] = tus[s][2 * ci : 3 * ci, :]
-        full[1, spot, :] = tus[s][3 * ci : 4 * ci, :]
+        spot = pl.ds(pl.multiple_of((me ^ s) * ci, ci), ci)
+        full[0, spot, :] = packs[s][0:ci, :]
+        full[1, spot, :] = packs[s][ci : 2 * ci, :]
         full[2, spot, :] = tus[s][0:ci, :]
         full[3, spot, :] = tus[s][ci : 2 * ci, :]
-        wbuf[spot, :] = tus[s][4 * ci :, : K * co].astype(F32)
+        wbuf[spot, :] = packs[s][2 * ci :, : K * co].astype(F32)
     for k in range(K):
         turned = wbuf[:, k * co : (k + 1) * co].T
         wt[k] = turned.astype(BF)
+    mine = pl.ds(pl.multiple_of(me * ci, ci), ci)
+    outl[...] = nn(wt[0, mine, :], full[0]) + nn(wt[1, mine, :], full[2]) - nn(wt[3, mine, :], full[2])
+    fgl[...] = nn(w[0], full[1]) + nn(w[1], full[3]) - nn(w[3], full[3])
     local = op[:, :own]
     tpre[...] = 2.0 * nt(full[2], local) - full[0].astype(F32)
     upre[...] = 2.0 * nn(full[3], local) - full[1].astype(F32)
-    wg[0] = nt(tus[me, 2 * ci : 3 * ci, :], full[1])
-    wg[1] = nt(tus[me, 0:ci, :], full[1])
-
-
-def second_kernel(q, y2, marks_ref, op, tpre, upre, full, wt, wg, w, x3, two, gh2, gh, low):
+    wg[0] = nt(packs[0][0:ci, :], full[1])
+    wg[1] = nt(tus[0][0:ci, :], full[1])
+
+
+def second_kernel(q, y2, z2, marks_ref, op, tpre, upre, full, wt, wg, w, x3, two, gh2, gh, low):
     n, ci, bw = marks_ref.shape
     total, own = tpre.shape
     nb = own // bw
     me = lax.axis_index("ch")
     mine = pl.ds(pl.multiple_of(me * ci, ci), ci)
-    for o in range(n):
-        for s in range(q):
-            gh[s * ci : (s + 1) * ci, o * bw : (o + 1) * bw] = y2[o * q + s, 0:ci, :]
+    half = q // 2
+    sources = []
+    for s in range(half):
+        own_at = 2 * s + me % 2
+        sources.append((s, y2, pl.ds(pl.multiple_of(own_at * ci, ci), ci)))
+        sources.append((s, z2, pl.ds(pl.multiple_of((own_at ^ 1) * ci, ci), ci)))
+    for o in range(n):
+        for s, came, spot in sources:
+            gh[spot, o * bw : (o + 1) * bw] = came[spread(o, s, n, half), 0:ci, :]
     two[0] = (tpre[...] + 2.0 * nt(gh[...], op[:, own:])).astype(BF)
     marks = [marks_ref[o].astype(F32) for o in range(n)]
-    for s in range(q):
+    for s, came, spot in sources:
         for b in range(nb):
             u = jnp.zeros((ci, bw), F32)
             for o in range(n):
-                u = u + jnp.where(marks[o] == b, y2[o * q + s, ci:, :].astype(F32), 0.0)
-            spot = (slice(s * ci, (s + 1) * ci), slice(b * bw, (b + 1) * bw))
-            two[(1,) + spot] = (upre[spot] + 2.0 * u).astype(BF)
+                u = u + jnp.where(marks[o] == b, came[spread(o, s, n, half), ci:, :].astype(F32), 0.0)
+            at = (spot, slice(b * bw, (b + 1) * bw))
+            two[(1,) + at] = (upre[at] + 2.0 * u).astype(BF)
     g = nn(wt[K - 1, mine, :], two[0]).astype(BF)
     h = nn(w[K - 1], two[1]).astype(BF)
     gh2[0] = g
@@ -208,31 +237,25 @@
         x3[member(o, n), 2 * ci :, :] = packed
 
 
-def local_kernel(op, full, two, gh2, wt, w, outl, fgl):
-    ci, own = outl.shape
-    me = lax.axis_index("ch")
-    mine = pl.ds(pl.multiple_of(me * ci, ci), ci)
-    local = op[:, :own]
-    out = nn(wt[0, mine, :], full[0]) + nn(wt[1, mine, :], full[2]) - nn(wt[3, mine, :], full[2])
-    outl[...] = out + nn(wt[2, mine, :], two[0]) + 2.0 * nt(gh2[0], local)
-    fg = nn(w[0], full[1]) + nn(w[1], full[3]) - nn(w[3], full[3])
-    fgl[...] = fg + nn(w[2], two[1]) + 2.0 * nn(gh2[1], local)
-
-
-def last_kernel(y3, marks_ref, op, outl, fgl, out, fg, wgrad, gh):
+def last_kernel(y3, marks_ref, op, outl, fgl, two, gh2, wt, w, out, fg, wgrad, gh):
     n, ci, bw = marks_ref.shape
     own = outl.shape[1]
     nb = own // bw
     co = wgrad.shape[2]
-    for o in range(n):
-        gh[:, o * bw : (o + 1) * bw] = y3[member(o, n), 0:ci, :]
-    out[...] = (outl[...] + 2.0 * nt(gh[...], op[:, own:])).astype(BF)
+    me = lax.axis_index("ch")
+    mine = pl.ds(pl.multiple_of(me * ci, ci), ci)
+    gh[:, :own] = gh2[0]
+    for o in range(n):
+        gh[:, own + o * bw : own + (o + 1) * bw] = y3[member(o, n), 0:ci, :]
+    out[...] = (outl[...] + nn(wt[2, mine, :], two[0]) + 2.0 * nt(gh[...], op[...])).astype(BF)
+    back = nn(gh2[1], op[:, :own])
+    base = fgl[...] + nn(w[2], two[1])
     for b in range(nb):
-        u = jnp.zeros((ci, bw), F32)
+        spot = slice(b * bw, (b + 1) * bw)
+        u = back[:, spot]
         for o in range(n):
             u = u + jnp.where(marks_ref[o].astype(F32) == b, y3[member(o, n), ci : 2 * ci, :].astype(F32), 0.0)
-        spot = slice(b * bw, (b + 1) * bw)
-        fg[:, spot] = (fgl[:, spot] + 2.0 * u).astype(BF)
+        fg[:, spot] = (base[:, spot] + 2.0 * u).astype(BF)
     wsum = y3[member(0, n), 2 * ci :, :].astype(F32)
     for o in range(1, n):
         wsum = wsum + y3[member(o, n), 2 * ci :, :].astype(F32)
@@ -260,11 +283,11 @@
     packed = pltpu.CompilerParams(vmem_limit_bytes=62 << 20)
 
     needs = needs.reshape(1, n)
-    x1 = pl.pallas_call(
+    x1, pack = pl.pallas_call(
         push_kernel,
-        out_shape=struct((n, (nb + 1) * ci + 8, bw), BF),
-        in_specs=[hbm] * 5,
-        out_specs=vmem,
+        out_shape=(struct((n, (nb + 1) * ci + 8, bw), BF), struct((3 * ci, own), BF)),
+        in_specs=[hbm] * 6,
+        out_specs=(vmem, vmem),
         scratch_shapes=[
             pltpu.SMEM((nb, tpr), jnp.int32),
             pltpu.SMEM((1, n), jnp.int32),
@@ -272,13 +295,14 @@
             pltpu.SMEM((nb * tpr,), jnp.int32),
             pltpu.VMEM((ci, own), BF),
             pltpu.VMEM((ci, own), BF),
+            pltpu.VMEM((K, ci, co), BF),
             pltpu.VMEM((nb * tpr, bw, bw), BF),
             pltpu.VMEM((n, ci, bw), F32),
-            pltpu.SemaphoreType.DMA((4 + nb,)),
+            pltpu.SemaphoreType.DMA((5 + nb,)),
         ],
         compiler_params=packed,
         name="push",
-    )(tile_cols, needs, features, cotangent, tiles)
+    )(tile_cols, needs, features, cotangent, weights, tiles)
     y1 = row_exchange(x1, n)
 
     op, lf, ltc = pl.pallas_call(
@@ -296,19 +320,25 @@
         name="combine",
     )(tile_cols, features, cotangent, tiles)
 
+    packs = [pack, swap(pack, q, 1), swap(pack, q, 2), swap(pack, q, 3)]
+    y1, *packs[1:] = lax.optimization_barrier((y1, *packs[1:]))
+
     x2, tu, marks = pl.pallas_call(
         first_kernel,
-        out_shape=(struct((n * q, 2 * ci, bw), BF), struct((5 * ci, own), BF), struct((n, ci, bw), BF)),
-        in_specs=[smem] + [vmem] * 7,
+        out_shape=(struct((n * (q // 2), 2 * ci, bw), BF), struct((2 * ci, own), BF), struct((n, ci, bw), BF)),
+        in_specs=[smem] + [vmem] * 4,
         out_specs=(vmem,) * 3,
         scratch_shapes=[pltpu.VMEM((ci, n * bw), BF)],
         compiler_params=params,
         name="first",
-    )(needs, y1, op, lf, ltc, features, cotangent, weights)
-    y2 = lax.all_to_all(x2, ("rows", "ch"), 0, 0)
-    tus = lax.all_gather(tu, "ch", axis=0)
-
-    tpre, upre, full, wt, wg = pl.pallas_call(
+    )(needs, y1, op, lf, ltc)
+    y2 = spread_exchange(x2, n, q)
+    tus = [tu, swap(tu, q, 1), swap(tu, q, 2)]
+    tus.append(swap(tu, q, 3))
+    y2, *tus[1:] = lax.optimization_barrier((y2, *tus[1:]))
+    z2 = swap(y2, q, 1)
+
+    tpre, upre, full, wt, wg, outl, fgl = pl.pallas_call(
         lambda *refs: gather_kernel(q, refs),
         out_shape=(
             struct((total, own), F32),
@@ -316,45 +346,37 @@
             struct((4, total, own), BF),
             struct((K, co, total), BF),
             struct((2, ci, co), F32),
+            struct((ci, own), F32),
+            struct((ci, own), F32),
         ),
-        in_specs=[vmem] * 2,
-        out_specs=(vmem,) * 5,
+        in_specs=[vmem] * (2 * q + 2),
+        out_specs=(vmem,) * 7,
         scratch_shapes=[pltpu.VMEM((total, K * co), F32)],
         compiler_params=params,
         cost_estimate=pl.CostEstimate(flops=4 * total * own * own, bytes_accessed=4 << 20, transcendentals=0),
         name="gather",
-    )(tus, op)
+    )(*packs, *tus, op, weights)
 
     x3, two, gh2 = pl.pallas_call(
         functools.partial(second_kernel, q),
         out_shape=(struct((n, 4 * ci, bw), BF), struct((2, total, own), BF), struct((2, ci, own), BF)),
-        in_specs=[vmem] * 9,
+        in_specs=[vmem] * 10,
         out_specs=(vmem,) * 3,
         scratch_shapes=[pltpu.VMEM((total, n * bw), BF), pltpu.VMEM((2 * ci, bw), F32)],
         compiler_params=params,
         name="second",
-    )(y2, marks, op, tpre, upre, full, wt, wg, weights)
+    )(y2, z2, marks, op, tpre, upre, full, wt, wg, weights)
     y3 = row_exchange(x3, n)
-
-    outl, fgl = pl.pallas_call(
-        local_kernel,
-        out_shape=(struct((ci, own), F32), struct((ci, own), F32)),
-        in_specs=[vmem] * 6,
-        out_specs=(vmem,) * 2,
-        compiler_params=params,
-        cost_estimate=pl.CostEstimate(flops=8 * total * ci * own, bytes_accessed=4 << 20, transcendentals=0),
-        name="local",
-    )(op, full, two, gh2, wt, weights)
 
     output, feature_grad, weight_grad = pl.pallas_call(
         last_kernel,
         out_shape=(struct((ci, own), BF), struct((ci, own), BF), struct((K, ci, co), F32)),
-        in_specs=[vmem] * 5,
+        in_specs=[vmem] * 9,
         out_specs=(vmem,) * 3,
-        scratch_shapes=[pltpu.VMEM((ci, n * bw), BF)],
+        scratch_shapes=[pltpu.VMEM((ci, wide), BF)],
         compiler_params=params,
         name="last",
-    )(y3, marks, op, outl, fgl)
+    )(y3, marks, op, outl, fgl, two, gh2, wt, weights)
     return output, feature_grad, weight_grad
 
 

time: 45.2 us -> 43.3 us (0.958)
  waiting for transfers between devices: 7.84 us -> 4.39 us
  blocking collectives: 8.05 us -> 9.34 us
  starting transfers between devices: 17.1 us -> 18.1 us
  Pallas kernels: 11 us -> 10.4 us
    all_to_all x0 -> x1, blocking collectives: none -> 9.34 us  [row_exchange(): return lax.all_to_all(value, 'rows', 0, 0, axis_index_groups=[order])]
    all_gather x1 -> x0, blocking collectives: 8.05 us -> none  [body(): tus = lax.all_gather(tu, 'ch', axis=0)]
    all_to_all x2 -> x1, waiting for transfers between devices: 5.69 us -> 0.01 us  [row_exchange(): return lax.all_to_all(value, 'rows', 0, 0, axis_index_groups=[order])]
    all_to_all x2 -> x1, starting transfers between devices: 13.4 us -> 8.41 us  [row_exchange(): return lax.all_to_all(value, 'rows', 0, 0, axis_index_groups=[order])]
    ppermute x0 -> x7, waiting for transfers between devices: none -> 4.38 us  [swap(): return lax.ppermute(value, 'ch', [(i, i ^ bit) for i in range(q)])]
    ppermute x0 -> x7, starting transfers between devices: none -> 3.83 us  [swap(): return lax.ppermute(value, 'ch', [(i, i ^ bit) for i in range(q)])]
    all_to_all x1, waiting for transfers between devices: 2.15 us -> 0.01 us  [spread_exchange(): return lax.all_to_all(value, ('rows', 'ch'), 0, 0, axis_index_groups=groups)]
    all_to_all x1, starting transfers between devices: 3.71 us -> 5.81 us  [spread_exchange(): return lax.all_to_all(value, ('rows', 'ch'), 0, 0, axis_index_groups=groups)]
  transfers between devices with their start and end apart: 3 -> 9, of which waited for: 3 -> 4; matrix products, arithmetic and copies ran while one was open for 0% -> 0% of each run, Pallas kernels for 9% -> 9%
where the time goes in v4:
time: 43.3 us; the launch traced here: 42.9 us
  starting transfers between devices  18.1 us (42%)
  Pallas kernels  10.4 us (24%)
  blocking collectives  9.34 us (22%)
  waiting for transfers between devices  4.39 us (10%)
  between operations  0.73 us (2%)
    all_to_all x1, blocking collectives, row_exchange(): return lax.all_to_all(value, 'rows', 0, 0, axis_index_groups=[order])  9.34 us
    all_to_all x1, starting transfers between devices, row_exchange(): return lax.all_to_all(value, 'rows', 0, 0, axis_index_groups=[order])  8.41 us
    all_to_all x1, starting transfers between devices, spread_exchange(): return lax.all_to_all(value, ('rows', 'ch'), 0, 0, axis_index_groups=groups)  5.81 us
    ppermute x7, waiting for transfers between devices, swap(): return lax.ppermute(value, 'ch', [(i, i ^ bit) for i in range(q)])  4.38 us
    ppermute x7, starting transfers between devices, swap(): return lax.ppermute(value, 'ch', [(i, i ^ bit) for i in range(q)])  3.83 us
    pallas_call x1, Pallas kernels, body(): pl.pallas_call(combine_kernel, out_shape=(struct((own, wide), BF), struct...  3.18 us
    pallas_call x1, Pallas kernels, body(): pl.pallas_call(push_kernel, out_shape=(struct((n, (nb + 1) * ci + 8, bw),...  2.7 us
    pallas_call x1, Pallas kernels, body(): pl.pallas_call(first_kernel, out_shape=(struct((n * (q // 2), 2 * ci, bw)...  1.71 us
  transfers between devices with their start and end apart: 9, of which 4 were waited for; matrix products, arithmetic and copies ran while one was open for 0% of the time, Pallas kernels for 9%

profile of v4, /device:TPU:0, one launch (start us, length us, event | category | flops | bytes accessed | tf_op | source)
XLA Modules:
  0.0 42.9 jit_solution(2124396248663604523)
XLA Ops:
  0.6 0.0 copy-start.2
  0.6 0.0 copy-start.1
  0.7 0.0 copy-start.4
  0.7 0.0 copy-start.5
  0.7 2.7 %push.1 = (bf16[8,88,128]{2,1,0:T(8,128)(2,1)}, bf16[48,512]{1,0:T(8,128)(2,1)}) custom-call(s32[4,20]{1,0:T(4,128)} %cols.1, s32[1,8]{1,0:T(1,128)} %bitcast.1, bf16[16,512]{1,0:T(8,128)(2,1)} %f.1, bf16[16,512]{1,0:T(8,128)(2,1)} %c.1, bf16[4,16,64]{2,1,0:T(8,128)(2,1)} %w.3, bf16[4,20,128,128]{3,2,1,0:T(8,128)(2,1)} %tiles.3), custom_call_target="tpu_custom_call" | custom-call | tf_op jit(solution)/shard_map/push/pallas_call | solution.py:286
  3.4 0.0 copy-start
  3.4 0.0 copy-start.3
  3.4 8.4 %all-to-all-start = ((bf16[8,88,128]{2,1,0:T(8,128)(2,1)}), bf16[8,88,128]{2,1,0:T(8,128)(2,1)S(1)}, u32[]{:S(2)}, u32[]{:S(2)}) async-start(bf16[8,88,128]{2,1,0:T(8,128)(2,1)} %get-tuple-element.29), calls=%async_computation | async-start | bytes 360448 | tf_op jit(solution)/shard_map/all_to_all | solution.py:39
  11.8 0.0 collective-permute-start
  11.8 1.5 %collective-permute-start.1 = (bf16[48,512]{1,0:T(8,128)(2,1)}, bf16[48,512]{1,0:T(8,128)(2,1)S(1)}, u32[]{:S(2)}, u32[]{:S(2)}) collective-permute-start(bf16[48,512]{1,0:T(8,128)(2,1)} %get-tuple-element.30.refs_0_), channel_id=1, source_target_pairs={{0,2},{1,3},{2,0},{3,1},{4,6},{5,7},{6,4},{7,5},{8,10},{9,11},{10,... | collective-permute-start | bytes 147464 | tf_op jit(solution)/shard_map/ppermute | solution.py:57
  13.3 0.3 collective-permute-start.2
  13.7 0.0 copy-done.2
  13.7 0.0 copy-done.1
  13.7 0.0 copy-done.4
  13.7 3.2 %combine.1 = (bf16[512,1536]{1,0:T(8,128)(2,1)S(1)}, f32[16,512]{1,0:T(8,128)S(1)}, f32[16,512]{1,0:T(8,128)S(1)}) custom-call(s32[4,20]{1,0:T(4,128)S(1)} %copy-done.4, bf16[16,512]{1,0:T(8,128)(2,1)S(1)} %copy-done.1, bf16[16,512]{1,0:T(8,128)(2,1)S(1)} %copy-done.2, bf16[4,20,128,128]{3,2,1,0:T(8,128)(2,1)} %tiles.3), custom_call_target="tpu_custom_call" | custom-call | flops 16777216 | bytes 8388608 | tf_op jit(solution)/shard_map/combine/pallas_call | solution.py:308
  16.9 0.0 collective-permute-done.refs_1_
  16.9 0.0 collective-permute-done.1.refs_2_
  16.9 0.4 collective-permute-done.2.refs_3_
  17.3 0.0 all-to-all-done.y1
  17.3 0.0 copy-done.5
  17.3 1.7 %first.1 = (bf16[16,32,128]{2,1,0:T(8,128)(2,1)}, bf16[32,512]{1,0:T(8,128)(2,1)S(1)}, bf16[8,16,128]{2,1,0:T(8,128)(2,1)S(1)}) custom-call(s32[1,8]{1,0:T(1,128)S(1)} %bitcast.2, bf16[8,88,128]{2,1,0:T(8,128)(2,1)S(1)} %all-to-all-done.y1, bf16[512,1536]{1,0:T(8,128)(2,1)S(1)} %get-tuple-element.32.op.refs_8_, f32[16,512]{1,0:T(8,128)S(1)} %get-tuple-element.33.lf, ...), custom_call_target="tpu_custom_call" | custom-call | tf_op jit(solution)/shard_map/first/pallas_call | solution.py:326
  19.0 5.8 %all-to-all-start.1 = ((bf16[16,32,128]{2,1,0:T(8,128)(2,1)}), bf16[16,32,128]{2,1,0:T(8,128)(2,1)S(1)}, u32[]{:S(2)}, u32[]{:S(2)}) async-start(bf16[16,32,128]{2,1,0:T(8,128)(2,1)} %get-tuple-element.35), calls=%async_computation.1 | async-start | bytes 262144 | tf_op jit(solution)/shard_map/all_to_all | solution.py:53
  24.8 0.0 collective-permute-start.3
  24.8 1.5 %collective-permute-start.4 = (bf16[32,512]{1,0:T(8,128)(2,1)S(1)}, bf16[32,512]{1,0:T(8,128)(2,1)S(1)}, u32[]{:S(2)}, u32[]{:S(2)}) collective-permute-start(bf16[32,512]{1,0:T(8,128)(2,1)S(1)} %get-tuple-element.36.refs_4_), channel_id=1, source_target_pairs={{0,2},{1,3},{2,0},{3,1},{4,6},{5,7},{6,4},{7,5},{8,10},{9,11},{10,... | collective-permute-start | bytes 98312 | tf_op jit(solution)/shard_map/ppermute | solution.py:57
  26.3 0.3 collective-permute-start.5
  26.7 0.0 collective-permute-done.3.refs_5_
  26.7 2.5 %collective-permute-done.4.refs_6_ = bf16[32,512]{1,0:T(8,128)(2,1)S(1)} collective-permute-done((bf16[32,512]{1,0:T(8,128)(2,1)S(1)}, bf16[32,512]{1,0:T(8,128)(2,1)S(1)}, u32[]{:S(2)}, u32[]{:S(2)}) %collective-permute-start.4) | collective-permute-done | bytes 32800 | tf_op jit(solution)/shard_map/ppermute | solution.py:57
  29.1 0.9 %collective-permute-done.5.refs_7_ = bf16[32,512]{1,0:T(8,128)(2,1)S(1)} collective-permute-done((bf16[32,512]{1,0:T(8,128)(2,1)S(1)}, bf16[32,512]{1,0:T(8,128)(2,1)S(1)}, u32[]{:S(2)}, u32[]{:S(2)}) %collective-permute-start.5) | collective-permute-done | bytes 32800 | tf_op jit(solution)/shard_map/ppermute | solution.py:57
  30.1 0.0 all-to-all-done.1.y2
  30.1 0.1 collective-permute-start.6
  30.2 0.0 copy-done
  30.2 0.0 copy-done.3
  30.2 0.6 %gather.1 = (f32[64,512]{1,0:T(8,128)S(1)}, f32[64,512]{1,0:T(8,128)S(1)}, bf16[4,64,512]{2,1,0:T(8,128)(2,1)S(1)}, bf16[4,64,64]{2,1,0:T(8,128)(2,1)S(1)}, f32[...) custom-call(bf16[48,512]{1,0:T(8,128)(2,1)S(1)} %copy-done.3, ...), custom_call_target="tpu_custom_call" | custom-call | flops 67108864 | bytes 4194304 | tf_op jit(solution)/shard_map/gather/pallas_call | solution.py:341
  30.8 0.6 %collective-permute-done.6.z2 = bf16[16,32,128]{2,1,0:T(8,128)(2,1)S(1)} collective-permute-done((bf16[16,32,128]{2,1,0:T(8,128)(2,1)S(1)}, bf16[16,32,128]{2,1,0:T(8,128)(2,1)S(1)}, u32[]{:S(2)}, u32[]{:S(2)}) %collective-permute-start.6) | collective-permute-done | bytes 131104 | tf_op jit(solution)/shard_map/ppermute | solution.py:57
  31.4 0.9 %second.1 = (bf16[8,64,128]{2,1,0:T(8,128)(2,1)S(1)}, bf16[2,64,512]{2,1,0:T(8,128)(2,1)S(1)}, bf16[2,16,512]{2,1,0:T(8,128)(2,1)S(1)}) custom-call(bf16[16,32,128]{2,1,0:T(8,128)(2,1)S(1)} %all-to-all-done.1.y2, bf16[16,32,128]{2,1,0:T(8,128)(2,1)S(1)} %collective-permute-done.6.z2, bf16[8,16,128]{2,1,0:T(8,128)(2,1)S(1)} %get-tuple-element.38.marks_ref, ...), custom_call_target="tpu_custom_call" | custom-call | tf_op jit(solution)/shard_map/second/pallas_call | solution.py:360
  32.3 9.3 %all_to_all.15.y3 = bf16[8,64,128]{2,1,0:T(8,128)(2,1)S(1)} all-to-all(bf16[8,64,128]{2,1,0:T(8,128)(2,1)S(1)} %get-tuple-element.50), channel_id=1, replica_groups={{20,24,28,0,4,8,12,16},{21,25,29,1,5,9,13,17},{22,26,30,2,6,10,14,18},{..., dimensions={0} | all-to-all | bytes 262144 | tf_op jit(solution)/shard_map/all_to_all | solution.py:39
  41.7 1.2 %last.1 = (bf16[16,512]{1,0:T(8,128)(2,1)}, bf16[16,512]{1,0:T(8,128)(2,1)}, f32[4,16,64]{2,1,0:T(8,128)}) custom-call(bf16[8,64,128]{2,1,0:T(8,128)(2,1)S(1)} %all_to_all.15.y3, bf16[8,16,128]{2,1,0:T(8,128)(2,1)S(1)} %get-tuple-element.38.marks_ref, bf16[512,1536]{1,0:T(8,128)(2,1)S(1)} %get-tuple-element.32.op.refs_8_, ...), custom_call_target="tpu_custom_call" | custom-call | tf_op jit(solution)/shard_map/last/pallas_call | solution.py:371
Async XLA Ops:
  0.6 13.0 %copy-start.2 = (bf16[16,512]{1,0:T(8,128)(2,1)S(1)}, bf16[16,512]{1,0:T(8,128)(2,1)}, u32[]{:S(2)}) copy-start(bf16[16,512]{1,0:T(8,128)(2,1)} %c.1) | copy-start | bytes 49156
  0.6 13.0 %copy-start.1 = (bf16[16,512]{1,0:T(8,128)(2,1)S(1)}, bf16[16,512]{1,0:T(8,128)(2,1)}, u32[]{:S(2)}) copy-start(bf16[16,512]{1,0:T(8,128)(2,1)} %f.1) | copy-start | bytes 49156
  0.7 13.0 %copy-start.4 = (s32[4,20]{1,0:T(4,128)S(1)}, s32[4,20]{1,0:T(4,128)}, u32[]{:S(2)}) copy-start(s32[4,20]{1,0:T(4,128)} %cols.1) | copy-start | bytes 964
  0.7 16.6 %copy-start.5 = (s32[1,8,1]{1,2,0:T(1,128)S(1)}, s32[1,8,1]{1,2,0:T(1,128)}, u32[]{:S(2)}) copy-start(s32[1,8,1]{1,2,0:T(1,128)} %param.9) | copy-start | bytes 100
  3.4 26.8 %copy-start = (bf16[4,16,64]{2,1,0:T(8,128)(2,1)S(1)}, bf16[4,16,64]{2,1,0:T(8,128)(2,1)}, u32[]{:S(2)}) copy-start(bf16[4,16,64]{2,1,0:T(8,128)(2,1)} %w.3) | copy-start | bytes 24580
  3.4 26.8 %copy-start.3 = (bf16[48,512]{1,0:T(8,128)(2,1)S(1)}, bf16[48,512]{1,0:T(8,128)(2,1)}, u32[]{:S(2)}) copy-start(bf16[48,512]{1,0:T(8,128)(2,1)} %get-tuple-element.30.refs_0_) | copy-start | bytes 147460
  3.4 13.9 %all-to-all-start = ((bf16[8,88,128]{2,1,0:T(8,128)(2,1)}), bf16[8,88,128]{2,1,0:T(8,128)(2,1)S(1)}, u32[]{:S(2)}, u32[]{:S(2)}) async-start(bf16[8,88,128]{2,1,0:T(8,128)(2,1)} %get-tuple-element.29), calls=%async_computation | async-start | bytes 360448 | tf_op jit(solution)/shard_map/all_to_all | solution.py:39
  11.8 5.1 %collective-permute-start = (bf16[48,512]{1,0:T(8,128)(2,1)}, bf16[48,512]{1,0:T(8,128)(2,1)S(1)}, u32[]{:S(2)}, u32[]{:S(2)}) collective-permute-start(bf16[48,512]{1,0:T(8,128)(2,1)} %get-tuple-element.30.refs_0_), channel_id=1, source_target_pairs={{0,1},{1,0},{2,3},{3,2},{4,5},{5,4},{6,7},{7,6},{8,9},{9,8},{10,11... | collective-permute-start | bytes 147464 | tf_op jit(solution)/shard_map/ppermute | solution.py:57
  11.8 5.1 %collective-permute-start.1 = (bf16[48,512]{1,0:T(8,128)(2,1)}, bf16[48,512]{1,0:T(8,128)(2,1)S(1)}, u32[]{:S(2)}, u32[]{:S(2)}) collective-permute-start(bf16[48,512]{1,0:T(8,128)(2,1)} %get-tuple-element.30.refs_0_), channel_id=1, source_target_pairs={{0,2},{1,3},{2,0},{3,1},{4,6},{5,7},{6,4},{7,5},{8,10},{9,11},{10,... | collective-permute-start | bytes 147464 | tf_op jit(solution)/shard_map/ppermute | solution.py:57
  13.3 3.9 %collective-permute-start.2 = (bf16[48,512]{1,0:T(8,128)(2,1)}, bf16[48,512]{1,0:T(8,128)(2,1)S(1)}, u32[]{:S(2)}, u32[]{:S(2)}) collective-permute-start(bf16[48,512]{1,0:T(8,128)(2,1)} %get-tuple-element.30.refs_0_), channel_id=1, source_target_pairs={{0,3},{1,2},{2,1},{3,0},{4,7},{5,6},{6,5},{7,4},{8,11},{9,10},{10,... | collective-permute-start | bytes 147464 | tf_op jit(solution)/shard_map/ppermute | solution.py:57
  19.0 11.1 %all-to-all-start.1 = ((bf16[16,32,128]{2,1,0:T(8,128)(2,1)}), bf16[16,32,128]{2,1,0:T(8,128)(2,1)S(1)}, u32[]{:S(2)}, u32[]{:S(2)}) async-start(bf16[16,32,128]{2,1,0:T(8,128)(2,1)} %get-tuple-element.35), calls=%async_computation.1 | async-start | bytes 262144 | tf_op jit(solution)/shard_map/all_to_all | solution.py:53
  24.8 1.9 %collective-permute-start.3 = (bf16[32,512]{1,0:T(8,128)(2,1)S(1)}, bf16[32,512]{1,0:T(8,128)(2,1)S(1)}, u32[]{:S(2)}, u32[]{:S(2)}) collective-permute-start(bf16[32,512]{1,0:T(8,128)(2,1)S(1)} %get-tuple-element.36.refs_4_), channel_id=1, source_target_pairs={{0,1},{1,0},{2,3},{3,2},{4,5},{5,4},{6,7},{7,6},{8,9},{9,8},{10,11... | collective-permute-start | bytes 98312 | tf_op jit(solution)/shard_map/ppermute | solution.py:57
  24.8 4.3 %collective-permute-start.4 = (bf16[32,512]{1,0:T(8,128)(2,1)S(1)}, bf16[32,512]{1,0:T(8,128)(2,1)S(1)}, u32[]{:S(2)}, u32[]{:S(2)}) collective-permute-start(bf16[32,512]{1,0:T(8,128)(2,1)S(1)} %get-tuple-element.36.refs_4_), channel_id=1, source_target_pairs={{0,2},{1,3},{2,0},{3,1},{4,6},{5,7},{6,4},{7,5},{8,10},{9,11},{10,... | collective-permute-start | bytes 98312 | tf_op jit(solution)/shard_map/ppermute | solution.py:57
  26.3 3.7 %collective-permute-start.5 = (bf16[32,512]{1,0:T(8,128)(2,1)S(1)}, bf16[32,512]{1,0:T(8,128)(2,1)S(1)}, u32[]{:S(2)}, u32[]{:S(2)}) collective-permute-start(bf16[32,512]{1,0:T(8,128)(2,1)S(1)} %get-tuple-element.36.refs_4_), channel_id=1, source_target_pairs={{0,3},{1,2},{2,1},{3,0},{4,7},{5,6},{6,5},{7,4},{8,11},{9,10},{10,... | collective-permute-start | bytes 98312 | tf_op jit(solution)/shard_map/ppermute | solution.py:57
  30.1 1.3 %collective-permute-start.6 = (bf16[16,32,128]{2,1,0:T(8,128)(2,1)S(1)}, bf16[16,32,128]{2,1,0:T(8,128)(2,1)S(1)}, u32[]{:S(2)}, u32[]{:S(2)}) collective-permute-start(bf16[16,32,128]{2,1,0:T(8,128)(2,1)S(1)} %all-to-all-done.1.y2), channel_id=1, source_target_pairs={{0,1},{1,0},{2,3},{3,2},{4,5},{5,4},{6,7},{7,6},{8,9},{9,8},{10,11... | collective-permute-start | bytes 393224 | tf_op jit(solution)/shard_map/ppermute | solution.py:57

commit v5 on v4

--- a/solution.py
+++ b/solution.py
@@ -40,7 +40,7 @@
 
 
 def spread(device, pair, n, half):
-    return (device * half + pair - turn(n) * half) % (n * half)
+    return (device * half + pair - turn(n) * half - 1) % (n * half)
 
 
 def spread_exchange(value, n, q):
@@ -48,7 +48,7 @@
     groups = []
     for parity in range(2):
         members = [row * q + 2 * pair + parity for row in range(n) for pair in range(half)]
-        start = turn(n) * half
+        start = turn(n) * half + 1
         groups.append(members[start:] + members[:start])
     return lax.all_to_all(value, ("rows", "ch"), 0, 0, axis_index_groups=groups)
 

time: 43.3 us -> 42.8 us (0.988)
  waiting for transfers between devices: 4.39 us -> 3.58 us
    ppermute x7, waiting for transfers between devices: 4.38 us -> 3.58 us  [swap(): return lax.ppermute(value, 'ch', [(i, i ^ bit) for i in range(q)])]
  transfers between devices with their start and end apart: 9 -> 9, of which waited for: 4 -> 3; matrix products, arithmetic and copies ran while one was open for 0% -> 0% of each run, Pallas kernels for 9% -> 9%
where the time goes in v5:
time: 42.8 us; the launch traced here: 42.3 us
  starting transfers between devices  18.3 us (43%)
  Pallas kernels  10.4 us (24%)
  blocking collectives  9.31 us (22%)
  waiting for transfers between devices  3.58 us (8%)
  between operations  0.73 us (2%)
    all_to_all x1, blocking collectives, row_exchange(): return lax.all_to_all(value, 'rows', 0, 0, axis_index_groups=[order])  9.31 us
    all_to_all x1, starting transfers between devices, row_exchange(): return lax.all_to_all(value, 'rows', 0, 0, axis_index_groups=[order])  8.41 us
    all_to_all x1, starting transfers between devices, spread_exchange(): return lax.all_to_all(value, ('rows', 'ch'), 0, 0, axis_index_groups=groups)  6.01 us
    ppermute x7, starting transfers between devices, swap(): return lax.ppermute(value, 'ch', [(i, i ^ bit) for i in range(q)])  3.88 us
    ppermute x7, waiting for transfers between devices, swap(): return lax.ppermute(value, 'ch', [(i, i ^ bit) for i in range(q)])  3.58 us
    pallas_call x1, Pallas kernels, body(): pl.pallas_call(combine_kernel, out_shape=(struct((own, wide), BF), struct...  3.18 us
    pallas_call x1, Pallas kernels, body(): pl.pallas_call(push_kernel, out_shape=(struct((n, (nb + 1) * ci + 8, bw),...  2.7 us
    pallas_call x1, Pallas kernels, body(): pl.pallas_call(first_kernel, out_shape=(struct((n * (q // 2), 2 * ci, bw)...  1.71 us
  transfers between devices with their start and end apart: 9, of which 3 were waited for; matrix products, arithmetic and copies ran while one was open for 0% of the time, Pallas kernels for 9%

profile of v5, /device:TPU:0, one launch (start us, length us, event | category | flops | bytes accessed | tf_op | source)
XLA Modules:
  0.0 42.3 jit_solution(15525629933237507870)
XLA Ops:
  0.6 0.0 copy-start.2
  0.6 0.0 copy-start.1
  0.7 0.0 copy-start.4
  0.7 0.0 copy-start.5
  0.7 2.7 %push.1 = (bf16[8,88,128]{2,1,0:T(8,128)(2,1)}, bf16[48,512]{1,0:T(8,128)(2,1)}) custom-call(s32[4,20]{1,0:T(4,128)} %cols.1, s32[1,8]{1,0:T(1,128)} %bitcast.1, bf16[16,512]{1,0:T(8,128)(2,1)} %f.1, bf16[16,512]{1,0:T(8,128)(2,1)} %c.1, bf16[4,16,64]{2,1,0:T(8,128)(2,1)} %w.3, bf16[4,20,128,128]{3,2,1,0:T(8,128)(2,1)} %tiles.3), custom_call_target="tpu_custom_call" | custom-call | tf_op jit(solution)/shard_map/push/pallas_call | solution.py:286
  3.4 0.0 copy-start
  3.4 0.0 copy-start.3
  3.4 8.4 %all-to-all-start = ((bf16[8,88,128]{2,1,0:T(8,128)(2,1)}), bf16[8,88,128]{2,1,0:T(8,128)(2,1)S(1)}, u32[]{:S(2)}, u32[]{:S(2)}) async-start(bf16[8,88,128]{2,1,0:T(8,128)(2,1)} %get-tuple-element.29), calls=%async_computation | async-start | bytes 360448 | tf_op jit(solution)/shard_map/all_to_all | solution.py:39
  11.8 0.0 collective-permute-start
  11.8 1.5 %collective-permute-start.1 = (bf16[48,512]{1,0:T(8,128)(2,1)}, bf16[48,512]{1,0:T(8,128)(2,1)S(1)}, u32[]{:S(2)}, u32[]{:S(2)}) collective-permute-start(bf16[48,512]{1,0:T(8,128)(2,1)} %get-tuple-element.30.refs_0_), channel_id=1, source_target_pairs={{0,2},{1,3},{2,0},{3,1},{4,6},{5,7},{6,4},{7,5},{8,10},{9,11},{10,... | collective-permute-start | bytes 147464 | tf_op jit(solution)/shard_map/ppermute | solution.py:57
  13.3 0.3 collective-permute-start.2
  13.7 0.0 copy-done.2
  13.7 0.0 copy-done.1
  13.7 0.0 copy-done.4
  13.7 3.2 %combine.1 = (bf16[512,1536]{1,0:T(8,128)(2,1)S(1)}, f32[16,512]{1,0:T(8,128)S(1)}, f32[16,512]{1,0:T(8,128)S(1)}) custom-call(s32[4,20]{1,0:T(4,128)S(1)} %copy-done.4, bf16[16,512]{1,0:T(8,128)(2,1)S(1)} %copy-done.1, bf16[16,512]{1,0:T(8,128)(2,1)S(1)} %copy-done.2, bf16[4,20,128,128]{3,2,1,0:T(8,128)(2,1)} %tiles.3), custom_call_target="tpu_custom_call" | custom-call | flops 16777216 | bytes 8388608 | tf_op jit(solution)/shard_map/combine/pallas_call | solution.py:308
  16.9 0.0 collective-permute-done.refs_1_
  16.9 0.0 collective-permute-done.1.refs_2_
  16.9 0.4 collective-permute-done.2.refs_3_
  17.3 0.0 all-to-all-done.y1
  17.3 0.0 copy-done.5
  17.3 1.7 %first.1 = (bf16[16,32,128]{2,1,0:T(8,128)(2,1)}, bf16[32,512]{1,0:T(8,128)(2,1)S(1)}, bf16[8,16,128]{2,1,0:T(8,128)(2,1)S(1)}) custom-call(s32[1,8]{1,0:T(1,128)S(1)} %bitcast.2, bf16[8,88,128]{2,1,0:T(8,128)(2,1)S(1)} %all-to-all-done.y1, bf16[512,1536]{1,0:T(8,128)(2,1)S(1)} %get-tuple-element.32.op.refs_8_, f32[16,512]{1,0:T(8,128)S(1)} %get-tuple-element.33.lf, ...), custom_call_target="tpu_custom_call" | custom-call | tf_op jit(solution)/shard_map/first/pallas_call | solution.py:326
  19.0 6.0 %all-to-all-start.1 = ((bf16[16,32,128]{2,1,0:T(8,128)(2,1)}), bf16[16,32,128]{2,1,0:T(8,128)(2,1)S(1)}, u32[]{:S(2)}, u32[]{:S(2)}) async-start(bf16[16,32,128]{2,1,0:T(8,128)(2,1)} %get-tuple-element.35), calls=%async_computation.1 | async-start | bytes 262144 | tf_op jit(solution)/shard_map/all_to_all | solution.py:53
  25.0 0.0 collective-permute-start.3
  25.0 0.6 %collective-permute-start.4 = (bf16[32,512]{1,0:T(8,128)(2,1)S(1)}, bf16[32,512]{1,0:T(8,128)(2,1)S(1)}, u32[]{:S(2)}, u32[]{:S(2)}) collective-permute-start(bf16[32,512]{1,0:T(8,128)(2,1)S(1)} %get-tuple-element.36.refs_4_), channel_id=1, source_target_pairs={{0,2},{1,3},{2,0},{3,1},{4,6},{5,7},{6,4},{7,5},{8,10},{9,11},{10,... | collective-permute-start | bytes 98312 | tf_op jit(solution)/shard_map/ppermute | solution.py:57
  25.6 1.2 %collective-permute-start.5 = (bf16[32,512]{1,0:T(8,128)(2,1)S(1)}, bf16[32,512]{1,0:T(8,128)(2,1)S(1)}, u32[]{:S(2)}, u32[]{:S(2)}) collective-permute-start(bf16[32,512]{1,0:T(8,128)(2,1)S(1)} %get-tuple-element.36.refs_4_), channel_id=1, source_target_pairs={{0,3},{1,2},{2,1},{3,0},{4,7},{5,6},{6,5},{7,4},{8,11},{9,10},{10,... | collective-permute-start | bytes 98312 | tf_op jit(solution)/shard_map/ppermute | solution.py:57
  26.9 0.0 collective-permute-done.3.refs_5_
  26.9 2.6 %collective-permute-done.4.refs_6_ = bf16[32,512]{1,0:T(8,128)(2,1)S(1)} collective-permute-done((bf16[32,512]{1,0:T(8,128)(2,1)S(1)}, bf16[32,512]{1,0:T(8,128)(2,1)S(1)}, u32[]{:S(2)}, u32[]{:S(2)}) %collective-permute-start.4) | collective-permute-done | bytes 32800 | tf_op jit(solution)/shard_map/ppermute | solution.py:57
  29.5 0.0 collective-permute-done.5.refs_7_
  29.5 0.0 all-to-all-done.1.y2
  29.5 0.2 collective-permute-start.6
  29.7 0.0 copy-done
  29.7 0.0 copy-done.3
  29.7 0.6 %gather.1 = (f32[64,512]{1,0:T(8,128)S(1)}, f32[64,512]{1,0:T(8,128)S(1)}, bf16[4,64,512]{2,1,0:T(8,128)(2,1)S(1)}, bf16[4,64,64]{2,1,0:T(8,128)(2,1)S(1)}, f32[...) custom-call(bf16[48,512]{1,0:T(8,128)(2,1)S(1)} %copy-done.3, ...), custom_call_target="tpu_custom_call" | custom-call | flops 67108864 | bytes 4194304 | tf_op jit(solution)/shard_map/gather/pallas_call | solution.py:341
  30.3 0.6 %collective-permute-done.6.z2 = bf16[16,32,128]{2,1,0:T(8,128)(2,1)S(1)} collective-permute-done((bf16[16,32,128]{2,1,0:T(8,128)(2,1)S(1)}, bf16[16,32,128]{2,1,0:T(8,128)(2,1)S(1)}, u32[]{:S(2)}, u32[]{:S(2)}) %collective-permute-start.6) | collective-permute-done | bytes 131104 | tf_op jit(solution)/shard_map/ppermute | solution.py:57
  30.9 0.9 %second.1 = (bf16[8,64,128]{2,1,0:T(8,128)(2,1)S(1)}, bf16[2,64,512]{2,1,0:T(8,128)(2,1)S(1)}, bf16[2,16,512]{2,1,0:T(8,128)(2,1)S(1)}) custom-call(bf16[16,32,128]{2,1,0:T(8,128)(2,1)S(1)} %all-to-all-done.1.y2, bf16[16,32,128]{2,1,0:T(8,128)(2,1)S(1)} %collective-permute-done.6.z2, bf16[8,16,128]{2,1,0:T(8,128)(2,1)S(1)} %get-tuple-element.38.marks_ref, ...), custom_call_target="tpu_custom_call" | custom-call | tf_op jit(solution)/shard_map/second/pallas_call | solution.py:360
  31.8 9.3 %all_to_all.15.y3 = bf16[8,64,128]{2,1,0:T(8,128)(2,1)S(1)} all-to-all(bf16[8,64,128]{2,1,0:T(8,128)(2,1)S(1)} %get-tuple-element.50), channel_id=1, replica_groups={{20,24,28,0,4,8,12,16},{21,25,29,1,5,9,13,17},{22,26,30,2,6,10,14,18},{..., dimensions={0} | all-to-all | bytes 262144 | tf_op jit(solution)/shard_map/all_to_all | solution.py:39
  41.1 1.2 %last.1 = (bf16[16,512]{1,0:T(8,128)(2,1)}, bf16[16,512]{1,0:T(8,128)(2,1)}, f32[4,16,64]{2,1,0:T(8,128)}) custom-call(bf16[8,64,128]{2,1,0:T(8,128)(2,1)S(1)} %all_to_all.15.y3, bf16[8,16,128]{2,1,0:T(8,128)(2,1)S(1)} %get-tuple-element.38.marks_ref, bf16[512,1536]{1,0:T(8,128)(2,1)S(1)} %get-tuple-element.32.op.refs_8_, ...), custom_call_target="tpu_custom_call" | custom-call | tf_op jit(solution)/shard_map/last/pallas_call | solution.py:371
Async XLA Ops:
  0.6 13.0 %copy-start.2 = (bf16[16,512]{1,0:T(8,128)(2,1)S(1)}, bf16[16,512]{1,0:T(8,128)(2,1)}, u32[]{:S(2)}) copy-start(bf16[16,512]{1,0:T(8,128)(2,1)} %c.1) | copy-start | bytes 49156
  0.6 13.0 %copy-start.1 = (bf16[16,512]{1,0:T(8,128)(2,1)S(1)}, bf16[16,512]{1,0:T(8,128)(2,1)}, u32[]{:S(2)}) copy-start(bf16[16,512]{1,0:T(8,128)(2,1)} %f.1) | copy-start | bytes 49156
  0.7 13.0 %copy-start.4 = (s32[4,20]{1,0:T(4,128)S(1)}, s32[4,20]{1,0:T(4,128)}, u32[]{:S(2)}) copy-start(s32[4,20]{1,0:T(4,128)} %cols.1) | copy-start | bytes 964
  0.7 16.6 %copy-start.5 = (s32[1,8,1]{1,2,0:T(1,128)S(1)}, s32[1,8,1]{1,2,0:T(1,128)}, u32[]{:S(2)}) copy-start(s32[1,8,1]{1,2,0:T(1,128)} %param.9) | copy-start | bytes 100
  3.4 26.3 %copy-start = (bf16[4,16,64]{2,1,0:T(8,128)(2,1)S(1)}, bf16[4,16,64]{2,1,0:T(8,128)(2,1)}, u32[]{:S(2)}) copy-start(bf16[4,16,64]{2,1,0:T(8,128)(2,1)} %w.3) | copy-start | bytes 24580
  3.4 26.3 %copy-start.3 = (bf16[48,512]{1,0:T(8,128)(2,1)S(1)}, bf16[48,512]{1,0:T(8,128)(2,1)}, u32[]{:S(2)}) copy-start(bf16[48,512]{1,0:T(8,128)(2,1)} %get-tuple-element.30.refs_0_) | copy-start | bytes 147460
  3.4 13.9 %all-to-all-start = ((bf16[8,88,128]{2,1,0:T(8,128)(2,1)}), bf16[8,88,128]{2,1,0:T(8,128)(2,1)S(1)}, u32[]{:S(2)}, u32[]{:S(2)}) async-start(bf16[8,88,128]{2,1,0:T(8,128)(2,1)} %get-tuple-element.29), calls=%async_computation | async-start | bytes 360448 | tf_op jit(solution)/shard_map/all_to_all | solution.py:39
  11.8 5.1 %collective-permute-start = (bf16[48,512]{1,0:T(8,128)(2,1)}, bf16[48,512]{1,0:T(8,128)(2,1)S(1)}, u32[]{:S(2)}, u32[]{:S(2)}) collective-permute-start(bf16[48,512]{1,0:T(8,128)(2,1)} %get-tuple-element.30.refs_0_), channel_id=1, source_target_pairs={{0,1},{1,0},{2,3},{3,2},{4,5},{5,4},{6,7},{7,6},{8,9},{9,8},{10,11... | collective-permute-start | bytes 147464 | tf_op jit(solution)/shard_map/ppermute | solution.py:57
  11.8 5.1 %collective-permute-start.1 = (bf16[48,512]{1,0:T(8,128)(2,1)}, bf16[48,512]{1,0:T(8,128)(2,1)S(1)}, u32[]{:S(2)}, u32[]{:S(2)}) collective-permute-start(bf16[48,512]{1,0:T(8,128)(2,1)} %get-tuple-element.30.refs_0_), channel_id=1, source_target_pairs={{0,2},{1,3},{2,0},{3,1},{4,6},{5,7},{6,4},{7,5},{8,10},{9,11},{10,... | collective-permute-start | bytes 147464 | tf_op jit(solution)/shard_map/ppermute | solution.py:57
  13.3 3.9 %collective-permute-start.2 = (bf16[48,512]{1,0:T(8,128)(2,1)}, bf16[48,512]{1,0:T(8,128)(2,1)S(1)}, u32[]{:S(2)}, u32[]{:S(2)}) collective-permute-start(bf16[48,512]{1,0:T(8,128)(2,1)} %get-tuple-element.30.refs_0_), channel_id=1, source_target_pairs={{0,3},{1,2},{2,1},{3,0},{4,7},{5,6},{6,5},{7,4},{8,11},{9,10},{10,... | collective-permute-start | bytes 147464 | tf_op jit(solution)/shard_map/ppermute | solution.py:57
  19.0 10.5 %all-to-all-start.1 = ((bf16[16,32,128]{2,1,0:T(8,128)(2,1)}), bf16[16,32,128]{2,1,0:T(8,128)(2,1)S(1)}, u32[]{:S(2)}, u32[]{:S(2)}) async-start(bf16[16,32,128]{2,1,0:T(8,128)(2,1)} %get-tuple-element.35), calls=%async_computation.1 | async-start | bytes 262144 | tf_op jit(solution)/shard_map/all_to_all | solution.py:53
  25.0 1.9 %collective-permute-start.3 = (bf16[32,512]{1,0:T(8,128)(2,1)S(1)}, bf16[32,512]{1,0:T(8,128)(2,1)S(1)}, u32[]{:S(2)}, u32[]{:S(2)}) collective-permute-start(bf16[32,512]{1,0:T(8,128)(2,1)S(1)} %get-tuple-element.36.refs_4_), channel_id=1, source_target_pairs={{0,1},{1,0},{2,3},{3,2},{4,5},{5,4},{6,7},{7,6},{8,9},{9,8},{10,11... | collective-permute-start | bytes 98312 | tf_op jit(solution)/shard_map/ppermute | solution.py:57
  25.0 4.5 %collective-permute-start.4 = (bf16[32,512]{1,0:T(8,128)(2,1)S(1)}, bf16[32,512]{1,0:T(8,128)(2,1)S(1)}, u32[]{:S(2)}, u32[]{:S(2)}) collective-permute-start(bf16[32,512]{1,0:T(8,128)(2,1)S(1)} %get-tuple-element.36.refs_4_), channel_id=1, source_target_pairs={{0,2},{1,3},{2,0},{3,1},{4,6},{5,7},{6,4},{7,5},{8,10},{9,11},{10,... | collective-permute-start | bytes 98312 | tf_op jit(solution)/shard_map/ppermute | solution.py:57
  25.6 3.9 %collective-permute-start.5 = (bf16[32,512]{1,0:T(8,128)(2,1)S(1)}, bf16[32,512]{1,0:T(8,128)(2,1)S(1)}, u32[]{:S(2)}, u32[]{:S(2)}) collective-permute-start(bf16[32,512]{1,0:T(8,128)(2,1)S(1)} %get-tuple-element.36.refs_4_), channel_id=1, source_target_pairs={{0,3},{1,2},{2,1},{3,0},{4,7},{5,6},{6,5},{7,4},{8,11},{9,10},{10,... | collective-permute-start | bytes 98312 | tf_op jit(solution)/shard_map/ppermute | solution.py:57
  29.5 1.4 %collective-permute-start.6 = (bf16[16,32,128]{2,1,0:T(8,128)(2,1)S(1)}, bf16[16,32,128]{2,1,0:T(8,128)(2,1)S(1)}, u32[]{:S(2)}, u32[]{:S(2)}) collective-permute-start(bf16[16,32,128]{2,1,0:T(8,128)(2,1)S(1)} %all-to-all-done.1.y2), channel_id=1, source_target_pairs={{0,1},{1,0},{2,3},{3,2},{4,5},{5,4},{6,7},{7,6},{8,9},{9,8},{10,11... | collective-permute-start | bytes 393224 | tf_op jit(solution)/shard_map/ppermute | solution.py:57

commit v6 on v5

--- a/solution.py
+++ b/solution.py
@@ -31,11 +31,11 @@
 
 
 def member(device, n):
-    return (device - turn(n)) % n
+    return (turn(n) - device) % n
 
 
 def row_exchange(value, n):
-    order = [(i + turn(n)) % n for i in range(n)]
+    order = [(turn(n) - i) % n for i in range(n)]
     return lax.all_to_all(value, "rows", 0, 0, axis_index_groups=[order])
 
 

time: 42.8 us -> 42.4 us (level)
  no operation moved by 1% of the time
where the time goes in v6:
time: 42.4 us; the launch traced here: 42 us
  starting transfers between devices  18.3 us (43%)
  Pallas kernels  10.4 us (25%)
  blocking collectives  8.97 us (21%)
  waiting for transfers between devices  3.58 us (8%)
  between operations  0.73 us (2%)
    all_to_all x1, blocking collectives, row_exchange(): return lax.all_to_all(value, 'rows', 0, 0, axis_index_groups=[order])  8.97 us
    all_to_all x1, starting transfers between devices, row_exchange(): return lax.all_to_all(value, 'rows', 0, 0, axis_index_groups=[order])  8.42 us
    all_to_all x1, starting transfers between devices, spread_exchange(): return lax.all_to_all(value, ('rows', 'ch'), 0, 0, axis_index_groups=groups)  6.01 us
    ppermute x7, starting transfers between devices, swap(): return lax.ppermute(value, 'ch', [(i, i ^ bit) for i in range(q)])  3.88 us
    ppermute x7, waiting for transfers between devices, swap(): return lax.ppermute(value, 'ch', [(i, i ^ bit) for i in range(q)])  3.58 us
    pallas_call x1, Pallas kernels, body(): pl.pallas_call(combine_kernel, out_shape=(struct((own, wide), BF), struct...  3.18 us
    pallas_call x1, Pallas kernels, body(): pl.pallas_call(push_kernel, out_shape=(struct((n, (nb + 1) * ci + 8, bw),...  2.7 us
    pallas_call x1, Pallas kernels, body(): pl.pallas_call(first_kernel, out_shape=(struct((n * (q // 2), 2 * ci, bw)...  1.72 us
  transfers between devices with their start and end apart: 9, of which 3 were waited for; matrix products, arithmetic and copies ran while one was open for 0% of the time, Pallas kernels for 9%

profile of v6, /device:TPU:0, one launch (start us, length us, event | category | flops | bytes accessed | tf_op | source)
XLA Modules:
  0.0 42.0 jit_solution(11970252258853421501)
XLA Ops:
  0.6 0.0 copy-start.2
  0.6 0.0 copy-start.1
  0.7 0.0 copy-start.4
  0.7 0.0 copy-start.5
  0.7 2.7 %push.1 = (bf16[8,88,128]{2,1,0:T(8,128)(2,1)}, bf16[48,512]{1,0:T(8,128)(2,1)}) custom-call(s32[4,20]{1,0:T(4,128)} %cols.1, s32[1,8]{1,0:T(1,128)} %bitcast.1, bf16[16,512]{1,0:T(8,128)(2,1)} %f.1, bf16[16,512]{1,0:T(8,128)(2,1)} %c.1, bf16[4,16,64]{2,1,0:T(8,128)(2,1)} %w.3, bf16[4,20,128,128]{3,2,1,0:T(8,128)(2,1)} %tiles.3), custom_call_target="tpu_custom_call" | custom-call | tf_op jit(solution)/shard_map/push/pallas_call | solution.py:286
  3.4 0.0 copy-start
  3.4 0.0 copy-start.3
  3.4 8.4 %all-to-all-start = ((bf16[8,88,128]{2,1,0:T(8,128)(2,1)}), bf16[8,88,128]{2,1,0:T(8,128)(2,1)S(1)}, u32[]{:S(2)}, u32[]{:S(2)}) async-start(bf16[8,88,128]{2,1,0:T(8,128)(2,1)} %get-tuple-element.29), calls=%async_computation | async-start | bytes 360448 | tf_op jit(solution)/shard_map/all_to_all | solution.py:39
  11.8 0.0 collective-permute-start
  11.8 1.5 %collective-permute-start.1 = (bf16[48,512]{1,0:T(8,128)(2,1)}, bf16[48,512]{1,0:T(8,128)(2,1)S(1)}, u32[]{:S(2)}, u32[]{:S(2)}) collective-permute-start(bf16[48,512]{1,0:T(8,128)(2,1)} %get-tuple-element.30.refs_0_), channel_id=1, source_target_pairs={{0,2},{1,3},{2,0},{3,1},{4,6},{5,7},{6,4},{7,5},{8,10},{9,11},{10,... | collective-permute-start | bytes 147464 | tf_op jit(solution)/shard_map/ppermute | solution.py:57
  13.3 0.3 collective-permute-start.2
  13.7 0.0 copy-done.2
  13.7 0.0 copy-done.1
  13.7 0.0 copy-done.4
  13.7 3.2 %combine.1 = (bf16[512,1536]{1,0:T(8,128)(2,1)S(1)}, f32[16,512]{1,0:T(8,128)S(1)}, f32[16,512]{1,0:T(8,128)S(1)}) custom-call(s32[4,20]{1,0:T(4,128)S(1)} %copy-done.4, bf16[16,512]{1,0:T(8,128)(2,1)S(1)} %copy-done.1, bf16[16,512]{1,0:T(8,128)(2,1)S(1)} %copy-done.2, bf16[4,20,128,128]{3,2,1,0:T(8,128)(2,1)} %tiles.3), custom_call_target="tpu_custom_call" | custom-call | flops 16777216 | bytes 8388608 | tf_op jit(solution)/shard_map/combine/pallas_call | solution.py:308
  16.9 0.0 collective-permute-done.refs_1_
  16.9 0.0 collective-permute-done.1.refs_2_
  16.9 0.4 collective-permute-done.2.refs_3_
  17.3 0.0 all-to-all-done.y1
  17.3 0.0 copy-done.5
  17.3 1.7 %first.1 = (bf16[16,32,128]{2,1,0:T(8,128)(2,1)}, bf16[32,512]{1,0:T(8,128)(2,1)S(1)}, bf16[8,16,128]{2,1,0:T(8,128)(2,1)S(1)}) custom-call(s32[1,8]{1,0:T(1,128)S(1)} %bitcast.2, bf16[8,88,128]{2,1,0:T(8,128)(2,1)S(1)} %all-to-all-done.y1, bf16[512,1536]{1,0:T(8,128)(2,1)S(1)} %get-tuple-element.32.op.refs_8_, f32[16,512]{1,0:T(8,128)S(1)} %get-tuple-element.33.lf, ...), custom_call_target="tpu_custom_call" | custom-call | tf_op jit(solution)/shard_map/first/pallas_call | solution.py:326
  19.0 6.0 %all-to-all-start.1 = ((bf16[16,32,128]{2,1,0:T(8,128)(2,1)}), bf16[16,32,128]{2,1,0:T(8,128)(2,1)S(1)}, u32[]{:S(2)}, u32[]{:S(2)}) async-start(bf16[16,32,128]{2,1,0:T(8,128)(2,1)} %get-tuple-element.35), calls=%async_computation.1 | async-start | bytes 262144 | tf_op jit(solution)/shard_map/all_to_all | solution.py:53
  25.0 0.0 collective-permute-start.3
  25.0 0.6 %collective-permute-start.4 = (bf16[32,512]{1,0:T(8,128)(2,1)S(1)}, bf16[32,512]{1,0:T(8,128)(2,1)S(1)}, u32[]{:S(2)}, u32[]{:S(2)}) collective-permute-start(bf16[32,512]{1,0:T(8,128)(2,1)S(1)} %get-tuple-element.36.refs_4_), channel_id=1, source_target_pairs={{0,2},{1,3},{2,0},{3,1},{4,6},{5,7},{6,4},{7,5},{8,10},{9,11},{10,... | collective-permute-start | bytes 98312 | tf_op jit(solution)/shard_map/ppermute | solution.py:57
  25.7 1.2 %collective-permute-start.5 = (bf16[32,512]{1,0:T(8,128)(2,1)S(1)}, bf16[32,512]{1,0:T(8,128)(2,1)S(1)}, u32[]{:S(2)}, u32[]{:S(2)}) collective-permute-start(bf16[32,512]{1,0:T(8,128)(2,1)S(1)} %get-tuple-element.36.refs_4_), channel_id=1, source_target_pairs={{0,3},{1,2},{2,1},{3,0},{4,7},{5,6},{6,5},{7,4},{8,11},{9,10},{10,... | collective-permute-start | bytes 98312 | tf_op jit(solution)/shard_map/ppermute | solution.py:57
  26.9 0.0 collective-permute-done.3.refs_5_
  26.9 2.6 %collective-permute-done.4.refs_6_ = bf16[32,512]{1,0:T(8,128)(2,1)S(1)} collective-permute-done((bf16[32,512]{1,0:T(8,128)(2,1)S(1)}, bf16[32,512]{1,0:T(8,128)(2,1)S(1)}, u32[]{:S(2)}, u32[]{:S(2)}) %collective-permute-start.4) | collective-permute-done | bytes 32800 | tf_op jit(solution)/shard_map/ppermute | solution.py:57
  29.5 0.0 collective-permute-done.5.refs_7_
  29.5 0.0 all-to-all-done.1.y2
  29.5 0.2 collective-permute-start.6
  29.7 0.0 copy-done
  29.7 0.0 copy-done.3
  29.7 0.6 %gather.1 = (f32[64,512]{1,0:T(8,128)S(1)}, f32[64,512]{1,0:T(8,128)S(1)}, bf16[4,64,512]{2,1,0:T(8,128)(2,1)S(1)}, bf16[4,64,64]{2,1,0:T(8,128)(2,1)S(1)}, f32[...) custom-call(bf16[48,512]{1,0:T(8,128)(2,1)S(1)} %copy-done.3, ...), custom_call_target="tpu_custom_call" | custom-call | flops 67108864 | bytes 4194304 | tf_op jit(solution)/shard_map/gather/pallas_call | solution.py:341
  30.3 0.6 %collective-permute-done.6.z2 = bf16[16,32,128]{2,1,0:T(8,128)(2,1)S(1)} collective-permute-done((bf16[16,32,128]{2,1,0:T(8,128)(2,1)S(1)}, bf16[16,32,128]{2,1,0:T(8,128)(2,1)S(1)}, u32[]{:S(2)}, u32[]{:S(2)}) %collective-permute-start.6) | collective-permute-done | bytes 131104 | tf_op jit(solution)/shard_map/ppermute | solution.py:57
  30.9 0.9 %second.1 = (bf16[8,64,128]{2,1,0:T(8,128)(2,1)S(1)}, bf16[2,64,512]{2,1,0:T(8,128)(2,1)S(1)}, bf16[2,16,512]{2,1,0:T(8,128)(2,1)S(1)}) custom-call(bf16[16,32,128]{2,1,0:T(8,128)(2,1)S(1)} %all-to-all-done.1.y2, bf16[16,32,128]{2,1,0:T(8,128)(2,1)S(1)} %collective-permute-done.6.z2, bf16[8,16,128]{2,1,0:T(8,128)(2,1)S(1)} %get-tuple-element.38.marks_ref, ...), custom_call_target="tpu_custom_call" | custom-call | tf_op jit(solution)/shard_map/second/pallas_call | solution.py:360
  31.8 9.0 %all_to_all.15.y3 = bf16[8,64,128]{2,1,0:T(8,128)(2,1)S(1)} all-to-all(bf16[8,64,128]{2,1,0:T(8,128)(2,1)S(1)} %get-tuple-element.50), channel_id=1, replica_groups={{20,16,12,8,4,0,28,24},{21,17,13,9,5,1,29,25},{22,18,14,10,6,2,30,26},{..., dimensions={0} | all-to-all | bytes 262144 | tf_op jit(solution)/shard_map/all_to_all | solution.py:39
  40.8 1.2 %last.1 = (bf16[16,512]{1,0:T(8,128)(2,1)}, bf16[16,512]{1,0:T(8,128)(2,1)}, f32[4,16,64]{2,1,0:T(8,128)}) custom-call(bf16[8,64,128]{2,1,0:T(8,128)(2,1)S(1)} %all_to_all.15.y3, bf16[8,16,128]{2,1,0:T(8,128)(2,1)S(1)} %get-tuple-element.38.marks_ref, bf16[512,1536]{1,0:T(8,128)(2,1)S(1)} %get-tuple-element.32.op.refs_8_, ...), custom_call_target="tpu_custom_call" | custom-call | tf_op jit(solution)/shard_map/last/pallas_call | solution.py:371
Async XLA Ops:
  0.6 13.1 %copy-start.2 = (bf16[16,512]{1,0:T(8,128)(2,1)S(1)}, bf16[16,512]{1,0:T(8,128)(2,1)}, u32[]{:S(2)}) copy-start(bf16[16,512]{1,0:T(8,128)(2,1)} %c.1) | copy-start | bytes 49156
  0.6 13.1 %copy-start.1 = (bf16[16,512]{1,0:T(8,128)(2,1)S(1)}, bf16[16,512]{1,0:T(8,128)(2,1)}, u32[]{:S(2)}) copy-start(bf16[16,512]{1,0:T(8,128)(2,1)} %f.1) | copy-start | bytes 49156
  0.7 13.0 %copy-start.4 = (s32[4,20]{1,0:T(4,128)S(1)}, s32[4,20]{1,0:T(4,128)}, u32[]{:S(2)}) copy-start(s32[4,20]{1,0:T(4,128)} %cols.1) | copy-start | bytes 964
  0.7 16.6 %copy-start.5 = (s32[1,8,1]{1,2,0:T(1,128)S(1)}, s32[1,8,1]{1,2,0:T(1,128)}, u32[]{:S(2)}) copy-start(s32[1,8,1]{1,2,0:T(1,128)} %param.9) | copy-start | bytes 100
  3.4 26.3 %copy-start = (bf16[4,16,64]{2,1,0:T(8,128)(2,1)S(1)}, bf16[4,16,64]{2,1,0:T(8,128)(2,1)}, u32[]{:S(2)}) copy-start(bf16[4,16,64]{2,1,0:T(8,128)(2,1)} %w.3) | copy-start | bytes 24580
  3.4 26.3 %copy-start.3 = (bf16[48,512]{1,0:T(8,128)(2,1)S(1)}, bf16[48,512]{1,0:T(8,128)(2,1)}, u32[]{:S(2)}) copy-start(bf16[48,512]{1,0:T(8,128)(2,1)} %get-tuple-element.30.refs_0_) | copy-start | bytes 147460
  3.4 13.9 %all-to-all-start = ((bf16[8,88,128]{2,1,0:T(8,128)(2,1)}), bf16[8,88,128]{2,1,0:T(8,128)(2,1)S(1)}, u32[]{:S(2)}, u32[]{:S(2)}) async-start(bf16[8,88,128]{2,1,0:T(8,128)(2,1)} %get-tuple-element.29), calls=%async_computation | async-start | bytes 360448 | tf_op jit(solution)/shard_map/all_to_all | solution.py:39
  11.8 5.1 %collective-permute-start = (bf16[48,512]{1,0:T(8,128)(2,1)}, bf16[48,512]{1,0:T(8,128)(2,1)S(1)}, u32[]{:S(2)}, u32[]{:S(2)}) collective-permute-start(bf16[48,512]{1,0:T(8,128)(2,1)} %get-tuple-element.30.refs_0_), channel_id=1, source_target_pairs={{0,1},{1,0},{2,3},{3,2},{4,5},{5,4},{6,7},{7,6},{8,9},{9,8},{10,11... | collective-permute-start | bytes 147464 | tf_op jit(solution)/shard_map/ppermute | solution.py:57
  11.8 5.1 %collective-permute-start.1 = (bf16[48,512]{1,0:T(8,128)(2,1)}, bf16[48,512]{1,0:T(8,128)(2,1)S(1)}, u32[]{:S(2)}, u32[]{:S(2)}) collective-permute-start(bf16[48,512]{1,0:T(8,128)(2,1)} %get-tuple-element.30.refs_0_), channel_id=1, source_target_pairs={{0,2},{1,3},{2,0},{3,1},{4,6},{5,7},{6,4},{7,5},{8,10},{9,11},{10,... | collective-permute-start | bytes 147464 | tf_op jit(solution)/shard_map/ppermute | solution.py:57
  13.3 3.9 %collective-permute-start.2 = (bf16[48,512]{1,0:T(8,128)(2,1)}, bf16[48,512]{1,0:T(8,128)(2,1)S(1)}, u32[]{:S(2)}, u32[]{:S(2)}) collective-permute-start(bf16[48,512]{1,0:T(8,128)(2,1)} %get-tuple-element.30.refs_0_), channel_id=1, source_target_pairs={{0,3},{1,2},{2,1},{3,0},{4,7},{5,6},{6,5},{7,4},{8,11},{9,10},{10,... | collective-permute-start | bytes 147464 | tf_op jit(solution)/shard_map/ppermute | solution.py:57
  19.0 10.5 %all-to-all-start.1 = ((bf16[16,32,128]{2,1,0:T(8,128)(2,1)}), bf16[16,32,128]{2,1,0:T(8,128)(2,1)S(1)}, u32[]{:S(2)}, u32[]{:S(2)}) async-start(bf16[16,32,128]{2,1,0:T(8,128)(2,1)} %get-tuple-element.35), calls=%async_computation.1 | async-start | bytes 262144 | tf_op jit(solution)/shard_map/all_to_all | solution.py:53
  25.0 1.9 %collective-permute-start.3 = (bf16[32,512]{1,0:T(8,128)(2,1)S(1)}, bf16[32,512]{1,0:T(8,128)(2,1)S(1)}, u32[]{:S(2)}, u32[]{:S(2)}) collective-permute-start(bf16[32,512]{1,0:T(8,128)(2,1)S(1)} %get-tuple-element.36.refs_4_), channel_id=1, source_target_pairs={{0,1},{1,0},{2,3},{3,2},{4,5},{5,4},{6,7},{7,6},{8,9},{9,8},{10,11... | collective-permute-start | bytes 98312 | tf_op jit(solution)/shard_map/ppermute | solution.py:57
  25.0 4.5 %collective-permute-start.4 = (bf16[32,512]{1,0:T(8,128)(2,1)S(1)}, bf16[32,512]{1,0:T(8,128)(2,1)S(1)}, u32[]{:S(2)}, u32[]{:S(2)}) collective-permute-start(bf16[32,512]{1,0:T(8,128)(2,1)S(1)} %get-tuple-element.36.refs_4_), channel_id=1, source_target_pairs={{0,2},{1,3},{2,0},{3,1},{4,6},{5,7},{6,4},{7,5},{8,10},{9,11},{10,... | collective-permute-start | bytes 98312 | tf_op jit(solution)/shard_map/ppermute | solution.py:57
  25.7 3.9 %collective-permute-start.5 = (bf16[32,512]{1,0:T(8,128)(2,1)S(1)}, bf16[32,512]{1,0:T(8,128)(2,1)S(1)}, u32[]{:S(2)}, u32[]{:S(2)}) collective-permute-start(bf16[32,512]{1,0:T(8,128)(2,1)S(1)} %get-tuple-element.36.refs_4_), channel_id=1, source_target_pairs={{0,3},{1,2},{2,1},{3,0},{4,7},{5,6},{6,5},{7,4},{8,11},{9,10},{10,... | collective-permute-start | bytes 98312 | tf_op jit(solution)/shard_map/ppermute | solution.py:57
  29.5 1.4 %collective-permute-start.6 = (bf16[16,32,128]{2,1,0:T(8,128)(2,1)S(1)}, bf16[16,32,128]{2,1,0:T(8,128)(2,1)S(1)}, u32[]{:S(2)}, u32[]{:S(2)}) collective-permute-start(bf16[16,32,128]{2,1,0:T(8,128)(2,1)S(1)} %all-to-all-done.1.y2), channel_id=1, source_target_pairs={{0,1},{1,0},{2,3},{3,2},{4,5},{5,4},{6,7},{7,6},{8,9},{9,8},{10,11... | collective-permute-start | bytes 393224 | tf_op jit(solution)/shard_map/ppermute | solution.py:57

commit v7 on v6

--- a/solution.py
+++ b/solution.py
@@ -40,7 +40,7 @@
 
 
 def spread(device, pair, n, half):
-    return (device * half + pair - turn(n) * half - 1) % (n * half)
+    return (turn(n) * half - 1 - device * half - pair) % (n * half)
 
 
 def spread_exchange(value, n, q):
@@ -48,8 +48,8 @@
     groups = []
     for parity in range(2):
         members = [row * q + 2 * pair + parity for row in range(n) for pair in range(half)]
-        start = turn(n) * half + 1
-        groups.append(members[start:] + members[:start])
+        start = turn(n) * half - 1
+        groups.append([members[(start - i) % len(members)] for i in range(len(members))])
     return lax.all_to_all(value, ("rows", "ch"), 0, 0, axis_index_groups=groups)
 
 

time: 42.4 us -> 42.4 us (level)
  starting transfers between devices: 18.3 us -> 17.5 us
  waiting for transfers between devices: 3.58 us -> 4.38 us
    all_to_all x1, starting transfers between devices: 6.01 us -> 5.35 us  [spread_exchange(): return lax.all_to_all(value, ('rows', 'ch'), 0, 0, axis_index_groups=groups)]
    all_to_all x1, waiting for transfers between devices: 0.01 us -> 0.55 us  [spread_exchange(): return lax.all_to_all(value, ('rows', 'ch'), 0, 0, axis_index_groups=groups)]
  transfers between devices with their start and end apart: 9 -> 9, of which waited for: 3 -> 4; matrix products, arithmetic and copies ran while one was open for 0% -> 0% of each run, Pallas kernels for 9% -> 9%
where the time goes in v7:
time: 42.4 us; the launch traced here: 42 us
  starting transfers between devices  17.5 us (41%)
  Pallas kernels  10.4 us (25%)
  blocking collectives  8.95 us (21%)
  waiting for transfers between devices  4.38 us (10%)
  between operations  0.73 us (2%)
    all_to_all x1, blocking collectives, row_exchange(): return lax.all_to_all(value, 'rows', 0, 0, axis_index_groups=[order])  8.95 us
    all_to_all x1, starting transfers between devices, row_exchange(): return lax.all_to_all(value, 'rows', 0, 0, axis_index_groups=[order])  8.42 us
    all_to_all x1, starting transfers between devices, spread_exchange(): return lax.all_to_all(value, ('rows', 'ch'), 0, 0, axis_index_groups=groups)  5.35 us
    ppermute x7, waiting for transfers between devices, swap(): return lax.ppermute(value, 'ch', [(i, i ^ bit) for i in range(q)])  3.83 us
    ppermute x7, starting transfers between devices, swap(): return lax.ppermute(value, 'ch', [(i, i ^ bit) for i in range(q)])  3.72 us
    pallas_call x1, Pallas kernels, body(): pl.pallas_call(combine_kernel, out_shape=(struct((own, wide), BF), struct...  3.18 us
    pallas_call x1, Pallas kernels, body(): pl.pallas_call(push_kernel, out_shape=(struct((n, (nb + 1) * ci + 8, bw),...  2.7 us
    pallas_call x1, Pallas kernels, body(): pl.pallas_call(first_kernel, out_shape=(struct((n * (q // 2), 2 * ci, bw)...  1.71 us
  transfers between devices with their start and end apart: 9, of which 4 were waited for; matrix products, arithmetic and copies ran while one was open for 0% of the time, Pallas kernels for 9%

profile of v7, /device:TPU:0, one launch (start us, length us, event | category | flops | bytes accessed | tf_op | source)
XLA Modules:
  0.0 42.0 jit_solution(12231562826599690312)
XLA Ops:
  0.6 0.0 copy-start.2
  0.6 0.0 copy-start.1
  0.7 0.0 copy-start.4
  0.7 0.0 copy-start.5
  0.7 2.7 %push.1 = (bf16[8,88,128]{2,1,0:T(8,128)(2,1)}, bf16[48,512]{1,0:T(8,128)(2,1)}) custom-call(s32[4,20]{1,0:T(4,128)} %cols.1, s32[1,8]{1,0:T(1,128)} %bitcast.1, bf16[16,512]{1,0:T(8,128)(2,1)} %f.1, bf16[16,512]{1,0:T(8,128)(2,1)} %c.1, bf16[4,16,64]{2,1,0:T(8,128)(2,1)} %w.3, bf16[4,20,128,128]{3,2,1,0:T(8,128)(2,1)} %tiles.3), custom_call_target="tpu_custom_call" | custom-call | tf_op jit(solution)/shard_map/push/pallas_call | solution.py:286
  3.4 0.0 copy-start
  3.4 0.0 copy-start.3
  3.4 8.4 %all-to-all-start = ((bf16[8,88,128]{2,1,0:T(8,128)(2,1)}), bf16[8,88,128]{2,1,0:T(8,128)(2,1)S(1)}, u32[]{:S(2)}, u32[]{:S(2)}) async-start(bf16[8,88,128]{2,1,0:T(8,128)(2,1)} %get-tuple-element.29), calls=%async_computation | async-start | bytes 360448 | tf_op jit(solution)/shard_map/all_to_all | solution.py:39
  11.8 0.0 collective-permute-start
  11.8 1.5 %collective-permute-start.1 = (bf16[48,512]{1,0:T(8,128)(2,1)}, bf16[48,512]{1,0:T(8,128)(2,1)S(1)}, u32[]{:S(2)}, u32[]{:S(2)}) collective-permute-start(bf16[48,512]{1,0:T(8,128)(2,1)} %get-tuple-element.30.refs_0_), channel_id=1, source_target_pairs={{0,2},{1,3},{2,0},{3,1},{4,6},{5,7},{6,4},{7,5},{8,10},{9,11},{10,... | collective-permute-start | bytes 147464 | tf_op jit(solution)/shard_map/ppermute | solution.py:57
  13.3 0.3 collective-permute-start.2
  13.7 0.0 copy-done.2
  13.7 0.0 copy-done.1
  13.7 0.0 copy-done.4
  13.7 3.2 %combine.1 = (bf16[512,1536]{1,0:T(8,128)(2,1)S(1)}, f32[16,512]{1,0:T(8,128)S(1)}, f32[16,512]{1,0:T(8,128)S(1)}) custom-call(s32[4,20]{1,0:T(4,128)S(1)} %copy-done.4, bf16[16,512]{1,0:T(8,128)(2,1)S(1)} %copy-done.1, bf16[16,512]{1,0:T(8,128)(2,1)S(1)} %copy-done.2, bf16[4,20,128,128]{3,2,1,0:T(8,128)(2,1)} %tiles.3), custom_call_target="tpu_custom_call" | custom-call | flops 16777216 | bytes 8388608 | tf_op jit(solution)/shard_map/combine/pallas_call | solution.py:308
  16.9 0.0 collective-permute-done.refs_1_
  16.9 0.0 collective-permute-done.1.refs_2_
  16.9 0.4 collective-permute-done.2.refs_3_
  17.3 0.0 all-to-all-done.y1
  17.3 0.0 copy-done.5
  17.3 1.7 %first.1 = (bf16[16,32,128]{2,1,0:T(8,128)(2,1)}, bf16[32,512]{1,0:T(8,128)(2,1)S(1)}, bf16[8,16,128]{2,1,0:T(8,128)(2,1)S(1)}) custom-call(s32[1,8]{1,0:T(1,128)S(1)} %bitcast.2, bf16[8,88,128]{2,1,0:T(8,128)(2,1)S(1)} %all-to-all-done.y1, bf16[512,1536]{1,0:T(8,128)(2,1)S(1)} %get-tuple-element.32.op.refs_8_, f32[16,512]{1,0:T(8,128)S(1)} %get-tuple-element.33.lf, ...), custom_call_target="tpu_custom_call" | custom-call | tf_op jit(solution)/shard_map/first/pallas_call | solution.py:326
  19.0 5.3 %all-to-all-start.1 = ((bf16[16,32,128]{2,1,0:T(8,128)(2,1)}), bf16[16,32,128]{2,1,0:T(8,128)(2,1)S(1)}, u32[]{:S(2)}, u32[]{:S(2)}) async-start(bf16[16,32,128]{2,1,0:T(8,128)(2,1)} %get-tuple-element.35), calls=%async_computation.1 | async-start | bytes 262144 | tf_op jit(solution)/shard_map/all_to_all | solution.py:53
  24.3 0.0 collective-permute-start.3
  24.4 0.6 %collective-permute-start.4 = (bf16[32,512]{1,0:T(8,128)(2,1)S(1)}, bf16[32,512]{1,0:T(8,128)(2,1)S(1)}, u32[]{:S(2)}, u32[]{:S(2)}) collective-permute-start(bf16[32,512]{1,0:T(8,128)(2,1)S(1)} %get-tuple-element.36.refs_4_), channel_id=1, source_target_pairs={{0,2},{1,3},{2,0},{3,1},{4,6},{5,7},{6,4},{7,5},{8,10},{9,11},{10,... | collective-permute-start | bytes 98312 | tf_op jit(solution)/shard_map/ppermute | solution.py:57
  25.0 1.2 %collective-permute-start.5 = (bf16[32,512]{1,0:T(8,128)(2,1)S(1)}, bf16[32,512]{1,0:T(8,128)(2,1)S(1)}, u32[]{:S(2)}, u32[]{:S(2)}) collective-permute-start(bf16[32,512]{1,0:T(8,128)(2,1)S(1)} %get-tuple-element.36.refs_4_), channel_id=1, source_target_pairs={{0,3},{1,2},{2,1},{3,0},{4,7},{5,6},{6,5},{7,4},{8,11},{9,10},{10,... | collective-permute-start | bytes 98312 | tf_op jit(solution)/shard_map/ppermute | solution.py:57
  26.2 0.0 collective-permute-done.3.refs_5_
  26.2 2.7 %collective-permute-done.4.refs_6_ = bf16[32,512]{1,0:T(8,128)(2,1)S(1)} collective-permute-done((bf16[32,512]{1,0:T(8,128)(2,1)S(1)}, bf16[32,512]{1,0:T(8,128)(2,1)S(1)}, u32[]{:S(2)}, u32[]{:S(2)}) %collective-permute-start.4) | collective-permute-done | bytes 32800 | tf_op jit(solution)/shard_map/ppermute | solution.py:57
  28.9 0.0 collective-permute-done.5.refs_7_
  29.0 0.5 %all-to-all-done.1.y2 = bf16[16,32,128]{2,1,0:T(8,128)(2,1)S(1)} async-done(((bf16[16,32,128]{2,1,0:T(8,128)(2,1)}), bf16[16,32,128]{2,1,0:T(8,128)(2,1)S(1)}, u32[]{:S(2)}, u32[]{:S(2)}) %all-to-all-start.1) | async-done | bytes 131104 | tf_op jit(solution)/shard_map/all_to_all | solution.py:53
  29.5 0.0 collective-permute-start.6
  29.5 0.0 copy-done
  29.5 0.0 copy-done.3
  29.5 0.6 %gather.1 = (f32[64,512]{1,0:T(8,128)S(1)}, f32[64,512]{1,0:T(8,128)S(1)}, bf16[4,64,512]{2,1,0:T(8,128)(2,1)S(1)}, bf16[4,64,64]{2,1,0:T(8,128)(2,1)S(1)}, f32[...) custom-call(bf16[48,512]{1,0:T(8,128)(2,1)S(1)} %copy-done.3, ...), custom_call_target="tpu_custom_call" | custom-call | flops 67108864 | bytes 4194304 | tf_op jit(solution)/shard_map/gather/pallas_call | solution.py:341
  30.1 0.7 %collective-permute-done.6.z2 = bf16[16,32,128]{2,1,0:T(8,128)(2,1)S(1)} collective-permute-done((bf16[16,32,128]{2,1,0:T(8,128)(2,1)S(1)}, bf16[16,32,128]{2,1,0:T(8,128)(2,1)S(1)}, u32[]{:S(2)}, u32[]{:S(2)}) %collective-permute-start.6) | collective-permute-done | bytes 131104 | tf_op jit(solution)/shard_map/ppermute | solution.py:57
  30.9 0.9 %second.1 = (bf16[8,64,128]{2,1,0:T(8,128)(2,1)S(1)}, bf16[2,64,512]{2,1,0:T(8,128)(2,1)S(1)}, bf16[2,16,512]{2,1,0:T(8,128)(2,1)S(1)}) custom-call(bf16[16,32,128]{2,1,0:T(8,128)(2,1)S(1)} %all-to-all-done.1.y2, bf16[16,32,128]{2,1,0:T(8,128)(2,1)S(1)} %collective-permute-done.6.z2, bf16[8,16,128]{2,1,0:T(8,128)(2,1)S(1)} %get-tuple-element.38.marks_ref, ...), custom_call_target="tpu_custom_call" | custom-call | tf_op jit(solution)/shard_map/second/pallas_call | solution.py:360
  31.8 8.9 %all_to_all.15.y3 = bf16[8,64,128]{2,1,0:T(8,128)(2,1)S(1)} all-to-all(bf16[8,64,128]{2,1,0:T(8,128)(2,1)S(1)} %get-tuple-element.50), channel_id=1, replica_groups={{20,16,12,8,4,0,28,24},{21,17,13,9,5,1,29,25},{22,18,14,10,6,2,30,26},{..., dimensions={0} | all-to-all | bytes 262144 | tf_op jit(solution)/shard_map/all_to_all | solution.py:39
  40.7 1.2 %last.1 = (bf16[16,512]{1,0:T(8,128)(2,1)}, bf16[16,512]{1,0:T(8,128)(2,1)}, f32[4,16,64]{2,1,0:T(8,128)}) custom-call(bf16[8,64,128]{2,1,0:T(8,128)(2,1)S(1)} %all_to_all.15.y3, bf16[8,16,128]{2,1,0:T(8,128)(2,1)S(1)} %get-tuple-element.38.marks_ref, bf16[512,1536]{1,0:T(8,128)(2,1)S(1)} %get-tuple-element.32.op.refs_8_, ...), custom_call_target="tpu_custom_call" | custom-call | tf_op jit(solution)/shard_map/last/pallas_call | solution.py:371
Async XLA Ops:
  0.6 13.1 %copy-start.2 = (bf16[16,512]{1,0:T(8,128)(2,1)S(1)}, bf16[16,512]{1,0:T(8,128)(2,1)}, u32[]{:S(2)}) copy-start(bf16[16,512]{1,0:T(8,128)(2,1)} %c.1) | copy-start | bytes 49156
  0.6 13.1 %copy-start.1 = (bf16[16,512]{1,0:T(8,128)(2,1)S(1)}, bf16[16,512]{1,0:T(8,128)(2,1)}, u32[]{:S(2)}) copy-start(bf16[16,512]{1,0:T(8,128)(2,1)} %f.1) | copy-start | bytes 49156
  0.7 13.0 %copy-start.4 = (s32[4,20]{1,0:T(4,128)S(1)}, s32[4,20]{1,0:T(4,128)}, u32[]{:S(2)}) copy-start(s32[4,20]{1,0:T(4,128)} %cols.1) | copy-start | bytes 964
  0.7 16.6 %copy-start.5 = (s32[1,8,1]{1,2,0:T(1,128)S(1)}, s32[1,8,1]{1,2,0:T(1,128)}, u32[]{:S(2)}) copy-start(s32[1,8,1]{1,2,0:T(1,128)} %param.9) | copy-start | bytes 100
  3.4 26.1 %copy-start = (bf16[4,16,64]{2,1,0:T(8,128)(2,1)S(1)}, bf16[4,16,64]{2,1,0:T(8,128)(2,1)}, u32[]{:S(2)}) copy-start(bf16[4,16,64]{2,1,0:T(8,128)(2,1)} %w.3) | copy-start | bytes 24580
  3.4 26.1 %copy-start.3 = (bf16[48,512]{1,0:T(8,128)(2,1)S(1)}, bf16[48,512]{1,0:T(8,128)(2,1)}, u32[]{:S(2)}) copy-start(bf16[48,512]{1,0:T(8,128)(2,1)} %get-tuple-element.30.refs_0_) | copy-start | bytes 147460
  3.4 13.9 %all-to-all-start = ((bf16[8,88,128]{2,1,0:T(8,128)(2,1)}), bf16[8,88,128]{2,1,0:T(8,128)(2,1)S(1)}, u32[]{:S(2)}, u32[]{:S(2)}) async-start(bf16[8,88,128]{2,1,0:T(8,128)(2,1)} %get-tuple-element.29), calls=%async_computation | async-start | bytes 360448 | tf_op jit(solution)/shard_map/all_to_all | solution.py:39
  11.8 5.1 %collective-permute-start = (bf16[48,512]{1,0:T(8,128)(2,1)}, bf16[48,512]{1,0:T(8,128)(2,1)S(1)}, u32[]{:S(2)}, u32[]{:S(2)}) collective-permute-start(bf16[48,512]{1,0:T(8,128)(2,1)} %get-tuple-element.30.refs_0_), channel_id=1, source_target_pairs={{0,1},{1,0},{2,3},{3,2},{4,5},{5,4},{6,7},{7,6},{8,9},{9,8},{10,11... | collective-permute-start | bytes 147464 | tf_op jit(solution)/shard_map/ppermute | solution.py:57
  11.8 5.1 %collective-permute-start.1 = (bf16[48,512]{1,0:T(8,128)(2,1)}, bf16[48,512]{1,0:T(8,128)(2,1)S(1)}, u32[]{:S(2)}, u32[]{:S(2)}) collective-permute-start(bf16[48,512]{1,0:T(8,128)(2,1)} %get-tuple-element.30.refs_0_), channel_id=1, source_target_pairs={{0,2},{1,3},{2,0},{3,1},{4,6},{5,7},{6,4},{7,5},{8,10},{9,11},{10,... | collective-permute-start | bytes 147464 | tf_op jit(solution)/shard_map/ppermute | solution.py:57
  13.3 3.9 %collective-permute-start.2 = (bf16[48,512]{1,0:T(8,128)(2,1)}, bf16[48,512]{1,0:T(8,128)(2,1)S(1)}, u32[]{:S(2)}, u32[]{:S(2)}) collective-permute-start(bf16[48,512]{1,0:T(8,128)(2,1)} %get-tuple-element.30.refs_0_), channel_id=1, source_target_pairs={{0,3},{1,2},{2,1},{3,0},{4,7},{5,6},{6,5},{7,4},{8,11},{9,10},{10,... | collective-permute-start | bytes 147464 | tf_op jit(solution)/shard_map/ppermute | solution.py:57
  19.0 10.5 %all-to-all-start.1 = ((bf16[16,32,128]{2,1,0:T(8,128)(2,1)}), bf16[16,32,128]{2,1,0:T(8,128)(2,1)S(1)}, u32[]{:S(2)}, u32[]{:S(2)}) async-start(bf16[16,32,128]{2,1,0:T(8,128)(2,1)} %get-tuple-element.35), calls=%async_computation.1 | async-start | bytes 262144 | tf_op jit(solution)/shard_map/all_to_all | solution.py:53
  24.3 1.9 %collective-permute-start.3 = (bf16[32,512]{1,0:T(8,128)(2,1)S(1)}, bf16[32,512]{1,0:T(8,128)(2,1)S(1)}, u32[]{:S(2)}, u32[]{:S(2)}) collective-permute-start(bf16[32,512]{1,0:T(8,128)(2,1)S(1)} %get-tuple-element.36.refs_4_), channel_id=1, source_target_pairs={{0,1},{1,0},{2,3},{3,2},{4,5},{5,4},{6,7},{7,6},{8,9},{9,8},{10,11... | collective-permute-start | bytes 98312 | tf_op jit(solution)/shard_map/ppermute | solution.py:57
  24.4 4.6 %collective-permute-start.4 = (bf16[32,512]{1,0:T(8,128)(2,1)S(1)}, bf16[32,512]{1,0:T(8,128)(2,1)S(1)}, u32[]{:S(2)}, u32[]{:S(2)}) collective-permute-start(bf16[32,512]{1,0:T(8,128)(2,1)S(1)} %get-tuple-element.36.refs_4_), channel_id=1, source_target_pairs={{0,2},{1,3},{2,0},{3,1},{4,6},{5,7},{6,4},{7,5},{8,10},{9,11},{10,... | collective-permute-start | bytes 98312 | tf_op jit(solution)/shard_map/ppermute | solution.py:57
  25.0 4.0 %collective-permute-start.5 = (bf16[32,512]{1,0:T(8,128)(2,1)S(1)}, bf16[32,512]{1,0:T(8,128)(2,1)S(1)}, u32[]{:S(2)}, u32[]{:S(2)}) collective-permute-start(bf16[32,512]{1,0:T(8,128)(2,1)S(1)} %get-tuple-element.36.refs_4_), channel_id=1, source_target_pairs={{0,3},{1,2},{2,1},{3,0},{4,7},{5,6},{6,5},{7,4},{8,11},{9,10},{10,... | collective-permute-start | bytes 98312 | tf_op jit(solution)/shard_map/ppermute | solution.py:57
  29.5 1.3 %collective-permute-start.6 = (bf16[16,32,128]{2,1,0:T(8,128)(2,1)S(1)}, bf16[16,32,128]{2,1,0:T(8,128)(2,1)S(1)}, u32[]{:S(2)}, u32[]{:S(2)}) collective-permute-start(bf16[16,32,128]{2,1,0:T(8,128)(2,1)S(1)} %all-to-all-done.1.y2), channel_id=1, source_target_pairs={{0,1},{1,0},{2,3},{3,2},{4,5},{5,4},{6,7},{7,6},{8,9},{9,8},{10,11... | collective-permute-start | bytes 393224 | tf_op jit(solution)/shard_map/ppermute | solution.py:57
